TPU v7x, 32 devices: a whole 2x2x4 slice. The times are simulated.
32 devices in a mesh: seq: 8 (over z, core), rows: 4 (over y, x).
Axes of the slice: x: 2, y: 2, z: 4, core: 2. Of those that a mesh axis runs over, the one named last changes fastest.
Arguments:
- hidden_in: bfloat16 [8, 1024, 1024], P('rows', 'seq'), may hold values from -6 to 6
- lengths: int32 [8, 16], P('rows'), may hold values from 1 to 256, 1024 in all within a row
- norm1_gain: bfloat16 [1024], P(('seq', 'rows')), may hold values from 0.099609375 to 1.8984375
- w_query: bfloat16 [1024, 1024], P(('seq', 'rows')), may hold values from -0.25 to 0.25
- w_key: bfloat16 [1024, 1024], P(('seq', 'rows')), may hold values from -0.25 to 0.25
- w_value: bfloat16 [1024, 1024], P(('seq', 'rows')), may hold values from -0.1875 to 0.1875
- w_out: bfloat16 [1024, 1024], P(('seq', 'rows')), may hold values from -0.5 to 0.5
- norm2_gain: bfloat16 [1024], P(('seq', 'rows')), may hold values from 0.099609375 to 1.8984375
- w_gate: bfloat16 [1024, 2816], P(('seq', 'rows')), may hold values from -0.1875 to 0.1875
- w_up: bfloat16 [1024, 2816], P(('seq', 'rows')), may hold values from -0.1875 to 0.1875
- w_down: bfloat16 [1024, 2816], P(('seq', 'rows')), may hold values from -0.15625 to 0.15625
- out_grad: bfloat16 [8, 1024, 1024], P('rows', 'seq'), may hold values from -6 to 6
Outputs:
- block_out: bfloat16 [8, 1024, 1024], P('rows', 'seq')
- grad_in: float32 [8, 1024, 1024], P('rows', 'seq')
- grad_norm1: float32 [1024], P(('seq', 'rows'))
- grad_query: float32 [1024, 1024], P(('seq', 'rows'))
- grad_key: float32 [1024, 1024], P(('seq', 'rows'))
- grad_value: float32 [1024, 1024], P(('seq', 'rows'))
- grad_wout: float32 [1024, 1024], P(('seq', 'rows'))
- grad_norm2: float32 [1024], P(('seq', 'rows'))
- grad_gate: float32 [1024, 2816], P(('seq', 'rows'))
- grad_up: float32 [1024, 2816], P(('seq', 'rows'))
- grad_down: float32 [1024, 2816], P(('seq', 'rows'))
Inputs may be any that keep to these rules, and one draw needn't show every extreme that they name: lengths[r] lists the lengths of the documents packed in order into row r; they sum to 1024, and the longest of each row has exactly 256 tokens.
All inputs are finite; a program needn't handle non-finite values.
Results may differ from a plain program's by a relative error of at most 0.014.
The roundings to bfloat16 on the way count: a program that leaves them out, or rounds other values in their place, can miss the bound.
Values may be sent and summed in bfloat16 or wider, within the bound.
A program may use at most 104 MiB of HBM per device.

v0:
```python
import math

import jax
import jax.numpy as jnp
from jax import lax
from jax.sharding import PartitionSpec as P

HEADS = 8
HEAD_DIM = 128
WINDOW = 64
MB = 2


def passed_along(block, axis, distance):
    devices = range(lax.axis_size(axis))
    route = [(i - distance, i) for i in devices if i - distance in devices]
    return lax.ppermute(block, axis, route)


def rms_scale(values, gain):
    factor = lax.rsqrt(jnp.mean(values * values, axis=-1, keepdims=True) + 1e-05)
    return values * factor * gain


def swiglu(gates, ups):
    return jax.nn.silu(gates) * ups


def project(left, weight):
    return jnp.dot(left, weight, preferred_element_type=jnp.float32)


def project_back(grad, weight):
    return lax.dot_general(
        grad, weight, (((2,), (1,)), ((), ())), preferred_element_type=jnp.float32
    )


def weight_grad(left, grad):
    return jnp.einsum("rtd,rtf->df", left, grad, preferred_element_type=jnp.float32)


def split_heads(values):
    return values.reshape(values.shape[0], values.shape[1], HEADS, HEAD_DIM)


def merge_heads(values):
    return values.reshape(values.shape[0], values.shape[1], HEADS * HEAD_DIM)


def window_mask(lengths, seq_index, tokens):
    ends = jnp.cumsum(lengths, axis=1)
    query_pos = seq_index * tokens + jnp.arange(tokens, dtype=jnp.int32)
    key_pos = seq_index * tokens - WINDOW + jnp.arange(tokens + WINDOW, dtype=jnp.int32)
    starts = jnp.max(
        jnp.where(
            ends[:, None, :] <= query_pos[None, :, None],
            ends[:, None, :],
            jnp.zeros_like(ends[:, None, :]),
        ),
        axis=2,
    )
    allowed = (
        (key_pos[None, None, :] >= starts[:, :, None])
        & (key_pos[None, None, :] <= query_pos[None, :, None])
        & (query_pos[None, :, None] - key_pos[None, None, :] < WINDOW)
    )
    return allowed[:, None]


def scores_of(queries, keys_all, allowed):
    score_scale = 1.0 / math.sqrt(HEAD_DIM)
    scores = (
        jnp.einsum(
            "rqhd,rkhd->rhqk",
            split_heads(queries),
            split_heads(keys_all),
            preferred_element_type=jnp.float32,
        )
        * score_scale
    )
    return jnp.where(allowed, scores, -1e30)


def layer_pass(hidden_in, lengths, out_grad, attn_shards, mlp_shards):
    score_scale = 1.0 / math.sqrt(HEAD_DIM)
    tokens = hidden_in.shape[1]
    gain_one_low, w_query, w_key, w_value, w_out = (
        lax.all_gather(attn_shards[0], ("seq", "rows"), axis=0, tiled=True),
        lax.all_gather(attn_shards[1], ("seq", "rows"), axis=0, tiled=True),
        lax.all_gather(attn_shards[2], ("seq", "rows"), axis=0, tiled=True),
        lax.all_gather(attn_shards[3], ("seq", "rows"), axis=0, tiled=True),
        lax.all_gather(attn_shards[4], ("seq", "rows"), axis=0, tiled=True),
    )
    inputs = hidden_in.astype(jnp.float32)
    gain_one = gain_one_low.astype(jnp.float32)
    normed_one = rms_scale(inputs, gain_one).astype(jnp.bfloat16)
    queries = project(normed_one, w_query).astype(jnp.bfloat16)
    keys = project(normed_one, w_key).astype(jnp.bfloat16)
    values = project(normed_one, w_value).astype(jnp.bfloat16)
    tails = jnp.stack([keys[:, tokens - WINDOW :], values[:, tokens - WINDOW :]])
    received = passed_along(tails, "seq", 1)
    keys_all = jnp.concatenate([received[0], keys], axis=1)
    values_all = jnp.concatenate([received[1], values], axis=1)
    allowed = window_mask(lengths, lax.axis_index("seq"), tokens)
    scores = scores_of(queries, keys_all, allowed)
    top = jnp.max(scores, axis=-1, keepdims=True)
    weights = jnp.exp(scores - top)
    totals = jnp.sum(weights, axis=-1, keepdims=True)
    probs = weights / totals
    log_total = top + jnp.log(totals)
    mixed = jnp.einsum(
        "rhqk,rkhd->rqhd",
        probs.astype(jnp.bfloat16),
        split_heads(values_all),
        preferred_element_type=jnp.float32,
    )
    attended = merge_heads(mixed).astype(jnp.bfloat16)
    middle = inputs + project(attended, w_out)
    gain_two_low, w_gate, w_up, w_down = (
        lax.all_gather(mlp_shards[0], ("seq", "rows"), axis=0, tiled=True),
        lax.all_gather(mlp_shards[1], ("seq", "rows"), axis=0, tiled=True),
        lax.all_gather(mlp_shards[2], ("seq", "rows"), axis=0, tiled=True),
        lax.all_gather(mlp_shards[3], ("seq", "rows"), axis=0, tiled=True),
    )
    gain_two = gain_two_low.astype(jnp.float32)
    normed_two = rms_scale(middle, gain_two).astype(jnp.bfloat16)
    gates = project(normed_two, w_gate)
    ups = project(normed_two, w_up)
    hidden_act = swiglu(gates, ups).astype(jnp.bfloat16)
    block_out = (middle + project_back(hidden_act, w_down)).astype(jnp.bfloat16)
    grad_hidden = project(out_grad, w_down)
    unused, swiglu_back = jax.vjp(swiglu, gates, ups)
    grad_gates, grad_ups = swiglu_back(grad_hidden)
    grad_gates = grad_gates.astype(jnp.bfloat16)
    grad_ups = grad_ups.astype(jnp.bfloat16)
    grad_normed_two = project_back(grad_gates, w_gate) + project_back(grad_ups, w_up)
    unused, norm_two_back = jax.vjp(rms_scale, middle, gain_two)
    grad_middle_part, grad_norm2 = norm_two_back(grad_normed_two)
    grad_middle = out_grad.astype(jnp.float32) + grad_middle_part
    grad_branch = grad_middle.astype(jnp.bfloat16)
    grad_attended = project_back(grad_branch, w_out).astype(jnp.bfloat16)
    probs_again = jnp.exp(scores_of(queries, keys_all, allowed) - log_total)
    probs_low = probs_again.astype(jnp.bfloat16)
    grad_heads = split_heads(grad_attended)
    grad_values_all = jnp.einsum(
        "rhqk,rqhd->rkhd", probs_low, grad_heads, preferred_element_type=jnp.float32
    )
    grad_probs = jnp.einsum(
        "rqhd,rkhd->rhqk", grad_heads, split_heads(values_all), preferred_element_type=jnp.float32
    )
    grad_scores = (
        probs_again * (grad_probs - jnp.sum(grad_probs * probs_again, axis=-1, keepdims=True))
    ).astype(jnp.bfloat16)
    grad_queries = (
        merge_heads(
            jnp.einsum(
                "rhqk,rkhd->rqhd",
                grad_scores,
                split_heads(keys_all),
                preferred_element_type=jnp.float32,
            )
        )
        * score_scale
    )
    grad_keys_all = (
        merge_heads(
            jnp.einsum(
                "rhqk,rqhd->rkhd",
                grad_scores,
                split_heads(queries),
                preferred_element_type=jnp.float32,
            )
        )
        * score_scale
    )
    grad_values_all = merge_heads(grad_values_all)
    halo_grads = jnp.stack([grad_keys_all[:, :WINDOW], grad_values_all[:, :WINDOW]])
    returned = passed_along(halo_grads.astype(jnp.bfloat16), "seq", -1).astype(halo_grads.dtype)
    grad_keys = (
        grad_keys_all[:, WINDOW:].at[:, tokens - WINDOW :].add(returned[0]).astype(jnp.bfloat16)
    )
    grad_values = (
        grad_values_all[:, WINDOW:].at[:, tokens - WINDOW :].add(returned[1]).astype(jnp.bfloat16)
    )
    grad_queries = grad_queries.astype(jnp.bfloat16)
    grad_normed_one = (
        project_back(grad_queries, w_query)
        + project_back(grad_keys, w_key)
        + project_back(grad_values, w_value)
    )
    unused, norm_one_back = jax.vjp(rms_scale, inputs, gain_one)
    grad_inputs_part, grad_norm1 = norm_one_back(grad_normed_one)
    grad_in = grad_middle + grad_inputs_part
    kept_attn = (normed_one, grad_queries, grad_keys, grad_values, attended, grad_branch)
    kept_mlp = (normed_two, grad_gates, grad_ups, hidden_act)
    return (block_out, grad_in, grad_norm1, grad_norm2, kept_attn, kept_mlp)


def shards(
    hidden_in,
    lengths,
    norm1_gain,
    w_query,
    w_key,
    w_value,
    w_out,
    norm2_gain,
    w_gate,
    w_up,
    w_down,
    out_grad,
):
    attn_shards = (norm1_gain, w_query, w_key, w_value, w_out)
    mlp_shards = (norm2_gain, w_gate, w_up, w_down)
    local_rows = hidden_in.shape[0]
    passes = MB
    width = local_rows // passes
    outputs = []
    gradients = []
    attn_saved = []
    mlp_saved = []
    norm_one_total = None
    norm_two_total = None
    for number in range(passes):
        first = number * width
        block_out, grad_in, grad_norm1, grad_norm2, kept_attn, kept_mlp = layer_pass(
            hidden_in[first : first + width],
            lengths[first : first + width],
            out_grad[first : first + width],
            attn_shards,
            mlp_shards,
        )
        outputs.append(block_out)
        gradients.append(grad_in)
        attn_saved.append(kept_attn)
        mlp_saved.append(kept_mlp)
        if norm_one_total is None:
            norm_one_total = grad_norm1
            norm_two_total = grad_norm2
        else:
            norm_one_total = norm_one_total + grad_norm1
            norm_two_total = norm_two_total + grad_norm2
    block_out = jnp.concatenate(outputs, axis=0)
    grad_in = jnp.concatenate(gradients, axis=0)
    normed_two, grad_gates, grad_ups, hidden_act = [
        jnp.concatenate([saved[k] for saved in mlp_saved], axis=0) for k in range(4)
    ]
    grad_down = weight_grad(out_grad, hidden_act)
    grad_gate = weight_grad(normed_two, grad_gates)
    grad_up = weight_grad(normed_two, grad_ups)
    mlp_total = (
        lax.psum_scatter(norm_two_total, ("seq", "rows"), scatter_dimension=0, tiled=True),
        lax.psum_scatter(grad_gate, ("seq", "rows"), scatter_dimension=0, tiled=True),
        lax.psum_scatter(grad_up, ("seq", "rows"), scatter_dimension=0, tiled=True),
        lax.psum_scatter(grad_down, ("seq", "rows"), scatter_dimension=0, tiled=True),
    )
    normed_one, grad_queries, grad_keys, grad_values, attended, grad_branch = [
        jnp.concatenate([saved[k] for saved in attn_saved], axis=0) for k in range(6)
    ]
    grad_query = weight_grad(normed_one, grad_queries)
    grad_key = weight_grad(normed_one, grad_keys)
    grad_value = weight_grad(normed_one, grad_values)
    grad_wout = weight_grad(attended, grad_branch)
    attn_total = (
        lax.psum_scatter(norm_one_total, ("seq", "rows"), scatter_dimension=0, tiled=True),
        lax.psum_scatter(grad_query, ("seq", "rows"), scatter_dimension=0, tiled=True),
        lax.psum_scatter(grad_key, ("seq", "rows"), scatter_dimension=0, tiled=True),
        lax.psum_scatter(grad_value, ("seq", "rows"), scatter_dimension=0, tiled=True),
        lax.psum_scatter(grad_wout, ("seq", "rows"), scatter_dimension=0, tiled=True),
    )
    return (
        block_out,
        grad_in,
        attn_total[0],
        attn_total[1],
        attn_total[2],
        attn_total[3],
        attn_total[4],
        mlp_total[0],
        mlp_total[1],
        mlp_total[2],
        mlp_total[3],
    )


def solution(mesh):
    in_specs = (
        P("rows", "seq", None),
        P("rows", None),
        P(("seq", "rows")),
        P(("seq", "rows"), None),
        P(("seq", "rows"), None),
        P(("seq", "rows"), None),
        P(("seq", "rows"), None),
        P(("seq", "rows")),
        P(("seq", "rows"), None),
        P(("seq", "rows"), None),
        P(("seq", "rows"), None),
        P("rows", "seq", None),
    )
    out_specs = (
        P("rows", "seq", None),
        P("rows", "seq", None),
        P(("seq", "rows")),
        P(("seq", "rows"), None),
        P(("seq", "rows"), None),
        P(("seq", "rows"), None),
        P(("seq", "rows"), None),
        P(("seq", "rows")),
        P(("seq", "rows"), None),
        P(("seq", "rows"), None),
        P(("seq", "rows"), None),
    )
    return jax.shard_map(shards, mesh=mesh, in_specs=in_specs, out_specs=out_specs, check_vma=False)
```

profile of v0, /device:TPU:0, one launch (start us, length us, event | category | flops | bytes accessed | tf_op | source)
XLA Modules:
  0.0 1813.4 jit_solution(18023055162785961135)
XLA Ops:
  13.6 42.2 %all-reduce.5 = (bf16[1024]{0:T(1024)(128)(2,1)S(1)}, bf16[1024]{0:T(1024)(128)(2,1)S(1)}) all-reduce(bf16[1024]{0:T(1024)(128)(2,1)S(1)} %dynamic-update-slice.12, bf16[1024]{0:T(1024)(128)(2,1)S(1)} %dynamic-update-slice.13), channel_id=1, replica_groups=mesh['seq'=8,'rows'=4] {'seq','rows'}, use_global_device_ids=true, to_apply=%add | all-reduce | flops 2048 | bytes 8192
  61.0 9.2 all-gather.10.cloned.1.call-done
  72.2 56.1 %all-gather.8.cloned.1.call-done = bf16[1024,1024]{1,0:T(8,128)(2,1)} async-done(((bf16[32,1024]{1,0:T(8,128)(2,1)}), bf16[1024,1024]{1,0:T(8,128)(2,1)}) %all-gather.8.cloned.1.call-update) | async-done | bytes 2097168 | tf_op jit(solution)/shard_map/all_gather | solution.py:91
  131.2 2.9 collective-permute-start.1
  139.0 47.5 %all-gather.12.cloned.1.call-done = bf16[1024,1024]{1,0:T(8,128)(2,1)} async-done(((bf16[32,1024]{1,0:T(8,128)(2,1)}), bf16[1024,1024]{1,0:T(8,128)(2,1)}) %all-gather.12.cloned.1.call-update) | async-done | bytes 2097168 | tf_op jit(solution)/shard_map/all_gather | solution.py:90
  196.0 48.5 %all-gather.14.cloned.1.call-done = bf16[1024,1024]{1,0:T(8,128)(2,1)} async-done(((bf16[32,1024]{1,0:T(8,128)(2,1)}), bf16[1024,1024]{1,0:T(8,128)(2,1)}) %all-gather.14.cloned.1.call-update) | async-done | bytes 2097168 | tf_op jit(solution)/shard_map/all_gather | solution.py:93
  250.5 63.0 %all-gather.16.cloned.1.call-done = bf16[1024,2816]{1,0:T(8,128)(2,1)} async-done(((bf16[32,2816]{1,0:T(8,128)(2,1)}), bf16[1024,2816]{1,0:T(8,128)(2,1)}) %all-gather.16.cloned.1.call-update) | async-done | bytes 5767184 | tf_op jit(solution)/shard_map/all_gather | solution.py:122
  313.5 4.8 fusion.119
  318.3 64.2 %all-gather.18.cloned.1.call-done = bf16[1024,2816]{1,0:T(8,128)(2,1)} async-done(((bf16[32,2816]{1,0:T(8,128)(2,1)}), bf16[1024,2816]{1,0:T(8,128)(2,1)}) %all-gather.18.cloned.1.call-update) | async-done | bytes 5767184 | tf_op jit(solution)/shard_map/all_gather | solution.py:123
  382.5 4.8 fusion.117
  387.3 64.4 %all-gather.20.cloned.1.call-done = bf16[1024,2816]{1,0:T(8,128)(2,1)} async-done(((bf16[32,2816]{1,0:T(8,128)(2,1)}), bf16[1024,2816]{1,0:T(8,128)(2,1)}) %all-gather.20.cloned.1.call-update) | async-done | bytes 5767184 | tf_op jit(solution)/shard_map/all_gather | solution.py:124
  451.7 5.9 multiply_convert_fusion.1
  457.6 5.1 fusion.163
  462.9 2.7 fusion.69
  481.8 2.7 convolution_bitcast_fusion.6
  485.7 2.7 convolution_bitcast_fusion.3
  499.5 2.8 convolution_bitcast_fusion.5
  502.4 2.7 convolution_bitcast_fusion.4
  506.6 5.9 convolution_bitcast_fusion.2
  513.9 5.9 convolution_bitcast_fusion.1
  521.0 7.1 convolution_bitcast_fusion
  528.1 11.9 copy.201
  540.7 4.9 fusion.25
  545.6 4.8 fusion.26
  559.4 45.0 %all-reduce.4 = (f32[1024]{0:T(1024)S(1)}, f32[1024]{0:T(1024)S(1)}) all-reduce(f32[1024]{0:T(1024)S(1)} %add.241, f32[1024]{0:T(1024)S(1)} %add.244), channel_id=2, replica_groups=mesh['seq'=8,'rows'=4] {'seq','rows'}, use_global_device_ids=true, to_apply=%region_20.21.clone | all-reduce | flops 2048 | bytes 16384
  608.3 17.0 reduce-scatter.10.cloned.1.call-done
  625.4 142.1 %reduce-scatter.16.cloned.1.call-done = f32[32,1024]{1,0:T(8,128)} async-done(((f32[1024,1024]{1,0:T(8,128)}), f32[32,1024]{1,0:T(8,128)}) %reduce-scatter.16.cloned.1.call-update) | async-done | bytes 131088 | tf_op jit(solution)/shard_map/reduce_scatter | solution.py:270
  767.5 142.4 %reduce-scatter.12.cloned.1.call-done = f32[32,1024]{1,0:T(8,128)} async-done(((f32[1024,1024]{1,0:T(8,128)}), f32[32,1024]{1,0:T(8,128)}) %reduce-scatter.12.cloned.1.call-update) | async-done | bytes 131088 | tf_op jit(solution)/shard_map/reduce_scatter | solution.py:268
  909.8 142.1 %reduce-scatter.14.cloned.1.call-done = f32[32,1024]{1,0:T(8,128)} async-done(((f32[1024,1024]{1,0:T(8,128)}), f32[32,1024]{1,0:T(8,128)}) %reduce-scatter.14.cloned.1.call-update) | async-done | bytes 131088 | tf_op jit(solution)/shard_map/reduce_scatter | solution.py:269
  1051.9 249.4 %reduce-scatter.18.cloned.1.call-done = f32[32,2816]{1,0:T(8,128)} async-done(((f32[1024,2816]{1,0:T(8,128)}), f32[32,2816]{1,0:T(8,128)}) %reduce-scatter.18.cloned.1.call-update) | async-done | bytes 360464 | tf_op jit(solution)/shard_map/reduce_scatter | solution.py:254
  1301.3 252.8 %reduce-scatter.20.cloned.1.call-done = f32[32,2816]{1,0:T(8,128)} async-done(((f32[1024,2816]{1,0:T(8,128)}), f32[32,2816]{1,0:T(8,128)}) %reduce-scatter.20.cloned.1.call-update) | async-done | bytes 360464 | tf_op jit(solution)/shard_map/reduce_scatter | solution.py:255
  1554.1 252.6 %reduce-scatter.22.cloned.1.call-done = f32[32,2816]{1,0:T(8,128)} async-done(((f32[1024,2816]{1,0:T(8,128)}), f32[32,2816]{1,0:T(8,128)}) %reduce-scatter.22.cloned.1.call-update) | async-done | bytes 360464
  (412 shorter events, 81.6 us)
Async XLA Ops:
  7.2 63.0 %all-gather.10.cloned.1.call-start = ((), (), s32[]{:S(2)}) async-start(), calls=%async_computation.8 | async-start | bytes 2162688 | tf_op jit(solution)/shard_map/all_gather | solution.py:92
  7.9 120.4 %all-gather.8.cloned.1.call-start = ((), (), s32[]{:S(2)}) async-start(), calls=%async_computation.7 | async-start | bytes 2162688 | tf_op jit(solution)/shard_map/all_gather | solution.py:91
  8.7 177.9 %all-gather.12.cloned.1.call-start = ((), (), s32[]{:S(2)}) async-start(), calls=%async_computation.9 | async-start | bytes 2162688 | tf_op jit(solution)/shard_map/all_gather | solution.py:90
  9.4 235.1 %all-gather.14.cloned.1.call-start = ((), (), s32[]{:S(2)}) async-start(), calls=%async_computation.10 | async-start | bytes 2162688 | tf_op jit(solution)/shard_map/all_gather | solution.py:93
  10.0 303.5 %all-gather.16.cloned.1.call-start = ((), (), s32[]{:S(2)}) async-start(), calls=%async_computation.11 | async-start | bytes 5947392 | tf_op jit(solution)/shard_map/all_gather | solution.py:122
  10.6 371.9 %all-gather.18.cloned.1.call-start = ((), (), s32[]{:S(2)}) async-start(), calls=%async_computation.12 | async-start | bytes 5947392 | tf_op jit(solution)/shard_map/all_gather | solution.py:123
  11.1 440.5 %all-gather.20.cloned.1.call-start = ((), (), s32[]{:S(2)}) async-start(), calls=%async_computation.13 | async-start | bytes 5947392 | tf_op jit(solution)/shard_map/all_gather | solution.py:124
  11.9 613.5 %reduce-scatter.10.cloned.1.call-start = ((), (), s32[]{:S(2)}) async-start(), calls=%async_computation.14 | async-start | bytes 4325376 | tf_op jit(solution)/shard_map/reduce_scatter | solution.py:267
  58.4 72.0 %copy-start.106 = (f32[128]{0:T(128)}, f32[128]{0:T(128)S(1)}, u32[]{:S(2)}) copy-start(f32[128]{0:T(128)S(1)} %get-tuple-element.114) | copy-start | bytes 1540
  59.0 71.4 %copy-start.100 = (f32[128]{0:T(128)}, f32[128]{0:T(128)S(1)}, u32[]{:S(2)}) copy-start(f32[128]{0:T(128)S(1)} %fusion.140) | copy-start | bytes 1540
  59.0 71.4 %copy-start.102 = (f32[128]{0:T(128)}, f32[128]{0:T(128)S(1)}, u32[]{:S(2)}) copy-start(f32[128]{0:T(128)S(1)} %fusion.142) | copy-start | bytes 1540
  60.9 125.6 %copy-start.8 = (bf16[1,128,1024]{2,1,0:T(8,128)(2,1)}, bf16[1,128,1024]{2,1,0:T(8,128)(2,1)S(1)}, u32[]{:S(2)}) copy-start(bf16[1,128,1024]{2,1,0:T(8,128)(2,1)S(1)} %get-tuple-element.130) | copy-start | bytes 786436
  72.2 61.8 %copy-start.4 = (bf16[1024,1024]{1,0:T(8,128)(2,1)S(1)}, bf16[1024,1024]{1,0:T(8,128)(2,1)}, u32[]{:S(2)}) copy-start(bf16[1024,1024]{1,0:T(8,128)(2,1)} %all-gather.10.cloned.1.call-done) | copy-start | bytes 6291460
  131.2 59.2 %collective-permute-start.1 = (bf16[2,1,64,1024]{3,2,1,0:T(8,128)(2,1)}, bf16[2,1,64,1024]{3,2,1,0:T(8,128)(2,1)}, u32[]{:S(2)}, u32[]{:S(2)}) collective-permute-start(bf16[2,1,64,1024]{3,2,1,0:T(8,128)(2,1)} %pad_maximum_fusion.7), channel_id=1, source_target_pairs={{0,4},{4,8},{8,12},{12,16},{16,20},{20,24},{24,28},{1,5},{5,9},{9,... | collective-permute-start | bytes 786440 | tf_op jit(solution)/shard_map/ppermute | solution.py:17
  135.7 56.5 %collective-permute-start = (bf16[2,1,64,1024]{3,2,1,0:T(8,128)(2,1)}, bf16[2,1,64,1024]{3,2,1,0:T(8,128)(2,1)S(1)}, u32[]{:S(2)}, u32[]{:S(2)}) collective-permute-start(bf16[2,1,64,1024]{3,2,1,0:T(8,128)(2,1)} %pad_maximum_fusion.6), channel_id=1, source_target_pairs={{0,4},{4,8},{8,12},{12,16},{16,20},{20,24},{24,28},{1,5},{5,9},{9,... | collective-permute-start | bytes 786440 | tf_op jit(solution)/shard_map/ppermute | solution.py:17
  194.3 53.0 %copy-start.89 = (f32[8,128]{1,0:T(8,128)}, f32[8,128]{1,0:T(8,128)S(1)}, u32[]{:S(2)}) copy-start(f32[8,128]{1,0:T(8,128)S(1)} %fusion.34) | copy-start | bytes 12292
  195.6 49.0 %copy-start.93 = (f32[8,128]{1,0:T(8,128)}, f32[8,128]{1,0:T(8,128)S(1)}, u32[]{:S(2)}) copy-start(f32[8,128]{1,0:T(8,128)S(1)} %fusion.33) | copy-start | bytes 12292
  195.6 49.0 %copy-start.20 = (bf16[2,128,1024]{2,1,0:T(8,128)(2,1)S(1)}, bf16[2,128,1024]{2,1,0:T(8,128)(2,1)}, u32[]{:S(2)}) copy-start(bf16[2,128,1024]{2,1,0:T(8,128)(2,1)} %param.20) | copy-start | bytes 1572868
  196.0 48.6 %copy-start.66 = (bf16[8,128,128]{2,1,0:T(8,128)(2,1)}, bf16[8,128,128]{2,1,0:T(8,128)(2,1)S(1)}, u32[]{:S(2)}) copy-start(bf16[8,128,128]{2,1,0:T(8,128)(2,1)S(1)} %convolution_convert_fusion.6) | copy-start | bytes 786436
  484.6 282.9 %reduce-scatter.16.cloned.1.call-start = ((), (), s32[]{:S(2)}) async-start(), calls=%async_computation.17 | async-start | bytes 4325376 | tf_op jit(solution)/shard_map/reduce_scatter | solution.py:270
  488.4 421.4 %reduce-scatter.12.cloned.1.call-start = ((), (), s32[]{:S(2)}) async-start(), calls=%async_computation.15 | async-start | bytes 4325376 | tf_op jit(solution)/shard_map/reduce_scatter | solution.py:268
  491.7 7.1 collective-permute-start.3
  495.2 4.1 collective-permute-start.2
  502.3 549.6 %reduce-scatter.14.cloned.1.call-start = ((), (), s32[]{:S(2)}) async-start(), calls=%async_computation.16 | async-start | bytes 4325376 | tf_op jit(solution)/shard_map/reduce_scatter | solution.py:269
  505.2 796.2 %reduce-scatter.18.cloned.1.call-start = ((), (), s32[]{:S(2)}) async-start(), calls=%async_computation.18 | async-start | bytes 11894784 | tf_op jit(solution)/shard_map/reduce_scatter | solution.py:254
  512.6 1041.6 %reduce-scatter.20.cloned.1.call-start = ((), (), s32[]{:S(2)}) async-start(), calls=%async_computation.19 | async-start | bytes 11894784 | tf_op jit(solution)/shard_map/reduce_scatter | solution.py:255
  519.8 1286.9 %reduce-scatter.22.cloned.1.call-start = ((), (), s32[]{:S(2)}) async-start(), calls=%async_computation.20 | async-start | bytes 11894784
  557.5 48.0 %copy-start.105 = (f32[128]{0:T(128)S(1)}, f32[128]{0:T(128)}, u32[]{:S(2)}) copy-start(f32[128]{0:T(128)} %copy-done.104) | copy-start | bytes 1540
  557.5 48.0 %copy-start.107 = (f32[128]{0:T(128)S(1)}, f32[128]{0:T(128)}, u32[]{:S(2)}) copy-start(f32[128]{0:T(128)} %copy-done.106) | copy-start | bytes 1540
  557.5 48.1 %copy-start.28 = (f32[128,1024]{1,0:T(8,128)S(1)}, f32[128,1024]{1,0:T(8,128)}, u32[]{:S(2)}) copy-start(f32[128,1024]{1,0:T(8,128)} %copy-done.27) | copy-start | bytes 1572868
  557.5 48.1 %copy-start.96 = (f32[128]{0:T(128)S(1)}, f32[128]{0:T(128)}, u32[]{:S(2)}) copy-start(f32[128]{0:T(128)} %fusion.143) | copy-start | bytes 1540
  557.6 48.1 %copy-start.111 = (f32[128]{0:T(128)S(1)}, f32[128]{0:T(128)}, u32[]{:S(2)}) copy-start(f32[128]{0:T(128)} %copy-done.110) | copy-start | bytes 1540
  (106 other events, 378.8 us)
Sparse Core Ops, SparseCore 0:
  10.9 59.2 all-gather.9
  73.0 55.2 all-gather.7
  131.2 55.2 all-gather.11
  189.3 55.2 all-gather.13
  247.3 66.1 all-gather.15
  316.2 66.2 all-gather.17
  385.4 66.2 all-gather.19
  484.7 140.6 reduce-scatter.9
  628.2 139.1 reduce-scatter.15
  770.2 139.6 reduce-scatter.11
  912.7 139.1 reduce-scatter.13
  1054.7 246.6 reduce-scatter.17
  1304.2 249.8 reduce-scatter.19
  1556.9 249.7 reduce-scatter.21
where the time goes:
time: 1820 us; the launch traced here: 1810 us
  waiting for transfers between devices  1560 us (86%)
  matrix products  94.2 us (5%)
  blocking collectives  87.2 us (5%)
  local copies, waits for them, and re-layouts  40.1 us (2%)
    unnamed x15, waiting for transfers between devices  257 us
    reduce_scatter x1, waiting for transfers between devices, shards(): lax.psum_scatter(grad_up, ('seq', 'rows'), scatter_dimension=0, tiled=True)  253 us
    reduce_scatter x1, waiting for transfers between devices, shards(): lax.psum_scatter(grad_gate, ('seq', 'rows'), scatter_dimension=0, tiled=T...  249 us
    reduce_scatter x1, waiting for transfers between devices, shards(): lax.psum_scatter(grad_key, ('seq', 'rows'), scatter_dimension=0, tiled=True)  142 us
    reduce_scatter x1, waiting for transfers between devices, shards(): lax.psum_scatter(grad_wout, ('seq', 'rows'), scatter_dimension=0, tiled=T...  142 us
    reduce_scatter x1, waiting for transfers between devices, shards(): lax.psum_scatter(grad_value, ('seq', 'rows'), scatter_dimension=0, tiled=...  142 us
    unnamed x2, blocking collectives  87.2 us
    all_gather x1, waiting for transfers between devices, layer_pass(): lax.all_gather(mlp_shards[3], ('seq', 'rows'), axis=0, tiled=True)  64.4 us
  transfers between devices with their start and end apart: 18, of which 15 were waited for; matrix products, arithmetic and copies ran while one was open for 6% of the time, Pallas kernels for 0%

commit v1 on v0

v1 whole, which is shorter than its diff:
```python
import functools
import math

import jax
import jax.numpy as jnp
from jax import lax
from jax.experimental import pallas as pl
from jax.experimental.pallas import tpu as pltpu
from jax.sharding import PartitionSpec as P

HEADS = 8
HEAD_DIM = 128
WINDOW = 64
LANES = 128
MESH = pl.DeviceIdType.MESH


def passed_along(block, axis, distance):
    devices = range(lax.axis_size(axis))
    route = [(i - distance, i) for i in devices if i - distance in devices]
    return lax.ppermute(block, axis, route)


def rms_scale(values, gain):
    factor = lax.rsqrt(jnp.mean(values * values, axis=-1, keepdims=True) + 1e-05)
    return values * factor * gain


def swiglu(gates, ups):
    return jax.nn.silu(gates) * ups


def project(left, weight):
    return jnp.dot(left, weight, preferred_element_type=jnp.float32)


def project_back(grad, weight):
    return lax.dot_general(
        grad, weight, (((2,), (1,)), ((), ())), preferred_element_type=jnp.float32
    )


def weight_grad(left, grad):
    return jnp.einsum("rtd,rtf->df", left, grad, preferred_element_type=jnp.float32)


def split_heads(values):
    return values.reshape(values.shape[0], values.shape[1], HEADS, HEAD_DIM)


def merge_heads(values):
    return values.reshape(values.shape[0], values.shape[1], HEADS * HEAD_DIM)


def window_mask(lengths, seq_index, tokens):
    docs = lengths.shape[1]
    upto = jnp.arange(docs)[:, None] >= jnp.arange(docs)[None, :]
    ends = jnp.sum(jnp.where(upto[None], lengths[:, None, :], 0), axis=2)
    query_pos = seq_index * tokens + jnp.arange(tokens, dtype=jnp.int32)
    key_pos = seq_index * tokens - WINDOW + jnp.arange(tokens + WINDOW, dtype=jnp.int32)
    starts = jnp.max(
        jnp.where(
            ends[:, None, :] <= query_pos[None, :, None],
            ends[:, None, :],
            jnp.zeros_like(ends[:, None, :]),
        ),
        axis=2,
    )
    allowed = (
        (key_pos[None, None, :] >= starts[:, :, None])
        & (key_pos[None, None, :] <= query_pos[None, :, None])
        & (query_pos[None, :, None] - key_pos[None, None, :] < WINDOW)
    )
    return allowed[:, None]


def scores_of(queries, keys_all, allowed):
    score_scale = 1.0 / math.sqrt(HEAD_DIM)
    scores = (
        jnp.einsum(
            "rqhd,rkhd->rhqk",
            split_heads(queries),
            split_heads(keys_all),
            preferred_element_type=jnp.float32,
        )
        * score_scale
    )
    return jnp.where(allowed, scores, -1e30)


def gathered_by_xla(shards):
    return [lax.all_gather(s, ("seq", "rows"), axis=0, tiled=True) for s in shards]


def scattered_by_xla(totals):
    return [
        lax.psum_scatter(t.astype(jnp.float32), ("seq", "rows"), scatter_dimension=0, tiled=True)
        for t in totals
    ]


class Place:
    def __init__(self):
        seq, rows = lax.axis_index("seq"), lax.axis_index("rows")
        self.z, self.c = seq // 2, seq % 2
        self.y, self.x = rows // 2, rows % 2
        self.turn_y, self.turn_x = 1 - 2 * self.y, 1 - 2 * self.x

    def column(self, near, far):
        y, x, c = self.y, self.x, self.c
        if near:
            y, x = y + c * self.turn_y, x + (1 - c) * self.turn_x
        if far:
            y, x = y + (1 - c) * self.turn_y, x + c * self.turn_x
        return y, x

    def device(self, z, c, column):
        return (2 * z + c, 2 * column[0] + column[1])

    def near(self):
        return self.device(self.z, self.c, self.column(True, False))

    def far(self):
        return self.device(self.z, self.c, self.column(False, True))

    def peer(self):
        return self.device(self.z, 1 - self.c, (self.y, self.x))

    def along_z(self, step):
        return self.device((self.z + step) % 4, self.c, (self.y, self.x))

    def partners(self):
        return [self.near(), self.far(), self.peer()] + [self.along_z(i) for i in (1, 2, 3)]


def greet(partners):
    barrier = pltpu.get_barrier_semaphore()
    for partner in partners:
        pl.semaphore_signal(barrier, inc=1, device_id=partner, device_id_type=MESH)
    pl.semaphore_wait(barrier, len(partners))


def remote(source, target, send, recv, device):
    return pltpu.make_async_remote_copy(
        src_ref=source, dst_ref=target, send_sem=send, recv_sem=recv,
        device_id=device, device_id_type=MESH,
    )


def gather_kernel(count, *refs):
    shards, wholes = refs[:count], refs[count : 2 * count]
    own_sem, send, recv = refs[2 * count :]
    here = Place()
    z, c = here.z, here.c
    own, near, far, both = (
        here.column(False, False), here.column(True, False),
        here.column(False, True), here.column(True, True),
    )
    greet(here.partners())

    def block(k, core, column):
        return wholes[k].at[:, core, column[0], column[1]]

    def copy(k, number, view, device):
        return remote(view, view, send.at[k, number], recv.at[k, number], device)

    for k in range(count):
        slot = wholes[k].at[z, c, own[0], own[1]]
        for step in (1, 2, 3):
            remote(shards[k], slot, send.at[k, step - 1], recv.at[k, step - 1], here.along_z(step)).start()
        pltpu.make_async_copy(shards[k], slot, own_sem.at[k]).start()

    def second(k):
        for step in (1, 2, 3):
            slot = wholes[k].at[(z + 4 - step) % 4, c, own[0], own[1]]
            remote(shards[k], slot, send.at[k, step - 1], recv.at[k, step - 1], here.along_z(step)).wait()
        pltpu.make_async_copy(shards[k], wholes[k].at[z, c, own[0], own[1]], own_sem.at[k]).wait()
        copy(k, 3, block(k, c, own), here.near()).start()
        copy(k, 4, block(k, c, own), here.far()).start()
        copy(k, 6, block(k, c, own), here.peer()).start()

    def third(k):
        copy(k, 3, block(k, c, near), here.near()).wait()
        copy(k, 5, block(k, c, near), here.far()).start()
        copy(k, 7, block(k, c, near), here.peer()).start()

    def fourth(k):
        copy(k, 4, block(k, c, far), here.far()).wait()
        copy(k, 8, block(k, c, far), here.peer()).start()
        copy(k, 5, block(k, c, both), here.far()).wait()
        copy(k, 9, block(k, c, both), here.peer()).start()

    def fifth(k):
        for number, column in ((6, own), (7, near), (8, far), (9, both)):
            copy(k, number, block(k, 1 - c, column), here.peer()).wait()

    for tick in range(count + 3):
        for lag, step in enumerate((second, third, fourth, fifth)):
            if 0 <= tick - lag < count:
                step(tick - lag)


def gathered(shards):
    count = len(shards)
    wholes = pl.pallas_call(
        functools.partial(gather_kernel, count),
        out_shape=[jax.ShapeDtypeStruct((4, 2, 2, 2, *s.shape), s.dtype) for s in shards],
        in_specs=[pl.BlockSpec(memory_space=pl.ANY)] * count,
        out_specs=[pl.BlockSpec(memory_space=pl.ANY)] * count,
        scratch_shapes=[
            pltpu.SemaphoreType.DMA((count,)),
            pltpu.SemaphoreType.DMA((count, 10)),
            pltpu.SemaphoreType.DMA((count, 10)),
        ],
        compiler_params=pltpu.CompilerParams(collective_id=0, has_side_effects=True),
        name="gather_weights",
    )(*shards)
    return [w.reshape(-1, w.shape[-1]) for w in wholes]


def scatter_kernel(plan, count, *refs):
    grads, sums = refs[:count], refs[count : 2 * count]
    refs = refs[2 * count :]
    total = len(plan)
    mine, paired, twos, fours = (refs[i * total : (i + 1) * total] for i in range(4))
    own_sem, send, recv = refs[4 * total :]
    here = Place()
    z, c = here.z, here.c
    own, near, far, both = (
        here.column(False, False), here.column(True, False),
        here.column(False, True), here.column(True, True),
    )
    greet(here.partners())

    def own_copy(k):
        number, first, width = plan[k]
        return pltpu.make_async_copy(
            grads[number].at[:, c, :, :, :, pl.ds(first, width)], mine[k], own_sem.at[k]
        )

    def to_peer(k):
        number, first, width = plan[k]
        return remote(
            grads[number].at[:, 1 - c, :, :, :, pl.ds(first, width)], paired[k],
            send.at[k, 0], recv.at[k, 0], here.peer(),
        )

    def to_far(k, which):
        column = both if which else far
        return remote(
            mine[k].at[:, column[0], column[1]], twos[k].at[which],
            send.at[k, 1 + which], recv.at[k, 1 + which], here.far(),
        )

    def to_near(k):
        return remote(
            mine[k].at[:, near[0], near[1]], twos[k].at[2],
            send.at[k, 3], recv.at[k, 3], here.near(),
        )

    def to_z(k, step):
        return remote(
            mine[k].at[(z + step) % 4, own[0], own[1]], fours[k].at[step - 1],
            send.at[k, 3 + step], recv.at[k, 3 + step], here.along_z(step),
        )

    def add(left, right):
        return (left.astype(jnp.float32) + right.astype(jnp.float32)).astype(jnp.bfloat16)

    for k in range(total):
        to_peer(k).start()
        own_copy(k).start()

    def first(k):
        own_copy(k).wait()
        to_peer(k).wait()

        @pl.loop(0, 4)
        def _(level):
            mine[k][level] = add(mine[k][level], paired[k][level])

        to_far(k, 1).start()
        to_far(k, 0).start()

    def second(k):
        to_far(k, 1).wait()

        @pl.loop(0, 4)
        def _(level):
            view = mine[k].at[level, near[0], near[1]]
            view[...] = add(view[...], twos[k][1, level])

        to_near(k).start()
        to_far(k, 0).wait()

        @pl.loop(0, 4)
        def _(level):
            view = mine[k].at[level, own[0], own[1]]
            view[...] = add(view[...], twos[k][0, level])

    def third(k):
        to_near(k).wait()

        @pl.loop(0, 4)
        def _(level):
            view = mine[k].at[level, own[0], own[1]]
            view[...] = add(view[...], twos[k][2, level])

        for step in (1, 2, 3):
            to_z(k, step).start()

    def fourth(k):
        number, begin, width = plan[k]
        for step in (1, 2, 3):
            to_z(k, step).wait()
        value = mine[k][z, own[0], own[1]].astype(jnp.float32)
        for step in (1, 2, 3):
            value = value + fours[k][step - 1].astype(jnp.float32)
        sums[number][:, pl.ds(begin, width)] = value

    for tick in range(total + 3):
        for lag, step in enumerate((first, second, third, fourth)):
            if 0 <= tick - lag < total:
                step(tick - lag)


def scattered(totals):
    count = len(totals)
    block = totals[0].shape[0] // 32
    plan = []
    for number, t in enumerate(totals):
        width = t.shape[1]
        parts = 2 if width > 1024 else 1
        for part in range(parts):
            plan.append((number, part * (width // parts), width // parts))
    halves = [(4, 2, 2, block, width) for _, _, width in plan]
    thirds = [(3, 4, block, width) for _, _, width in plan]
    ends = [(3, block, width) for _, _, width in plan]
    return pl.pallas_call(
        functools.partial(scatter_kernel, plan, count),
        out_shape=[jax.ShapeDtypeStruct((block, t.shape[1]), jnp.float32) for t in totals],
        in_specs=[pl.BlockSpec(memory_space=pl.ANY)] * count,
        out_specs=[pl.BlockSpec(memory_space=pltpu.VMEM)] * count,
        scratch_shapes=[
            *[pltpu.VMEM(s, jnp.bfloat16) for shapes in (halves, halves, thirds, ends) for s in shapes],
            pltpu.SemaphoreType.DMA((len(plan),)),
            pltpu.SemaphoreType.DMA((len(plan), 7)),
            pltpu.SemaphoreType.DMA((len(plan), 7)),
        ],
        compiler_params=pltpu.CompilerParams(
            collective_id=1, has_side_effects=True, vmem_limit_bytes=60 * 2**20
        ),
        name="scatter_grads",
    )(*[t.astype(jnp.bfloat16).reshape(4, 2, 2, 2, block, t.shape[1]) for t in totals])


def layer(hidden_in, lengths, out_grad, gains, weights):
    score_scale = 1.0 / math.sqrt(HEAD_DIM)
    tokens = hidden_in.shape[1]
    gain_one, gain_two = gains
    w_query, w_key, w_value, w_out, w_gate, w_up, w_down = weights
    inputs = hidden_in.astype(jnp.float32)
    normed_one = rms_scale(inputs, gain_one).astype(jnp.bfloat16)
    queries = project(normed_one, w_query).astype(jnp.bfloat16)
    keys = project(normed_one, w_key).astype(jnp.bfloat16)
    values = project(normed_one, w_value).astype(jnp.bfloat16)
    tails = jnp.stack([keys[:, tokens - WINDOW :], values[:, tokens - WINDOW :]])
    received = passed_along(tails, "seq", 1)
    keys_all = jnp.concatenate([received[0], keys], axis=1)
    values_all = jnp.concatenate([received[1], values], axis=1)
    allowed = window_mask(lengths, lax.axis_index("seq"), tokens)
    scores = scores_of(queries, keys_all, allowed)
    top = jnp.max(scores, axis=-1, keepdims=True)
    exps = jnp.exp(scores - top)
    probs = exps / jnp.sum(exps, axis=-1, keepdims=True)
    probs_low = probs.astype(jnp.bfloat16)
    mixed = jnp.einsum(
        "rhqk,rkhd->rqhd", probs_low, split_heads(values_all), preferred_element_type=jnp.float32
    )
    attended = merge_heads(mixed).astype(jnp.bfloat16)
    middle = inputs + project(attended, w_out)
    normed_two = rms_scale(middle, gain_two).astype(jnp.bfloat16)
    gates = project(normed_two, w_gate)
    ups = project(normed_two, w_up)
    hidden_act = swiglu(gates, ups).astype(jnp.bfloat16)
    block_out = (middle + project_back(hidden_act, w_down)).astype(jnp.bfloat16)
    grad_hidden = project(out_grad, w_down)
    unused, swiglu_back = jax.vjp(swiglu, gates, ups)
    grad_gates, grad_ups = swiglu_back(grad_hidden)
    grad_gates = grad_gates.astype(jnp.bfloat16)
    grad_ups = grad_ups.astype(jnp.bfloat16)
    grad_down = weight_grad(out_grad, hidden_act)
    grad_gate = weight_grad(normed_two, grad_gates)
    grad_up = weight_grad(normed_two, grad_ups)
    grad_normed_two = project_back(grad_gates, w_gate) + project_back(grad_ups, w_up)
    unused, norm_two_back = jax.vjp(rms_scale, middle, gain_two)
    grad_middle_part, grad_norm2 = norm_two_back(grad_normed_two)
    grad_middle = out_grad.astype(jnp.float32) + grad_middle_part
    grad_branch = grad_middle.astype(jnp.bfloat16)
    grad_wout = weight_grad(attended, grad_branch)
    grad_attended = project_back(grad_branch, w_out).astype(jnp.bfloat16)
    grad_heads = split_heads(grad_attended)
    grad_values_all = jnp.einsum(
        "rhqk,rqhd->rkhd", probs_low, grad_heads, preferred_element_type=jnp.float32
    )
    grad_probs = jnp.einsum(
        "rqhd,rkhd->rhqk", grad_heads, split_heads(values_all), preferred_element_type=jnp.float32
    )
    grad_scores = (
        probs * (grad_probs - jnp.sum(grad_probs * probs, axis=-1, keepdims=True))
    ).astype(jnp.bfloat16)
    grad_queries = score_scale * merge_heads(
        jnp.einsum(
            "rhqk,rkhd->rqhd", grad_scores, split_heads(keys_all),
            preferred_element_type=jnp.float32,
        )
    )
    grad_keys_all = score_scale * merge_heads(
        jnp.einsum(
            "rhqk,rqhd->rkhd", grad_scores, split_heads(queries),
            preferred_element_type=jnp.float32,
        )
    )
    grad_values_all = merge_heads(grad_values_all)
    halo_grads = jnp.stack([grad_keys_all[:, :WINDOW], grad_values_all[:, :WINDOW]])
    returned = passed_along(halo_grads.astype(jnp.bfloat16), "seq", -1).astype(halo_grads.dtype)
    grad_keys = (
        grad_keys_all[:, WINDOW:].at[:, tokens - WINDOW :].add(returned[0]).astype(jnp.bfloat16)
    )
    grad_values = (
        grad_values_all[:, WINDOW:].at[:, tokens - WINDOW :].add(returned[1]).astype(jnp.bfloat16)
    )
    grad_queries = grad_queries.astype(jnp.bfloat16)
    grad_query = weight_grad(normed_one, grad_queries)
    grad_key = weight_grad(normed_one, grad_keys)
    grad_value = weight_grad(normed_one, grad_values)
    grad_normed_one = (
        project_back(grad_queries, w_query)
        + project_back(grad_keys, w_key)
        + project_back(grad_values, w_value)
    )
    unused, norm_one_back = jax.vjp(rms_scale, inputs, gain_one)
    grad_inputs_part, grad_norm1 = norm_one_back(grad_normed_one)
    grad_in = grad_middle + grad_inputs_part
    grads = (grad_query, grad_key, grad_value, grad_wout, grad_gate, grad_up, grad_down)
    return block_out, grad_in, (grad_norm1, grad_norm2), grads


def shards(
    hidden_in, lengths, norm1_gain, w_query, w_key, w_value, w_out,
    norm2_gain, w_gate, w_up, w_down, out_grad,
):
    gain_shards = (norm1_gain, norm2_gain)
    weight_shards = (w_query, w_key, w_value, w_out, w_gate, w_up, w_down)
    kernels = (lax.axis_size("seq"), lax.axis_size("rows")) == (8, 4)
    if kernels:
        both = jnp.concatenate(
            [jnp.broadcast_to(g[:, None], (g.shape[0], LANES)) for g in gain_shards], axis=1
        )
        both, *weights = gathered([both, *weight_shards])
        gains = [both[:, 0], both[:, LANES]]
    else:
        gains = gathered_by_xla(gain_shards)
        weights = gathered_by_xla(weight_shards)
    gains = [g.astype(jnp.float32) for g in gains]
    block_out, grad_in, norms, grads = layer(hidden_in, lengths, out_grad, gains, weights)
    if kernels:
        both = jnp.concatenate(
            [jnp.broadcast_to(g[:, None], (g.shape[0], LANES)) for g in norms], axis=1
        )
        *grads, both = scattered([*grads, both])
        norms = [both[:, 0], both[:, LANES]]
    else:
        norms = scattered_by_xla(norms)
        grads = scattered_by_xla(grads)
    return (
        block_out, grad_in, norms[0], grads[0], grads[1], grads[2], grads[3],
        norms[1], grads[4], grads[5], grads[6],
    )


def solution(mesh):
    tokens = P("rows", "seq", None)
    vector = P(("seq", "rows"))
    matrix = P(("seq", "rows"), None)
    in_specs = (
        tokens, P("rows", None), vector, matrix, matrix, matrix, matrix,
        vector, matrix, matrix, matrix, tokens,
    )
    out_specs = (
        tokens, tokens, vector, matrix, matrix, matrix, matrix,
        vector, matrix, matrix, matrix,
    )
    return jax.shard_map(shards, mesh=mesh, in_specs=in_specs, out_specs=out_specs, check_vma=False)
```

time: 1820 us -> 365 us (0.20)
  waiting for transfers between devices: 1560 us -> 0.01 us
  Pallas kernels: 0 us -> 274 us
  blocking collectives: 87.2 us -> 0 us
  matrix products: 94.2 us -> 55.2 us
  local copies, waits for them, and re-layouts: 40.1 us -> 18.5 us
    reduce_scatter x6 -> x0, waiting for transfers between devices: 946 us -> none  [the longest x1 253 us: shards(): lax.psum_scatter(grad_up, ('seq', 'rows'), scatter_dimension=0, tiled=True)]
    all_gather x7 -> x0, waiting for transfers between devices: 353 us -> none  [the longest x1 64.4 us: layer_pass(): lax.all_gather(mlp_shards[3], ('seq', 'rows'), axis=0, tiled=True)]
    pallas_call x0 -> x2, Pallas kernels: none -> 274 us  [the longest x1 140 us: scattered(): pl.pallas_call(functools.partial(scatter_kernel, plan, count), out_shape=...]
    unnamed x15 -> x0, waiting for transfers between devices: 257 us -> none
    unnamed x2 -> x0, blocking collectives: 87.2 us -> none
    unnamed x265 -> x89, local copies, waits for them, and re-layouts: 31 us -> 11.4 us
  transfers between devices with their start and end apart: 18 -> 2, of which waited for: 15 -> 0; matrix products, arithmetic and copies ran while one was open for 6% -> 4% of each run, Pallas kernels for 0% -> 0%
where the time goes in v1:
time: 365 us; the launch traced here: 364 us
  Pallas kernels  274 us (75%)
  matrix products  55.2 us (15%)
  local copies, waits for them, and re-layouts  18.5 us (5%)
  other arithmetic  10.6 us (3%)
  starting transfers between devices  4.6 us (1%)
    pallas_call x1, Pallas kernels, scattered(): pl.pallas_call(functools.partial(scatter_kernel, plan, count), out_shape=...  140 us
    pallas_call x1, Pallas kernels, gathered(): pl.pallas_call(functools.partial(gather_kernel, count), out_shape=[jax.Sh...  134 us
    dot_general x7, matrix products, weight_grad(): jnp.einsum('rtd,rtf->df', left, grad, preferred_element_type=jnp.float32)  22.9 us
    dot_general x7, matrix products, project(): return jnp.dot(left, weight, preferred_element_type=jnp.float32)  14.5 us
    dot_general x7, matrix products, project_back(): lax.dot_general(grad, weight, (((2,), (1,)), ((), ())), preferred_element...  13.1 us
    unnamed x89, local copies, waits for them, and re-layouts  11.4 us
  transfers between devices with their start and end apart: 2, of which 0 were waited for; matrix products, arithmetic and copies ran while one was open for 4% of the time, Pallas kernels for 0%

profile of v1, /device:TPU:0, one launch (start us, length us, event | category | flops | bytes accessed | tf_op | source)
XLA Modules:
  0.0 364.5 jit_solution(18054131602992724329)
XLA Ops:
  0.7 1.3 fusion.17
  4.0 134.0 %gather_weights.1 = (bf16[4,2,2,2,32,256]{5,4,3,2,1,0:T(8,128)(2,1)}, bf16[4,2,2,2,32,1024]{5,4,3,2,1,0:T(8,128)(2,1)}, bf16[4,2,2,2,32,1024]{5,4,3,2,1,0:T(8,12...) custom-call(bf16[32,256]{1,0:T(8,128)(2,1)} %pad_maximum_fusion.3.re, ...), custom_call_target="tpu_custom_call" | custom-call | tf_op jit(solution)/shard_map/gather_weights/pallas_call | solution.py:205
  138.1 2.0 slice_convert_fusion.2
  140.1 1.2 copy.110
  145.4 3.1 collective-permute-start
  149.1 1.6 fusion.11
  150.7 1.2 fusion.57
  152.2 0.9 copy-done.29
  154.0 2.2 convolution_convert_fusion.1
  157.5 4.8 %fusion.62 = f32[2,128,2816]{2,1,0:T(8,128)S(1)} fusion(bf16[2,128,1024]{2,1,0:T(8,128)(2,1)S(1)} %multiply_convert_fusion.3, bf16[1024,2816,1]{1,0,2:T(8,128)(2,1)} %bitcast.179), kind=kOutput, calls=%fused_computation.121 | convolution fusion | flops 1476395008 | bytes 9175040 | tf_op jit(solution)/shard_map/dot_general | solution.py:34
  162.3 1.7 fusion.61
  164.1 4.1 %multiply_convert_fusion = (bf16[2,128,2816]{2,1,0:T(8,128)(2,1)S(1)}, bf16[2,128,2816]{2,1,0:T(8,128)(2,1)S(1)}, bf16[2,128,2816]{2,1,0:T(8,128)(2,1)}) fusion(f32[2,128,2816]{2,1,0:T(8,128)S(1)} %fusion.61, f32[2,128,2816]{2,1,0:T(8,128)S(1)} %fusion.62, bf16[1024,2816,1]{1,0,2:T(8,128)(2,1)S(1)} %bitcast.222, bf16[2,128,1024]{2,1,0:T(8,128)(2,1)S(1)} %copy-done.13), kind=kOutput, calls=%fused_computation.13 | convolution fusion | flops 1487929344 | bytes 16384000 | tf_op jit(solution)/shard_map/dot_general | solution.py:34
  168.2 1.7 fusion.63
  169.9 1.9 multiply_reduce_fusion.1
  178.7 0.9 slice.121
  179.5 2.0 bitcast_convert_fusion.3
  181.6 1.7 fusion.64
  183.3 2.2 bitcast_convert_fusion.6
  185.5 4.2 %bitcast_convert_fusion.1 = bf16[1024,2816]{1,0:T(8,128)(2,1)} fusion(bf16[2,128,1024]{2,1,0:T(8,128)(2,1)S(1)} %multiply_convert_fusion.3, bf16[2,128,2816]{2,1,0:T(8,128)(2,1)S(1)} %get-tuple-element.73), kind=kOutput, calls=%fused_computation.2 | convolution fusion | flops 1479278592 | bytes 7733248 | tf_op jit(solution)/shard_map/rtd,rtf->df/dot_general | solution.py:44
  189.7 4.2 %bitcast_convert_fusion.2 = bf16[1024,2816]{1,0:T(8,128)(2,1)} fusion(bf16[2,128,1024]{2,1,0:T(8,128)(2,1)S(1)} %multiply_convert_fusion.3, bf16[2,128,2816]{2,1,0:T(8,128)(2,1)S(1)} %get-tuple-element.74), kind=kOutput, calls=%fused_computation.3 | convolution fusion | flops 1479278592 | bytes 7733248 | tf_op jit(solution)/shard_map/rtd,rtf->df/dot_general | solution.py:44
  194.0 1.0 pad_maximum_fusion.1
  195.0 1.5 collective-permute-start.1
  196.5 5.8 %bitcast_convert_fusion = bf16[2816,1024]{0,1:T(8,128)(2,1)} fusion(bf16[2,128,2816]{2,1,0:T(8,128)(2,1)} %get-tuple-element.75, bf16[2,128,1024]{2,1,0:T(8,128)(2,1)} %param.27), kind=kOutput, calls=%fused_computation.1 | convolution fusion | flops 1479278592 | bytes 7733248 | tf_op jit(solution)/shard_map/rtd,rtf->df/dot_general | solution.py:44
  202.3 5.2 %fusion.7 = bf16[2,128,1024]{2,1,0:T(8,128)(2,1)} fusion(f32[2,128,1024]{2,1,0:T(8,128)S(1)} %get-tuple-element.87, bf16[2,128,2816]{2,1,0:T(8,128)(2,1)S(1)} %copy-done.6, bf16[1024,2816,1]{1,0,2:T(8,128)(2,1)} %bitcast.219), kind=kOutput, calls=%fused_computation.38 | convolution fusion | flops 1476919296 | bytes 8781824 | tf_op jit(solution)/shard_map/dot_general | solution.py:38
  207.6 1.3 fusion.25
  209.0 2.2 bitcast_convert_fusion.5
  212.0 2.2 bitcast_convert_fusion.4
  214.2 1.1 fusion.14
  215.8 0.9 pad_maximum_fusion.2.refs_7_
  216.7 140.2 %scatter_grads.1 = (f32[32,1024]{1,0:T(8,128)}, f32[32,1024]{1,0:T(8,128)}, f32[32,1024]{1,0:T(8,128)}, f32[32,1024]{1,0:T(8,128)}, f32[32,2816]{1,0:T(8,128)}, ...) custom-call(bf16[4,2,2,2,32,1024]{5,4,3,2,1,0:T(8,128)(2,1)} %bitcast.176, ...), custom_call_target="tpu_custom_call" | custom-call | tf_op jit(solution)/shard_map/scatter_grads/pallas_call | solution.py:339
  356.9 1.4 slice_reduce_fusion
  358.4 1.3 fusion.16
  (133 shorter events, 22.1 us)
Async XLA Ops:
  0.6 140.7 %copy-start = (bf16[2,128,1024]{2,1,0:T(8,128)(2,1)S(1)}, bf16[2,128,1024]{2,1,0:T(8,128)(2,1)}, u32[]{:S(2)}) copy-start(bf16[2,128,1024]{2,1,0:T(8,128)(2,1)} %param.16) | copy-start | bytes 1572868
  138.1 3.3 copy-start.7
  141.3 1.6 copy-start.11
  142.1 2.4 copy-start.18
  142.9 5.6 %copy-start.31 = (s32[2,16]{1,0:T(2,128)S(1)}, s32[2,16]{1,0:T(2,128)}, u32[]{:S(2)}) copy-start(s32[2,16]{1,0:T(2,128)} %param.17) | copy-start | bytes 388
  144.5 4.6 %copy-start.9 = (bf16[4,2,2,2,32,1024]{5,4,3,2,1,0:T(8,128)(2,1)S(1)}, bf16[4,2,2,2,32,1024]{5,4,3,2,1,0:T(8,128)(2,1)}, u32[]{:S(2)}) copy-start(bf16[4,2,2,2,32,1024]{5,4,3,2,1,0:T(8,128)(2,1)} %get-tuple-element.54) | copy-start | bytes 6291460
  145.4 5.3 %collective-permute-start = (bf16[2,2,64,1024]{3,2,1,0:T(8,128)(2,1)}, bf16[2,2,64,1024]{3,2,1,0:T(8,128)(2,1)}, u32[]{:S(2)}, u32[]{:S(2)}) collective-permute-start(bf16[2,2,64,1024]{3,2,1,0:T(8,128)(2,1)} %pad_maximum_fusion), channel_id=1, source_target_pairs={{0,4},{4,8},{8,12},{12,16},{16,20},{20,24},{24,28},{1,5},{5,9},{9,... | collective-permute-start | bytes 1572872 | tf_op jit(solution)/shard_map/ppermute | solution.py:21
  150.7 2.4 copy-start.17
  154.0 2.3 copy-start.14
  154.0 2.4 copy-start.1
  156.4 7.6 %slice-start.4 = ((s8[5767168]{0:T(1024)(128)(4,1)}), s8[4194304]{0:T(1024)(128)(4,1)S(1)}, s32[]{:S(2)}) async-start(s8[5767168]{0:T(1024)(128)(4,1)} %bitcast.220), calls=%async_computation.4 | async-start | bytes 8388608
  157.3 5.0 %slice-start.2 = ((s8[5767168]{0:T(1024)(128)(4,1)}), s8[4194304]{0:T(1024)(128)(4,1)S(1)}, s32[]{:S(2)}) async-start(s8[5767168]{0:T(1024)(128)(4,1)} %bitcast.183), calls=%async_computation.2 | async-start | bytes 8388608
  157.4 4.8 %slice-start.3 = ((s8[5767168]{0:T(1024)(128)(4,1)}), s8[1572864]{0:T(1024)(128)(4,1)S(1)}, s32[]{:S(2)}) async-start(s8[5767168]{0:T(1024)(128)(4,1)} %bitcast.183), calls=%async_computation.3 | async-start | bytes 3145728
  157.5 6.6 %slice-start.5 = ((s8[5767168]{0:T(1024)(128)(4,1)}), s8[1572864]{0:T(1024)(128)(4,1)S(1)}, s32[]{:S(2)}) async-start(s8[5767168]{0:T(1024)(128)(4,1)} %bitcast.220), calls=%async_computation.5 | async-start | bytes 3145728
  162.3 1.7 copy-start.13
  162.3 7.6 %slice-start = ((s8[5767168]{0:T(1024)(128)(4,1)}), s8[4194304]{0:T(1024)(128)(4,1)S(1)}, s32[]{:S(2)}) async-start(s8[5767168]{0:T(1024)(128)(4,1)} %bitcast.180), calls=%async_computation | async-start | bytes 8388608
  164.0 5.8 %slice-start.1 = ((s8[5767168]{0:T(1024)(128)(4,1)}), s8[1572864]{0:T(1024)(128)(4,1)S(1)}, s32[]{:S(2)}) async-start(s8[5767168]{0:T(1024)(128)(4,1)} %bitcast.180), calls=%async_computation.1 | async-start | bytes 3145728
  172.2 1.6 copy-start.30
  179.5 2.1 copy-start.10
  195.0 12.5 %collective-permute-start.1 = (bf16[2,2,64,1024]{3,2,1,0:T(8,128)(2,1)S(1)}, bf16[2,2,64,1024]{3,2,1,0:T(8,128)(2,1)S(1)}, u32[]{:S(2)}, u32[]{:S(2)}) collective-permute-start(bf16[2,2,64,1024]{3,2,1,0:T(8,128)(2,1)S(1)} %pad_maximum_fusion.1), channel_id=1, source_target_pairs={{4,0},{8,4},{12,8},{16,12},{20,16},{24,20},{28,24},{5,1},{9,5},{13... | collective-permute-start | bytes 1572872 | tf_op jit(solution)/shard_map/ppermute | solution.py:21
  196.5 5.8 %copy-start.6 = (bf16[2,128,2816]{2,1,0:T(8,128)(2,1)S(1)}, bf16[2,128,2816]{2,1,0:T(8,128)(2,1)}, u32[]{:S(2)}) copy-start(bf16[2,128,2816]{2,1,0:T(8,128)(2,1)} %get-tuple-element.75) | copy-start | bytes 4325380
  202.3 5.3 %copy-start.4 = (bf16[2,128,1024]{2,1,0:T(8,128)(2,1)S(1)}, bf16[2,128,1024]{2,1,0:T(8,128)(2,1)}, u32[]{:S(2)}) copy-start(bf16[2,128,1024]{2,1,0:T(8,128)(2,1)} %slice.121) | copy-start | bytes 1572868
  209.0 2.2 copy-start.5
  209.0 2.2 copy-start.12
  211.9 2.2 copy-start.8
  356.9 2.7 copy-start.28
  356.9 3.3 copy-start.27
  358.4 2.6 copy-start.26
  358.4 3.2 copy-start.25
  358.4 3.9 %copy-start.24 = (f32[32,2816]{1,0:T(8,128)S(1)}, f32[32,2816]{1,0:T(8,128)}, u32[]{:S(2)}) copy-start(f32[32,2816]{1,0:T(8,128)} %get-tuple-element.113) | copy-start | bytes 1081348
  358.4 4.6 %copy-start.23 = (f32[32,2816]{1,0:T(8,128)S(1)}, f32[32,2816]{1,0:T(8,128)}, u32[]{:S(2)}) copy-start(f32[32,2816]{1,0:T(8,128)} %get-tuple-element.114) | copy-start | bytes 1081348
  359.6 4.1 %copy-start.22 = (f32[32,2816]{1,0:T(8,128)S(1)}, f32[32,2816]{1,0:T(8,128)}, u32[]{:S(2)}) copy-start(f32[32,2816]{1,0:T(8,128)} %get-tuple-element.115) | copy-start | bytes 1081348
  (8 other events, 9.3 us)

commit v2 on v1

--- a/solution.py
+++ b/solution.py
@@ -129,6 +129,15 @@
     def along_z(self, step):
         return self.device((self.z + step) % 4, self.c, (self.y, self.x))
 
+    def following(self):
+        return ((2 * self.z + self.c + 1) % 8, 2 * self.y + self.x)
+
+    def preceding(self):
+        return ((2 * self.z + self.c + 7) % 8, 2 * self.y + self.x)
+
+    def cross(self):
+        return ((2 * self.z + self.c + 7 - 6 * self.c) % 8, 2 * self.y + self.x)
+
     def partners(self):
         return [self.near(), self.far(), self.peer()] + [self.along_z(i) for i in (1, 2, 3)]
 
@@ -147,211 +156,721 @@
     )
 
 
-def gather_kernel(count, *refs):
-    shards, wholes = refs[:count], refs[count : 2 * count]
-    own_sem, send, recv = refs[2 * count :]
+SEQ_PIECES = 8
+ROW_GROUPS = 4
+TILE = 256
+HALF = 512
+PAD = 128
+
+
+def nt_dot(left, right):
+    return lax.dot_general(left, right, (((1,), (1,)), ((), ())), preferred_element_type=jnp.float32)
+
+
+def tn_dot(left, right):
+    return lax.dot_general(left, right, (((0,), (0,)), ((), ())), preferred_element_type=jnp.float32)
+
+
+def mm(left, right):
+    return jnp.dot(left, right, preferred_element_type=jnp.float32)
+
+
+def flat(value):
+    return value.reshape(-1, value.shape[-1])
+
+
+class Gather:
+    def __init__(self, here, own_sem, send, recv):
+        self.here, self.own_sem, self.send, self.recv = here, own_sem, send, recv
+        self.own, self.near = here.column(False, False), here.column(True, False)
+        self.far, self.both = here.column(False, True), here.column(True, True)
+
+    def slot(self, whole, z):
+        return whole.at[z, self.here.c, self.own[0], self.own[1]]
+
+    def block(self, whole, core, column):
+        return whole.at[:, core, column[0], column[1]]
+
+    def copy(self, k, number, view, device):
+        return remote(view, view, self.send.at[k, number], self.recv.at[k, number], device)
+
+    def fetch(self, k, parts, whole):
+        slot = self.slot(whole, self.here.z)
+        return [
+            pltpu.make_async_copy(view, slot.at[:, pl.ds(first, width)], self.own_sem.at[k, i])
+            for i, (view, first, width) in enumerate(parts)
+        ]
+
+    def first(self, k, parts, whole):
+        for copy in self.fetch(k, parts, whole):
+            copy.wait()
+        slot = self.slot(whole, self.here.z)
+        for step in (1, 2, 3):
+            self.copy(k, step - 1, slot, self.here.along_z(step)).start()
+
+    def second(self, k, whole):
+        here = self.here
+        for step in (1, 2, 3):
+            self.copy(k, step - 1, self.slot(whole, (here.z + 4 - step) % 4), here.along_z(step)).wait()
+        block = self.block(whole, here.c, self.own)
+        self.copy(k, 3, block, here.near()).start()
+        self.copy(k, 4, block, here.far()).start()
+        self.copy(k, 6, block, here.peer()).start()
+
+    def third(self, k, whole):
+        here = self.here
+        block = self.block(whole, here.c, self.near)
+        self.copy(k, 3, block, here.near()).wait()
+        self.copy(k, 5, block, here.far()).start()
+        self.copy(k, 7, block, here.peer()).start()
+
+    def fourth(self, k, whole):
+        here = self.here
+        for number, column in ((4, self.far), (5, self.both)):
+            block = self.block(whole, here.c, column)
+            self.copy(k, number, block, here.far()).wait()
+            self.copy(k, number + 4, block, here.peer()).start()
+
+    def fifth(self, k, whole):
+        here = self.here
+        for number, column in ((6, self.own), (7, self.near), (8, self.far), (9, self.both)):
+            self.copy(k, number, self.block(whole, 1 - here.c, column), here.peer()).wait()
+
+
+def forward_kernel(
+    x_ref, og_ref, lengths_ref, gains_in, wq_in, wk_in, wv_in, wo_in, wg_in, wu_in, wd_in,
+    out_ref, gm_ref, no_ref, q_ref, k_ref, v_ref, at_ref, p_ref, wa_out, gr_out, norm_ref,
+    wn, wa, wm, mid, acc, gn, nt, side, side_peer, nt_t, og_t, tri, tri_peer, stage,
+    own_sem, send, recv, halo_send, halo_recv, side_send, side_recv, tri_send, tri_recv,
+    keep_sem, stage_sem,
+):
     here = Place()
     z, c = here.z, here.c
-    own, near, far, both = (
-        here.column(False, False), here.column(True, False),
-        here.column(False, True), here.column(True, True),
-    )
-    greet(here.partners())
-
-    def block(k, core, column):
-        return wholes[k].at[:, core, column[0], column[1]]
-
-    def copy(k, number, view, device):
-        return remote(view, view, send.at[k, number], recv.at[k, number], device)
-
-    for k in range(count):
-        slot = wholes[k].at[z, c, own[0], own[1]]
+    seq = lax.axis_index("seq")
+    tiles = wm.shape[0]
+    scale = 1.0 / math.sqrt(HEAD_DIM)
+    tokens = x_ref.shape[0] // 2
+    gather = Gather(here, own_sem, send, recv)
+
+    attn = [(gains_in, 0, LANES)]
+    for source in (wk_in, wv_in, wq_in, wo_in):
+        attn += [(source, 0, HALF), (source, HALF, HALF)]
+    early = len(attn)
+    total = early + tiles
+
+    def whole_of(k):
+        return wn if k == 0 else wa.at[k - 1]
+
+    def attn_parts(k):
+        source, first, width = attn[k]
+        return [(source.at[:, pl.ds(first, width)], 0, width)]
+
+    def mlp_parts(f):
+        column = pl.ds(pl.multiple_of(f * TILE, TILE), TILE)
+        return [(w.at[:, column], i * TILE, TILE) for i, w in enumerate((wg_in, wu_in, wd_in))]
+
+    for k in range(early):
+        for copy in gather.fetch(k, attn_parts(k), whole_of(k)):
+            copy.start()
+
+    @pl.loop(0, tiles)
+    def _(f):
+        for copy in gather.fetch(early + f, mlp_parts(f), wm.at[f]):
+            copy.start()
+
+    @pl.when(seq == 0)
+    def _():
+        k_ref[:, 0:PAD, :] = jnp.zeros((2, PAD, k_ref.shape[2]), jnp.bfloat16)
+        v_ref[:, 0:PAD, :] = jnp.zeros((2, PAD, v_ref.shape[2]), jnp.bfloat16)
+
+    @pl.when(seq > 0)
+    def _():
+        k_ref[:, 0 : PAD - WINDOW, :] = jnp.zeros((2, PAD - WINDOW, k_ref.shape[2]), jnp.bfloat16)
+        v_ref[:, 0 : PAD - WINDOW, :] = jnp.zeros((2, PAD - WINDOW, v_ref.shape[2]), jnp.bfloat16)
+
+    greet(here.partners() + [here.cross()])
+
+    def tick(t):
+        for lag in range(5):
+            k = t - lag
+            if not 0 <= k < total:
+                continue
+            whole = whole_of(k) if k < early else wm.at[k - early]
+            if lag == 0:
+                gather.first(k, attn_parts(k) if k < early else mlp_parts(k - early), whole)
+            else:
+                (gather.second, gather.third, gather.fourth, gather.fifth)[lag - 1](k, whole)
+
+    def keep(k):
+        return pltpu.make_async_copy(wa.at[k - 1], wa_out.at[k - 1], keep_sem.at[k - 1])
+
+    def halo(which):
+        ref = (k_ref, v_ref)[which]
+        ends = ref.at[:, pl.ds(ref.shape[1] - WINDOW, WINDOW), :]
+        begins = ref.at[:, pl.ds(PAD - WINDOW, WINDOW), :]
+        return remote(ends, begins, halo_send.at[which], halo_recv.at[which], here.following())
+
+    def sides(number):
+        return remote(
+            side.at[number, :, 1 - c], side_peer.at[number],
+            side_send.at[number], side_recv.at[number], here.peer(),
+        )
+
+    def spread(number, value):
+        for i in range(8):
+            side[number, i // 2, i % 2] = value[:, i * LANES : (i + 1) * LANES]
+
+    def turned(number, target):
+        for level in range(4):
+            rows = slice(level * LANES, (level + 1) * LANES)
+            target[rows, 0 : 2 * tokens] = (
+                side[number, level, c].astype(jnp.float32).T.astype(jnp.bfloat16)
+            )
+            target[rows, 2 * tokens : 4 * tokens] = (
+                side_peer[number, level].astype(jnp.float32).T.astype(jnp.bfloat16)
+            )
+
+    for t in range(4):
+        tick(t)
+        if t == 1:
+            spread(0, og_ref[...])
+            sides(0).start()
+        if t == 3:
+            sides(0).wait()
+            turned(0, og_t)
+
+    tick(4)
+    gain_rows = flat(wn[...]).astype(jnp.float32).T
+    norm_ref[0:8, :] = jnp.broadcast_to(gain_rows[0:1, :], (8, gain_rows.shape[1]))
+    norm_ref[8:16, :] = jnp.broadcast_to(gain_rows[64:65, :], (8, gain_rows.shape[1]))
+    x = x_ref[...].astype(jnp.float32)
+    factor = lax.rsqrt(jnp.mean(x * x, axis=-1, keepdims=True) + 1e-05)
+    no_ref[...] = (x * factor * norm_ref[0:1, :]).astype(jnp.bfloat16)
+
+    def projected(k):
+        tick(4 + k)
+        keep(k).start()
+        return mm(no_ref[...], flat(wa[k - 1])).astype(jnp.bfloat16)
+
+    for k in range(1, 7):
+        part = projected(k)
+        cols = slice(((k - 1) % 2) * HALF, ((k - 1) % 2 + 1) * HALF)
+        if k < 5:
+            ref = k_ref if k < 3 else v_ref
+            ref[:, PAD : PAD + tokens, cols] = part.reshape(2, tokens, HALF)
+        else:
+            q_ref[:, cols] = part
+        if k in (2, 4):
+
+            @pl.when(seq < SEQ_PIECES - 1)
+            def _(which=k // 2 - 1):
+                halo(which).start()
+
+    for which in range(2):
+
+        @pl.when(seq > 0)
+        def _(which=which):
+            halo(which).wait_recv()
+
+        @pl.when(seq < SEQ_PIECES - 1)
+        def _(which=which):
+            halo(which).wait_send()
+
+    def attend(row):
+        ends = []
+        reached = 0
+        for doc in range(lengths_ref.shape[1]):
+            reached = reached + lengths_ref[row, doc]
+            ends.append(reached)
+        query_pos = seq * tokens + lax.broadcasted_iota(jnp.int32, (tokens, PAD + tokens), 0)
+        key_pos = seq * tokens - PAD + lax.broadcasted_iota(jnp.int32, (tokens, PAD + tokens), 1)
+        start = jnp.zeros((tokens, PAD + tokens), jnp.int32)
+        for end in ends:
+            start = jnp.maximum(start, jnp.where(query_pos >= end, end, 0))
+        allowed = (key_pos >= start) & (key_pos <= query_pos) & (query_pos - key_pos < WINDOW)
+        for head in range(HEADS):
+            cols = slice(head * HEAD_DIM, (head + 1) * HEAD_DIM)
+            rows = slice(row * tokens, (row + 1) * tokens)
+            scores = nt_dot(q_ref[rows, cols], k_ref[row, :, cols]) * scale
+            scores = jnp.where(allowed, scores, -1e30)
+            exps = jnp.exp(scores - jnp.max(scores, axis=-1, keepdims=True))
+            probs = exps / jnp.sum(exps, axis=-1, keepdims=True)
+            p_ref[row * HEADS + head] = probs
+            at_ref[rows, cols] = mm(probs.astype(jnp.bfloat16), v_ref[row, :, cols]).astype(jnp.bfloat16)
+
+    attend(0)
+    tick(11)
+    keep(7).start()
+    attend(1)
+    tick(12)
+    keep(8).start()
+    for k in (7, 8):
+        cols = slice((k - 7) * HALF, (k - 6) * HALF)
+        mid[:, cols] = x_ref[:, cols].astype(jnp.float32) + mm(at_ref[...], flat(wa[k - 1]))
+
+    middle = mid[...]
+    factor = lax.rsqrt(jnp.mean(middle * middle, axis=-1, keepdims=True) + 1e-05)
+    normed_two = (middle * factor * norm_ref[8:9, :]).astype(jnp.bfloat16)
+    nt[...] = normed_two
+    spread(1, normed_two)
+    sides(1).start()
+    acc[...] = middle
+    gn[...] = jnp.zeros(gn.shape, jnp.float32)
+    sides(1).wait()
+    turned(1, nt_t)
+
+    def to_peer(f):
+        return remote(tri.at[f % 2], tri_peer.at[f], tri_send.at[f], tri_recv.at[f], here.peer())
+
+    def stored(f):
+        return pltpu.make_async_copy(stage.at[f % 2], gr_out.at[f], stage_sem.at[f])
+
+    def weight_grads(f):
+        to_peer(f).wait()
+
+        @pl.when(f >= 2)
+        def _():
+            stored(f - 2).wait()
+
+        n = 2 * tokens
+        for i, turn in ((0, nt_t), (1, nt_t), (2, og_t)):
+            grad = mm(turn[:, 0:n], tri[f % 2, i]) + mm(turn[:, n : 2 * n], tri_peer[f, i])
+            stage[f % 2, :, :, :, :, i * TILE : (i + 1) * TILE] = (
+                grad.astype(jnp.bfloat16).reshape(4, 2, 2, -1, TILE)
+            )
+        stored(f).start()
+
+    @pl.loop(0, tiles)
+    def _(f):
+        for lag, step in enumerate((None, gather.second, gather.third, gather.fourth)):
+            ahead = f + 4 - lag
+
+            @pl.when(ahead < tiles)
+            def _(ahead=ahead, step=step):
+                if step is None:
+                    gather.first(early + ahead, mlp_parts(ahead), wm.at[ahead])
+                else:
+                    step(early + ahead, wm.at[ahead])
+
+        gather.fifth(early + f, wm.at[f])
+        w_gate = flat(wm[f, :, :, :, :, :, 0:TILE])
+        w_up = flat(wm[f, :, :, :, :, :, TILE : 2 * TILE])
+        w_down = flat(wm[f, :, :, :, :, :, 2 * TILE : 3 * TILE])
+        gates = mm(nt[...], w_gate)
+        ups = mm(nt[...], w_up)
+        grad_hidden = mm(og_ref[...], w_down)
+        sigmoid = 1.0 / (1.0 + jnp.exp(-gates))
+        silu = gates * sigmoid
+        hidden = (silu * ups).astype(jnp.bfloat16)
+        grad_gates = (grad_hidden * ups * sigmoid * (1.0 + gates * (1.0 - sigmoid))).astype(jnp.bfloat16)
+        grad_ups = (grad_hidden * silu).astype(jnp.bfloat16)
+        tri[f % 2, 0] = grad_gates
+        tri[f % 2, 1] = grad_ups
+        tri[f % 2, 2] = hidden
+        to_peer(f).start()
+        acc[...] += nt_dot(hidden, w_down)
+        gn[...] += nt_dot(grad_gates, w_gate) + nt_dot(grad_ups, w_up)
+
+        @pl.when(f >= 1)
+        def _():
+            weight_grads(f - 1)
+
+    weight_grads(tiles - 1)
+    out_ref[...] = acc[...].astype(jnp.bfloat16)
+    middle = mid[...]
+    factor = lax.rsqrt(jnp.mean(middle * middle, axis=-1, keepdims=True) + 1e-05)
+    grad_normed = gn[...]
+    through = grad_normed * norm_ref[8:9, :]
+    shift = jnp.mean(through * middle, axis=-1, keepdims=True) * factor * factor * factor
+    gm_ref[...] = og_ref[...].astype(jnp.float32) + factor * through - middle * shift
+    norm_ref[8:16, :] = jnp.broadcast_to(
+        jnp.sum(grad_normed * middle * factor, axis=0, keepdims=True), (8, middle.shape[1])
+    )
+    stored(tiles - 2).wait()
+    stored(tiles - 1).wait()
+    for k in range(1, early):
+        keep(k).wait()
+
+
+def forward(hidden, out_grad, lengths, gains, weights):
+    tokens, width = hidden.shape
+    rows = gains.shape[0]
+    tiles = weights[4].shape[1] // TILE
+    low, full = jnp.bfloat16, jnp.float32
+    whole = (4, 2, 2, 2, rows)
+    early = 9
+    count = early + tiles
+    dma = pltpu.SemaphoreType.DMA
+    vmem, anywhere = pl.BlockSpec(memory_space=pltpu.VMEM), pl.BlockSpec(memory_space=pl.ANY)
+    shape = jax.ShapeDtypeStruct
+    keys = (2, PAD + tokens // 2, width)
+    return pl.pallas_call(
+        forward_kernel,
+        out_shape=[
+            shape((tokens, width), low), shape((tokens, width), full), shape((tokens, width), low),
+            shape((tokens, width), low), shape(keys, low), shape(keys, low),
+            shape((tokens, width), low), shape((2 * HEADS, tokens // 2, PAD + tokens // 2), full),
+            shape((8, *whole, HALF), low), shape((tiles, 4, 2, 2, rows, 3 * TILE), low),
+            shape((16, width), full),
+        ],
+        in_specs=[vmem, vmem, pl.BlockSpec(memory_space=pltpu.SMEM)] + [anywhere] * 8,
+        out_specs=[vmem] * 8 + [anywhere] * 2 + [vmem],
+        scratch_shapes=[
+            pltpu.VMEM((*whole, LANES), low), pltpu.VMEM((8, *whole, HALF), low),
+            pltpu.VMEM((tiles, *whole, 3 * TILE), low),
+            pltpu.VMEM((tokens, width), full), pltpu.VMEM((tokens, width), full),
+            pltpu.VMEM((tokens, width), full), pltpu.VMEM((tokens, width), low),
+            pltpu.VMEM((2, 4, 2, tokens, LANES), low), pltpu.VMEM((2, 4, tokens, LANES), low),
+            pltpu.VMEM((width // 2, 2 * tokens), low), pltpu.VMEM((width // 2, 2 * tokens), low),
+            pltpu.VMEM((2, 3, tokens, TILE), low), pltpu.VMEM((tiles, 3, tokens, TILE), low),
+            pltpu.VMEM((2, 4, 2, 2, rows, 3 * TILE), low),
+            dma((count, 3)), dma((count, 10)), dma((count, 10)), dma((2,)), dma((2,)),
+            dma((2,)), dma((2,)), dma((tiles,)), dma((tiles,)), dma((8,)), dma((tiles,)),
+        ],
+        compiler_params=pltpu.CompilerParams(
+            collective_id=0, has_side_effects=True, vmem_limit_bytes=60 * 2**20
+        ),
+        name="gather_and_forward",
+    )(hidden, out_grad, lengths, gains, *weights)
+
+
+class Scatter:
+    def __init__(self, here, send, recv):
+        self.here, self.send, self.recv = here, send, recv
+        self.own, self.near = here.column(False, False), here.column(True, False)
+        self.far, self.both = here.column(False, True), here.column(True, True)
+
+    def copy(self, k, number, source, target, device):
+        return remote(source, target, self.send.at[k, number], self.recv.at[k, number], device)
+
+    def to_far(self, k, source, twos):
+        return [
+            self.copy(k, i, source.at[:, column[0], column[1]], twos.at[i], self.here.far())
+            for i, column in enumerate((self.both, self.far))
+        ]
+
+    def to_near(self, k, near, twos):
+        return self.copy(k, 2, near, twos.at[2], self.here.near())
+
+    def to_z(self, k, own, fours, step):
+        return self.copy(
+            k, 2 + step, own.at[(self.here.z + step) % 4], fours.at[step - 1], self.here.along_z(step)
+        )
+
+    def first(self, k, source, twos):
+        for copy in self.to_far(k, source, twos):
+            copy.start()
+
+    def add(self, target, other):
+        @pl.loop(0, 4)
+        def _(level):
+            target[level] = (
+                target[level].astype(jnp.float32) + other[level].astype(jnp.float32)
+            ).astype(jnp.bfloat16)
+
+    def second(self, k, source, own, near, twos):
+        both, far = self.to_far(k, source, twos)
+        both.wait()
+        self.add(near, twos.at[0])
+        self.to_near(k, near, twos).start()
+        far.wait()
+        self.add(own, twos.at[1])
+
+    def third(self, k, own, near, twos, fours):
+        self.to_near(k, near, twos).wait()
+        self.add(own, twos.at[2])
         for step in (1, 2, 3):
-            remote(shards[k], slot, send.at[k, step - 1], recv.at[k, step - 1], here.along_z(step)).start()
-        pltpu.make_async_copy(shards[k], slot, own_sem.at[k]).start()
-
-    def second(k):
+            self.to_z(k, own, fours, step).start()
+
+    def fourth(self, k, own, fours):
         for step in (1, 2, 3):
-            slot = wholes[k].at[(z + 4 - step) % 4, c, own[0], own[1]]
-            remote(shards[k], slot, send.at[k, step - 1], recv.at[k, step - 1], here.along_z(step)).wait()
-        pltpu.make_async_copy(shards[k], wholes[k].at[z, c, own[0], own[1]], own_sem.at[k]).wait()
-        copy(k, 3, block(k, c, own), here.near()).start()
-        copy(k, 4, block(k, c, own), here.far()).start()
-        copy(k, 6, block(k, c, own), here.peer()).start()
-
-    def third(k):
-        copy(k, 3, block(k, c, near), here.near()).wait()
-        copy(k, 5, block(k, c, near), here.far()).start()
-        copy(k, 7, block(k, c, near), here.peer()).start()
-
-    def fourth(k):
-        copy(k, 4, block(k, c, far), here.far()).wait()
-        copy(k, 8, block(k, c, far), here.peer()).start()
-        copy(k, 5, block(k, c, both), here.far()).wait()
-        copy(k, 9, block(k, c, both), here.peer()).start()
-
-    def fifth(k):
-        for number, column in ((6, own), (7, near), (8, far), (9, both)):
-            copy(k, number, block(k, 1 - c, column), here.peer()).wait()
-
-    for tick in range(count + 3):
-        for lag, step in enumerate((second, third, fourth, fifth)):
-            if 0 <= tick - lag < count:
-                step(tick - lag)
-
-
-def gathered(shards):
-    count = len(shards)
-    wholes = pl.pallas_call(
-        functools.partial(gather_kernel, count),
-        out_shape=[jax.ShapeDtypeStruct((4, 2, 2, 2, *s.shape), s.dtype) for s in shards],
-        in_specs=[pl.BlockSpec(memory_space=pl.ANY)] * count,
-        out_specs=[pl.BlockSpec(memory_space=pl.ANY)] * count,
-        scratch_shapes=[
-            pltpu.SemaphoreType.DMA((count,)),
-            pltpu.SemaphoreType.DMA((count, 10)),
-            pltpu.SemaphoreType.DMA((count, 10)),
-        ],
-        compiler_params=pltpu.CompilerParams(collective_id=0, has_side_effects=True),
-        name="gather_weights",
-    )(*shards)
-    return [w.reshape(-1, w.shape[-1]) for w in wholes]
-
-
-def scatter_kernel(plan, count, *refs):
-    grads, sums = refs[:count], refs[count : 2 * count]
-    refs = refs[2 * count :]
-    total = len(plan)
-    mine, paired, twos, fours = (refs[i * total : (i + 1) * total] for i in range(4))
-    own_sem, send, recv = refs[4 * total :]
+            self.to_z(k, own, fours, step).wait()
+        total = own[self.here.z].astype(jnp.float32)
+        for step in (1, 2, 3):
+            total = total + fours[step - 1].astype(jnp.float32)
+        return total
+
+
+def backward_kernel(
+    x_ref, gm_ref, no_ref, q_ref, k_ref, v_ref, at_ref, p_ref, norm_in, wa_in, gr_in,
+    gi_ref, oq_ref, ok_ref, ov_ref, oo_ref, og_ref, ou_ref, od_ref, on_ref,
+    wa, gat, gk_full, gv_full, edge, edge_in, outs, outs_peer, side, side_peer, no_t, at_t,
+    mine, mlp_twos, mlp_fours, mg, attn_twos, attn_fours, nb, nb_peer, nb_sum, norm_twos, norm_fours,
+    own_sem, send, recv, edge_send, edge_recv, side_send, side_recv, out_send, out_recv, pair_send,
+    pair_recv, wa_sem,
+):
     here = Place()
     z, c = here.z, here.c
-    own, near, far, both = (
-        here.column(False, False), here.column(True, False),
-        here.column(False, True), here.column(True, True),
-    )
-    greet(here.partners())
-
-    def own_copy(k):
-        number, first, width = plan[k]
-        return pltpu.make_async_copy(
-            grads[number].at[:, c, :, :, :, pl.ds(first, width)], mine[k], own_sem.at[k]
+    seq = lax.axis_index("seq")
+    tiles = gr_in.shape[0]
+    scale = 1.0 / math.sqrt(HEAD_DIM)
+    tokens = x_ref.shape[0] // 2
+    scatter = Scatter(here, send, recv)
+    own, near = scatter.own, scatter.near
+    attn = mg.shape[0]
+    norm_at = tiles + attn - 1
+    total = tiles + attn + 1
+
+    @pl.when(seq == SEQ_PIECES - 1)
+    def _():
+        edge_in[...] = jnp.zeros(edge_in.shape, jnp.bfloat16)
+
+    greet(here.partners() + [here.cross()])
+
+    def chunk(k):
+        if k < tiles:
+            return gr_in.at[k], mine.at[k, 0], mine.at[k, 1], mlp_twos.at[k], mlp_fours.at[k]
+        if k == norm_at:
+            source, twos, fours = nb_sum, norm_twos, norm_fours
+        else:
+            i = k - tiles - (1 if k > norm_at else 0)
+            source, twos, fours = mg.at[i], attn_twos.at[i], attn_fours.at[i]
+        return source, source.at[:, own[0], own[1]], source.at[:, near[0], near[1]], twos, fours
+
+    def fetches(k):
+        return [
+            pltpu.make_async_copy(gr_in.at[k, :, column[0], column[1]], mine.at[k, i], own_sem.at[k, i])
+            for i, column in enumerate((own, near))
+        ]
+
+    weights = [pltpu.make_async_copy(wa_in.at[i], wa.at[i], wa_sem.at[i]) for i in range(8)]
+
+    def store(k, value):
+        if k < tiles:
+            for i, ref in enumerate((og_ref, ou_ref, od_ref)):
+                ref[:, k * TILE : (k + 1) * TILE] = value[:, i * TILE : (i + 1) * TILE]
+        elif k == norm_at:
+            on_ref[...] = value
+        else:
+            i = k - tiles - (1 if k > norm_at else 0)
+            ref = (oo_ref, ov_ref, ok_ref, oq_ref)[i // 2]
+            ref[:, (i % 2) * HALF : (i % 2 + 1) * HALF] = value
+
+    def tick(t):
+        for lag in range(4):
+            k = t - lag
+            if not 0 <= k < total:
+                continue
+            source, own_block, near_block, twos, fours = chunk(k)
+            if lag == 0:
+                scatter.first(k, source, twos)
+                if k < tiles:
+                    for copy in fetches(k):
+                        copy.start()
+            elif lag == 1:
+                if k < tiles:
+                    for copy in fetches(k):
+                        copy.wait()
+                scatter.second(k, source, own_block, near_block, twos)
+            elif lag == 2:
+                scatter.third(k, own_block, near_block, twos, fours)
+            else:
+                store(k, scatter.fourth(k, own_block, fours))
+
+    def sides(number):
+        return remote(
+            side.at[number, :, 1 - c], side_peer.at[number],
+            side_send.at[number], side_recv.at[number], here.peer(),
         )
 
-    def to_peer(k):
-        number, first, width = plan[k]
+    def spread(number, value):
+        for i in range(8):
+            side[number, i // 2, i % 2] = value[:, i * LANES : (i + 1) * LANES]
+
+    def turned(number, target):
+        for level in range(4):
+            rows = slice(level * LANES, (level + 1) * LANES)
+            target[rows, 0 : 2 * tokens] = (
+                side[number, level, c].astype(jnp.float32).T.astype(jnp.bfloat16)
+            )
+            target[rows, 2 * tokens : 4 * tokens] = (
+                side_peer[number, level].astype(jnp.float32).T.astype(jnp.bfloat16)
+            )
+
+    def out_copy(number):
         return remote(
-            grads[number].at[:, 1 - c, :, :, :, pl.ds(first, width)], paired[k],
-            send.at[k, 0], recv.at[k, 0], here.peer(),
+            outs.at[number], outs_peer.at[number], out_send.at[number], out_recv.at[number], here.peer()
         )
 
-    def to_far(k, which):
-        column = both if which else far
-        return remote(
-            mine[k].at[:, column[0], column[1]], twos[k].at[which],
-            send.at[k, 1 + which], recv.at[k, 1 + which], here.far(),
+    def edge_copy():
+        return remote(edge, edge_in, edge_send.at[0], edge_recv.at[0], here.preceding())
+
+    def pair_copy():
+        return remote(nb.at[:, 1 - c], nb_peer, pair_send.at[0], pair_recv.at[0], here.peer())
+
+    def begin():
+        for copy in weights[6:] + weights[:6]:
+            copy.start()
+        outs[0] = gm_ref[...].astype(jnp.bfloat16)
+        out_copy(0).start()
+        spread(0, at_ref[...])
+        sides(0).start()
+        spread(1, no_ref[...])
+        sides(1).start()
+
+    def to_attended():
+        for i in (6, 7):
+            weights[i].wait()
+        grad = nt_dot(outs[0, :, 0:HALF], flat(wa[6])) + nt_dot(outs[0, :, HALF:], flat(wa[7]))
+        gat[...] = grad.astype(jnp.bfloat16)
+
+    def attend_back(row):
+        rows = slice(row * tokens, (row + 1) * tokens)
+        for head in range(HEADS):
+            cols = slice(head * HEAD_DIM, (head + 1) * HEAD_DIM)
+            grad = gat[rows, cols]
+            probs = p_ref[row * HEADS + head]
+            gv_full[row, :, cols] = tn_dot(probs.astype(jnp.bfloat16), grad)
+            grad_probs = nt_dot(grad, v_ref[row, :, cols])
+            inner = jnp.sum(grad_probs * probs, axis=-1, keepdims=True)
+            grad_scores = (probs * (grad_probs - inner)).astype(jnp.bfloat16)
+            outs[3, rows, cols] = (mm(grad_scores, k_ref[row, :, cols]) * scale).astype(jnp.bfloat16)
+            gk_full[row, :, cols] = tn_dot(grad_scores, q_ref[rows, cols]) * scale
+        before = slice(PAD - WINDOW, PAD)
+        edge[0, row] = gk_full[row, before, :].astype(jnp.bfloat16)
+        edge[1, row] = gv_full[row, before, :].astype(jnp.bfloat16)
+
+    def send_edge():
+        out_copy(3).start()
+
+        @pl.when(seq > 0)
+        def _():
+            edge_copy().start()
+
+    def close_edge():
+        @pl.when(seq < SEQ_PIECES - 1)
+        def _():
+            edge_copy().wait_recv()
+
+        @pl.when(seq > 0)
+        def _():
+            edge_copy().wait_send()
+
+        inside = tokens - WINDOW
+        for which, number, source in ((0, 2, gk_full), (1, 1, gv_full)):
+            for row in range(2):
+                first = row * tokens
+                outs[number, first : first + inside, :] = (
+                    source[row, PAD : PAD + inside, :].astype(jnp.bfloat16)
+                )
+                outs[number, first + inside : first + tokens, :] = (
+                    source[row, PAD + inside : PAD + tokens, :]
+                    + edge_in[which, row].astype(jnp.float32)
+                ).astype(jnp.bfloat16)
+        out_copy(1).start()
+        out_copy(2).start()
+
+    def to_input():
+        for i in range(6):
+            weights[i].wait()
+        grad_normed = jnp.zeros(gi_ref.shape, jnp.float32)
+        for number, i in ((2, 0), (1, 2), (3, 4)):
+            grad_normed = grad_normed + (
+                nt_dot(outs[number, :, 0:HALF], flat(wa[i])) + nt_dot(outs[number, :, HALF:], flat(wa[i + 1]))
+            )
+        x = x_ref[...].astype(jnp.float32)
+        factor = lax.rsqrt(jnp.mean(x * x, axis=-1, keepdims=True) + 1e-05)
+        through = grad_normed * norm_in[0:1, :]
+        shift = jnp.mean(through * x, axis=-1, keepdims=True) * factor * factor * factor
+        gi_ref[...] = gm_ref[...] + factor * through - x * shift
+        one = jnp.sum(grad_normed * x * factor, axis=0, keepdims=True)
+        width = one.shape[1]
+        stacked = jnp.concatenate(
+            [
+                jnp.broadcast_to(one, (LANES // 2, width)),
+                jnp.broadcast_to(norm_in[8:9, :], (LANES // 2, width)),
+            ],
+            axis=0,
         )
-
-    def to_near(k):
-        return remote(
-            mine[k].at[:, near[0], near[1]], twos[k].at[2],
-            send.at[k, 3], recv.at[k, 3], here.near(),
-        )
-
-    def to_z(k, step):
-        return remote(
-            mine[k].at[(z + step) % 4, own[0], own[1]], fours[k].at[step - 1],
-            send.at[k, 3 + step], recv.at[k, 3 + step], here.along_z(step),
-        )
-
-    def add(left, right):
-        return (left.astype(jnp.float32) + right.astype(jnp.float32)).astype(jnp.bfloat16)
-
-    for k in range(total):
-        to_peer(k).start()
-        own_copy(k).start()
-
-    def first(k):
-        own_copy(k).wait()
-        to_peer(k).wait()
-
-        @pl.loop(0, 4)
-        def _(level):
-            mine[k][level] = add(mine[k][level], paired[k][level])
-
-        to_far(k, 1).start()
-        to_far(k, 0).start()
-
-    def second(k):
-        to_far(k, 1).wait()
-
-        @pl.loop(0, 4)
-        def _(level):
-            view = mine[k].at[level, near[0], near[1]]
-            view[...] = add(view[...], twos[k][1, level])
-
-        to_near(k).start()
-        to_far(k, 0).wait()
-
-        @pl.loop(0, 4)
-        def _(level):
-            view = mine[k].at[level, own[0], own[1]]
-            view[...] = add(view[...], twos[k][0, level])
-
-    def third(k):
-        to_near(k).wait()
-
-        @pl.loop(0, 4)
-        def _(level):
-            view = mine[k].at[level, own[0], own[1]]
-            view[...] = add(view[...], twos[k][2, level])
-
-        for step in (1, 2, 3):
-            to_z(k, step).start()
-
-    def fourth(k):
-        number, begin, width = plan[k]
-        for step in (1, 2, 3):
-            to_z(k, step).wait()
-        value = mine[k][z, own[0], own[1]].astype(jnp.float32)
-        for step in (1, 2, 3):
-            value = value + fours[k][step - 1].astype(jnp.float32)
-        sums[number][:, pl.ds(begin, width)] = value
-
-    for tick in range(total + 3):
-        for lag, step in enumerate((first, second, third, fourth)):
-            if 0 <= tick - lag < total:
-                step(tick - lag)
-
-
-def scattered(totals):
-    count = len(totals)
-    block = totals[0].shape[0] // 32
-    plan = []
-    for number, t in enumerate(totals):
-        width = t.shape[1]
-        parts = 2 if width > 1024 else 1
-        for part in range(parts):
-            plan.append((number, part * (width // parts), width // parts))
-    halves = [(4, 2, 2, block, width) for _, _, width in plan]
-    thirds = [(3, 4, block, width) for _, _, width in plan]
-    ends = [(3, block, width) for _, _, width in plan]
+        nb[...] = stacked.T.astype(jnp.bfloat16).reshape(nb.shape)
+        pair_copy().start()
+
+    def close_norm():
+        pair_copy().wait()
+        nb_sum[...] = (
+            nb[:, c].astype(jnp.float32) + nb_peer[...].astype(jnp.float32)
+        ).astype(jnp.bfloat16)
+
+    def weight_grads(number):
+        out_copy(number).wait()
+        turn = at_t if number == 0 else no_t
+        n = 2 * tokens
+        for half in range(2):
+            cols = slice(half * HALF, (half + 1) * HALF)
+            grad = mm(turn[:, 0:n], outs[number, :, cols]) + mm(turn[:, n : 2 * n], outs_peer[number, :, cols])
+            mg[2 * number + half] = grad.astype(jnp.bfloat16).reshape(mg.shape[1:])
+
+    def turn_sides():
+        sides(0).wait()
+        turned(0, at_t)
+        sides(1).wait()
+        turned(1, no_t)
+
+    work = {
+        0: [begin], 1: [to_attended], 2: [lambda: attend_back(0)], 3: [lambda: attend_back(1), send_edge],
+        4: [turn_sides], 5: [close_edge], 6: [to_input], 7: [lambda: weight_grads(0)],
+        8: [lambda: weight_grads(1), close_norm], 9: [lambda: weight_grads(2)], 10: [lambda: weight_grads(3)],
+    }
+    for t in range(total + 3):
+        tick(t)
+        for step in work.get(t, ()):
+            step()
+
+
+def backward(hidden, saved):
+    grad_middle, normed, queries, keys, values, attended, probs, weights, grads, norm = saved
+    tokens, width = hidden.shape
+    tiles, rows = grads.shape[0], grads.shape[4]
+    low, full = jnp.bfloat16, jnp.float32
+    dma = pltpu.SemaphoreType.DMA
+    vmem, anywhere = pl.BlockSpec(memory_space=pltpu.VMEM), pl.BlockSpec(memory_space=pl.ANY)
+    shape = jax.ShapeDtypeStruct
+    attn = 8
+    total = tiles + attn + 1
+    wide, grid = 3 * TILE, (4, 2, 2, rows)
+    scratch = [
+        ((8, 4, 2, 2, 2, rows, HALF), low), ((tokens, width), low),
+        (keys.shape, full), (keys.shape, full),
+        ((2, 2, WINDOW, width), low), ((2, 2, WINDOW, width), low),
+        ((4, tokens, width), low), ((4, tokens, width), low),
+        ((2, 4, 2, tokens, LANES), low), ((2, 4, tokens, LANES), low),
+        ((width // 2, 2 * tokens), low), ((width // 2, 2 * tokens), low),
+        ((tiles, 2, 4, rows, wide), low), ((tiles, 3, 4, rows, wide), low), ((tiles, 3, rows, wide), low),
+        ((attn, *grid, HALF), low), ((attn, 3, 4, rows, HALF), low), ((attn, 3, rows, HALF), low),
+        ((4, 2, 2, 2, rows, LANES), low), ((*grid, LANES), low), ((*grid, LANES), low),
+        ((3, 4, rows, LANES), low), ((3, rows, LANES), low),
+    ]
     return pl.pallas_call(
-        functools.partial(scatter_kernel, plan, count),
-        out_shape=[jax.ShapeDtypeStruct((block, t.shape[1]), jnp.float32) for t in totals],
-        in_specs=[pl.BlockSpec(memory_space=pl.ANY)] * count,
-        out_specs=[pl.BlockSpec(memory_space=pltpu.VMEM)] * count,
-        scratch_shapes=[
-            *[pltpu.VMEM(s, jnp.bfloat16) for shapes in (halves, halves, thirds, ends) for s in shapes],
-            pltpu.SemaphoreType.DMA((len(plan),)),
-            pltpu.SemaphoreType.DMA((len(plan), 7)),
-            pltpu.SemaphoreType.DMA((len(plan), 7)),
+        backward_kernel,
+        out_shape=[shape((tokens, width), full)]
+        + [shape((rows, width), full)] * 4 + [shape((rows, tiles * TILE), full)] * 3
+        + [shape((rows, LANES), full)],
+        in_specs=[vmem] * 9 + [anywhere] * 2,
+        out_specs=[vmem] * 9,
+        scratch_shapes=[pltpu.VMEM(*s) for s in scratch]
+        + [
+            dma((tiles, 2)), dma((total, 6)), dma((total, 6)), dma((1,)), dma((1,)), dma((2,)), dma((2,)),
+            dma((4,)), dma((4,)), dma((1,)), dma((1,)), dma((8,)),
         ],
         compiler_params=pltpu.CompilerParams(
-            collective_id=1, has_side_effects=True, vmem_limit_bytes=60 * 2**20
+            collective_id=1, has_side_effects=True, vmem_limit_bytes=62 * 2**20
         ),
-        name="scatter_grads",
-    )(*[t.astype(jnp.bfloat16).reshape(4, 2, 2, 2, block, t.shape[1]) for t in totals])
+        name="scatter_and_backward",
+    )(hidden, grad_middle, normed, queries, keys, values, attended, probs, norm, weights, grads)
+
+
+def fused(hidden_in, lengths, out_grad, gain_shards, weight_shards):
+    flat_in = hidden_in.reshape(-1, hidden_in.shape[-1])
+    flat_grad = out_grad.reshape(flat_in.shape)
+    gains = jnp.concatenate(
+        [jnp.broadcast_to(g[:, None], (g.shape[0], LANES // 2)) for g in gain_shards], axis=1
+    )
+    block_out, *saved = forward(flat_in, flat_grad, lengths, gains, weight_shards)
+    grad_in, query, key, value, wout, gate, up, down, norms = backward(flat_in, saved)
+    return (
+        block_out.reshape(hidden_in.shape), grad_in.reshape(hidden_in.shape),
+        norms[:, 0], query, key, value, wout, norms[:, LANES // 2], gate, up, down,
+    )
 
 
 def layer(hidden_in, lengths, out_grad, gains, weights):
@@ -451,28 +970,14 @@
     norm2_gain, w_gate, w_up, w_down, out_grad,
 ):
     gain_shards = (norm1_gain, norm2_gain)
+    if (lax.axis_size("seq"), lax.axis_size("rows")) == (SEQ_PIECES, ROW_GROUPS):
+        weight_shards = (w_query, w_key, w_value, w_out, w_gate, w_up, w_down)
+        return fused(hidden_in, lengths, out_grad, gain_shards, weight_shards)
     weight_shards = (w_query, w_key, w_value, w_out, w_gate, w_up, w_down)
-    kernels = (lax.axis_size("seq"), lax.axis_size("rows")) == (8, 4)
-    if kernels:
-        both = jnp.concatenate(
-            [jnp.broadcast_to(g[:, None], (g.shape[0], LANES)) for g in gain_shards], axis=1
-        )
-        both, *weights = gathered([both, *weight_shards])
-        gains = [both[:, 0], both[:, LANES]]
-    else:
-        gains = gathered_by_xla(gain_shards)
-        weights = gathered_by_xla(weight_shards)
-    gains = [g.astype(jnp.float32) for g in gains]
+    gains = [g.astype(jnp.float32) for g in gathered_by_xla(gain_shards)]
+    weights = gathered_by_xla(weight_shards)
     block_out, grad_in, norms, grads = layer(hidden_in, lengths, out_grad, gains, weights)
-    if kernels:
-        both = jnp.concatenate(
-            [jnp.broadcast_to(g[:, None], (g.shape[0], LANES)) for g in norms], axis=1
-        )
-        *grads, both = scattered([*grads, both])
-        norms = [both[:, 0], both[:, LANES]]
-    else:
-        norms = scattered_by_xla(norms)
-        grads = scattered_by_xla(grads)
+    norms, grads = scattered_by_xla(norms), scattered_by_xla(grads)
     return (
         block_out, grad_in, norms[0], grads[0], grads[1], grads[2], grads[3],
         norms[1], grads[4], grads[5], grads[6],

time: 365 us -> 280 us (0.77)
  matrix products: 55.2 us -> 0 us
  Pallas kernels: 274 us -> 261 us
  other arithmetic: 10.6 us -> 0.68 us
  starting transfers between devices: 4.6 us -> 0 us
    dot_general x26 -> x0, matrix products: 54.5 us -> none  [the longest x7 22.9 us: weight_grad(): jnp.einsum('rtd,rtf->df', left, grad, preferred_element_type=jnp.float32)]
    pallas_call x2, Pallas kernels: 274 us -> 261 us  [the longest x1 132 us: forward(): pl.pallas_call(forward_kernel, out_shape=[shape((tokens, width), low), sh...]
    ppermute x2 -> x0, starting transfers between devices: 4.6 us -> none  [passed_along(): return lax.ppermute(block, axis, route)]
    unnamed x89 -> x11, local copies, waits for them, and re-layouts: 11.4 us -> 14.6 us
  transfers between devices with their start and end apart: 2 -> 0, of which waited for: 0 -> 0; matrix products, arithmetic and copies ran while one was open for 4% -> 0% of each run, Pallas kernels for 0% -> 0%
where the time goes in v2:
time: 280 us
  Pallas kernels  261 us (93%)
  local copies, waits for them, and re-layouts  17.5 us (6%)
    pallas_call x1, Pallas kernels, forward(): pl.pallas_call(forward_kernel, out_shape=[shape((tokens, width), low), sh...  132 us
    pallas_call x1, Pallas kernels, backward(): pl.pallas_call(backward_kernel, out_shape=[shape((tokens, width), full)]...  129 us
    unnamed x11, local copies, waits for them, and re-layouts  14.6 us

profile of v2, /device:TPU:0, one launch (start us, length us, event | category | flops | bytes accessed | tf_op | source)
XLA Modules:
  0.0 280.0 jit_solution(5523512330742344938)
XLA Ops:
  0.6 0.7 broadcast_in_dim.4
  1.4 0.7 broadcast_in_dim.5
  2.1 0.7 pad_maximum_fusion.gains_in
  2.8 132.4 %gather_and_forward.1 = (bf16[256,1024]{1,0:T(8,128)(2,1)}, f32[256,1024]{1,0:T(8,128)}, bf16[256,1024]{1,0:T(8,128)(2,1)}, bf16[256,1024]{1,0:T(8,128)(2,1)}, b...) custom-call(bf16[256,1024]{1,0:T(8,128)(2,1)} %bitcast.4, ...), custom_call_target="tpu_custom_call" | custom-call | tf_op jit(solution)/shard_map/gather_and_forward/pallas_call | solution.py:507
  135.2 0.0 copy-start
  135.2 128.7 %scatter_and_backward.1 = (f32[256,1024]{1,0:T(8,128)}, f32[32,1024]{1,0:T(8,128)}, f32[32,1024]{1,0:T(8,128)}, f32[32,1024]{1,0:T(8,128)}, f32[32,1024]{1,0:T(8...) custom-call(bf16[256,1024]{1,0:T(8,128)(2,1)} %bitcast.5, ...), custom_call_target="tpu_custom_call" | custom-call | tf_op jit(solution)/shard_map/scatter_and_backward/pallas_call | solution.py:843
  263.9 1.5 slice_reduce_fusion
  265.4 0.0 copy-done
  265.4 0.8 copy.32
  266.2 2.3 copy.33
  268.5 1.6 copy.34
  270.0 1.6 copy.35
  271.6 1.6 copy.36
  273.2 1.6 copy.37
  274.7 1.7 copy.38
  276.5 1.7 copy.39
  278.2 1.7 copy.40
Async XLA Ops:
  135.2 130.2 %copy-start = (bf16[256,1024]{1,0:T(8,128)(2,1)S(1)}, bf16[256,1024]{1,0:T(8,128)(2,1)}, u32[]{:S(2)}) copy-start(bf16[256,1024]{1,0:T(8,128)(2,1)} %get-tuple-element.31) | copy-start | bytes 1572868

commit v3 on v1

v3 whole, which is shorter than its diff:
```python
import functools
import math

import jax
import jax.numpy as jnp
from jax import lax
from jax.experimental import pallas as pl
from jax.experimental.pallas import tpu as pltpu
from jax.sharding import PartitionSpec as P

HEADS = 8
HEAD_DIM = 128
WINDOW = 64
LANES = 128
MESH = pl.DeviceIdType.MESH


def passed_along(block, axis, distance):
    devices = range(lax.axis_size(axis))
    route = [(i - distance, i) for i in devices if i - distance in devices]
    return lax.ppermute(block, axis, route)


def rms_scale(values, gain):
    factor = lax.rsqrt(jnp.mean(values * values, axis=-1, keepdims=True) + 1e-05)
    return values * factor * gain


def swiglu(gates, ups):
    return jax.nn.silu(gates) * ups


def project(left, weight):
    return jnp.dot(left, weight, preferred_element_type=jnp.float32)


def project_back(grad, weight):
    return lax.dot_general(
        grad, weight, (((2,), (1,)), ((), ())), preferred_element_type=jnp.float32
    )


def weight_grad(left, grad):
    return jnp.einsum("rtd,rtf->df", left, grad, preferred_element_type=jnp.float32)


def split_heads(values):
    return values.reshape(values.shape[0], values.shape[1], HEADS, HEAD_DIM)


def merge_heads(values):
    return values.reshape(values.shape[0], values.shape[1], HEADS * HEAD_DIM)


def window_mask(lengths, seq_index, tokens):
    docs = lengths.shape[1]
    upto = jnp.arange(docs)[:, None] >= jnp.arange(docs)[None, :]
    ends = jnp.sum(jnp.where(upto[None], lengths[:, None, :], 0), axis=2)
    query_pos = seq_index * tokens + jnp.arange(tokens, dtype=jnp.int32)
    key_pos = seq_index * tokens - WINDOW + jnp.arange(tokens + WINDOW, dtype=jnp.int32)
    starts = jnp.max(
        jnp.where(
            ends[:, None, :] <= query_pos[None, :, None],
            ends[:, None, :],
            jnp.zeros_like(ends[:, None, :]),
        ),
        axis=2,
    )
    allowed = (
        (key_pos[None, None, :] >= starts[:, :, None])
        & (key_pos[None, None, :] <= query_pos[None, :, None])
        & (query_pos[None, :, None] - key_pos[None, None, :] < WINDOW)
    )
    return allowed[:, None]


def scores_of(queries, keys_all, allowed):
    score_scale = 1.0 / math.sqrt(HEAD_DIM)
    scores = (
        jnp.einsum(
            "rqhd,rkhd->rhqk",
            split_heads(queries),
            split_heads(keys_all),
            preferred_element_type=jnp.float32,
        )
        * score_scale
    )
    return jnp.where(allowed, scores, -1e30)


def gathered_by_xla(shards):
    return [lax.all_gather(s, ("seq", "rows"), axis=0, tiled=True) for s in shards]


def scattered_by_xla(totals):
    return [
        lax.psum_scatter(t.astype(jnp.float32), ("seq", "rows"), scatter_dimension=0, tiled=True)
        for t in totals
    ]


SEQ_PIECES = 8
ROW_GROUPS = 4
PART = 128
HALF = 512
PAD = 128
AHEAD = (11, 3, 2, 1)
FIRST_TILES = 7
SUM_LAGS = (0, 2, 4)


class Place:
    def __init__(self):
        seq, rows = lax.axis_index("seq"), lax.axis_index("rows")
        self.z, self.c = seq // 2, seq % 2
        self.k, self.h = self.z // 2, self.z % 2
        self.y, self.x = rows // 2, rows % 2
        self.turn_y, self.turn_x = 1 - 2 * self.y, 1 - 2 * self.x

    def column(self, near, far):
        y, x, c = self.y, self.x, self.c
        if near:
            y, x = y + c * self.turn_y, x + (1 - c) * self.turn_x
        if far:
            y, x = y + (1 - c) * self.turn_y, x + c * self.turn_x
        return y, x

    def device(self, z, c, column):
        return (2 * z + c, 2 * column[0] + column[1])

    def near(self):
        return self.device(self.z, self.c, self.column(True, False))

    def far(self):
        return self.device(self.z, self.c, self.column(False, True))

    def peer(self):
        return self.device(self.z, 1 - self.c, (self.y, self.x))

    def mate(self):
        return self.device(2 * self.k + 1 - self.h, self.c, (self.y, self.x))

    def across(self):
        return self.device(2 * (1 - self.k) + self.h, self.c, (self.y, self.x))

    def cross(self):
        return self.device(2 * (1 - self.k) + self.h, 1 - self.c, (self.y, self.x))

    def along_z(self, step):
        return self.device((self.z + step) % 4, self.c, (self.y, self.x))

    def partners(self):
        return [self.near(), self.far(), self.peer(), self.cross()] + [self.along_z(i) for i in (1, 2, 3)]


def greet(partners):
    barrier = pltpu.get_barrier_semaphore()
    for partner in partners:
        pl.semaphore_signal(barrier, inc=1, device_id=partner, device_id_type=MESH)
    pl.semaphore_wait(barrier, len(partners))


def remote(source, target, send, recv, device):
    return pltpu.make_async_remote_copy(
        src_ref=source, dst_ref=target, send_sem=send, recv_sem=recv,
        device_id=device, device_id_type=MESH,
    )


def nt_dot(left, right):
    return lax.dot_general(left, right, (((1,), (1,)), ((), ())), preferred_element_type=jnp.float32)


def tn_dot(left, right):
    return lax.dot_general(left, right, (((0,), (0,)), ((), ())), preferred_element_type=jnp.float32)


def mm(left, right):
    return jnp.dot(left, right, preferred_element_type=jnp.float32)


def flat(value):
    return value.reshape(-1, value.shape[-1])


def low(value):
    return value.astype(jnp.bfloat16)


def wide(value):
    return value.astype(jnp.float32)


def lanes_at(first, width):
    return pl.ds(pl.multiple_of(first, PART), width)


class Gather:
    def __init__(self, here, own_sem, send, recv):
        self.here, self.own_sem, self.send, self.recv = here, own_sem, send, recv
        self.own, self.near = here.column(False, False), here.column(True, False)
        self.far, self.both = here.column(False, True), here.column(True, True)

    def slot(self, whole):
        return whole.at[self.here.z, self.here.c, self.own[0], self.own[1]]

    def block(self, whole, core, column):
        return whole.at[:, core, column[0], column[1]]

    def copy(self, n, number, source, target, device):
        return remote(source, target, self.send.at[n, number], self.recv.at[n, number], device)

    def wait(self, n, number, view, device):
        self.copy(n, number, view, view, device).wait()

    def begin(self, n, parts, whole, pack):
        slot = self.slot(whole)
        for kept, given, first, width in parts:
            pltpu.make_async_copy(kept, slot.at[:, pl.ds(first, width)], self.own_sem.at[n, 0]).start()
            if pack is not None:
                pltpu.make_async_copy(given, pack.at[:, pl.ds(first, width)], self.own_sem.at[n, 1]).start()

    def first(self, n, whole, pack):
        slot = self.slot(whole)
        pltpu.make_async_copy(slot, slot, self.own_sem.at[n, 0]).wait()
        if pack is not None:
            pltpu.make_async_copy(pack, pack, self.own_sem.at[n, 1]).wait()
        for step in (1, 2, 3):
            source = slot if pack is None or step == 2 else pack
            self.copy(n, 0, source, slot, self.here.along_z(step)).start()

    def second(self, n, whole):
        here = self.here
        self.wait(n, 0, whole.at[pl.ds(0, 3), here.c, self.own[0], self.own[1]], here.along_z(1))
        block = self.block(whole, here.c, self.own)
        self.copy(n, 1, block, block, here.near()).start()
        self.copy(n, 2, block, block, here.far()).start()
        self.copy(n, 3, block, block, here.peer()).start()

    def third(self, n, whole):
        here = self.here
        block = self.block(whole, here.c, self.near)
        self.wait(n, 1, block, here.near())
        self.copy(n, 2, block, block, here.far()).start()
        self.copy(n, 3, block, block, here.peer()).start()

    def fourth(self, n, whole):
        here = self.here
        self.wait(n, 2, whole.at[:, here.c, 0], here.far())
        for column in (self.far, self.both):
            block = self.block(whole, here.c, column)
            self.copy(n, 3, block, block, here.peer()).start()

    def fifth(self, n, whole):
        self.wait(n, 3, whole.at[:, 1 - self.here.c], self.here.peer())


class Scatter:
    def __init__(self, here, send, recv):
        self.here, self.send, self.recv = here, send, recv
        self.own, self.near = here.column(False, False), here.column(True, False)
        self.far, self.both = here.column(False, True), here.column(True, True)

    def copy(self, n, number, source, target, device):
        return remote(source, target, self.send.at[n, number], self.recv.at[n, number], device)

    def view(self, source, column):
        if len(source.shape) == 5:
            return source.at[:, column[0], column[1]]
        return source.at[:, 2 * column[0] + column[1]]

    def to_far(self, n, source, twos):
        return [
            self.copy(n, i, self.view(source, column), twos.at[i], self.here.far())
            for i, column in enumerate((self.both, self.far))
        ]

    def to_near(self, n, source, twos):
        return self.copy(n, 2, self.view(source, self.near), twos.at[2], self.here.near())

    def first(self, n, source, twos):
        for copy in self.to_far(n, source, twos):
            copy.start()

    def add(self, target, other):
        @pl.loop(0, 4)
        def _(level):
            target[level] = low(wide(target[level]) + wide(other[level]))

    def second(self, n, source, twos):
        both, far = self.to_far(n, source, twos)
        both.wait()
        self.add(self.view(source, self.near), twos.at[0])
        self.to_near(n, source, twos).start()
        far.wait()
        self.add(self.view(source, self.own), twos.at[1])

    def third(self, n, source, twos, ends):
        self.to_near(n, source, twos).wait()
        own = self.view(source, self.own)
        self.add(own, twos.at[2])
        for step in (1, 2, 3):
            block = own.at[(self.here.z + step) % 4]
            self.copy(n, 3, block, ends.at[step - 1], self.here.along_z(step)).start()

    def fourth(self, n, source, ends):
        self.copy(n, 3, ends, ends, self.here.along_z(1)).wait()
        own = self.view(source, self.own)
        return wide(own[self.here.z]), [wide(ends[i]) for i in range(3)]


def layer_kernel(
    x_in, og_in, lengths_ref, gains_in, wq_in, wk_in, wv_in, wo_in, wg_in, wu_in, wd_in,
    out_ref, gi_ref, oq_ref, ok_ref, ov_ref, oo_ref, og_out, ou_out, od_out, on_ref,
    wn, wa, wo, wm, pack_a, pack_m, xm, og8, nt8, no8, at8, atb, og_peer, nt_peer, no_peer, at_peer,
    og_t, nt_t, q_ref, k_ref, v_ref, p_ref, mid, acc, gn, gain, tri, tri_peer,
    swap, swap_in, gat, edge, edge_in, outs, outs_peer, gb, gb_peer, mga,
    nb_peer, nb_sum, mlp_twos, mlp_ends, mga_twos, mga_ends, mgo_twos, mgo_ends, nb_twos, nb_ends,
    own_sem, g_send, g_recv, s_send, s_recv, halo_send, halo_recv, edge_send, edge_recv,
    side_send, side_recv, tri_send, tri_recv, swap_send, swap_recv, out_send, out_recv, host_sem,
):
    nb, ga_send, no_t = wn, swap.at[0, :, 0:HALF], nt_t
    here = Place()
    z, c, k, h = here.z, here.c, here.k, here.h
    tiles = wm.shape[0]
    span = tiles * PART
    scale = 1.0 / math.sqrt(HEAD_DIM)
    tokens = x_in.shape[0]
    piece = tokens // 2
    rows = wn.shape[4]
    gather = Gather(here, own_sem, g_send, g_recv)
    scatter = Scatter(here, s_send, s_recv)
    early = 6
    total = early + tiles

    def whole_of(n):
        if n == 0:
            return wn
        return wa.at[n - 1] if n < 4 else wo.at[n - 4]

    def pack_of(n):
        return pack_a.at[n - 1] if 1 <= n < 4 else None

    def parts_of(n):
        if n == 0:
            return [(gains_in, None, 0, LANES)]
        if n < 4:
            source = (wk_in, wv_in, wq_in)[n - 1]
            return [(source.at[:, lanes_at(h * HALF, HALF)], source.at[:, lanes_at((1 - h) * HALF, HALF)], 0, HALF)]
        return [(wo_in.at[:, pl.ds((n - 4) * HALF, HALF)], None, 0, HALF)]

    def mlp_parts(f):
        return [
            (
                w.at[:, lanes_at(h * span + f * PART, PART)],
                w.at[:, lanes_at((1 - h) * span + f * PART, PART)],
                i * PART, PART,
            )
            for i, w in enumerate((wg_in, wu_in, wd_in))
        ]

    def step(stage, n):
        late = n >= early
        whole = wm.at[n - early] if late else whole_of(n)
        if stage == 0:
            gather.first(n, whole, pack_m.at[n - early] if late else pack_of(n))
        else:
            (gather.second, gather.third, gather.fourth, gather.fifth)[stage - 1](n, whole)

    def steps(stage, *chunks_of):
        for n in chunks_of:
            step(stage, n)

    def tile_steps(f):
        for stage, ahead in enumerate(AHEAD):
            tile = f + ahead

            @pl.when(tile < tiles)
            def _(stage=stage, tile=tile):
                if stage == 0:
                    gather.first(early + tile, wm.at[tile], pack_m.at[tile])
                else:
                    (gather.second, gather.third, gather.fourth)[stage - 1](early + tile, wm.at[tile])

    def halo(which, kind):
        ref = (k_ref, v_ref)[which]
        tail, head = pl.ds((PAD + piece - WINDOW) // rows, WINDOW // rows), pl.ds((PAD - WINDOW) // rows, WINDOW // rows)
        if kind == 0:
            source, target, device = ref.at[:, tail], ref.at[:, head], here.peer()
        elif kind == 1:
            source, target, device = ref.at[pl.ds(0, 2), tail], ref.at[pl.ds(2, 2), head], here.peer()
        else:
            source, target, device = ref.at[pl.ds(2, 2), tail], ref.at[pl.ds(0, 2), head], here.cross()
        return remote(source, target, halo_send.at[which, kind // 2], halo_recv.at[which, kind // 2], device)

    def edge_copy(kind):
        if kind == 0:
            source, target, device = edge, edge_in, here.peer()
        elif kind == 1:
            source, target, device = edge.at[:, 1], edge_in.at[:, 0], here.peer()
        else:
            source, target, device = edge.at[:, 0], edge_in.at[:, 1], here.cross()
        return remote(source, target, edge_send.at[kind // 2], edge_recv.at[kind // 2], device)

    def x_copy():
        return remote(x_in, xm, swap_send.at[0], swap_recv.at[0], here.mate())

    def og_copy(slot):
        view = og8.at[:, :, slot]
        return remote(view, view, swap_send.at[1], swap_recv.at[1], here.mate())

    def nt_copy(slot):
        view = nt8.at[:, :, slot]
        return remote(view, view, swap_send.at[2], swap_recv.at[2], here.mate())

    def at_copy():
        return remote(atb.at[1 - h], at8.at[pl.ds(2 * h, 2)], swap_send.at[3], swap_recv.at[3], here.mate())

    def ga_copy():
        return remote(ga_send, gat.at[h], swap_send.at[4], swap_recv.at[4], here.mate())

    def swap_copy(number):
        return remote(
            swap.at[number % 2], swap_in.at[number], swap_send.at[5 + number], swap_recv.at[5 + number], here.mate()
        )

    def out_store():
        return pltpu.make_async_copy(swap.at[1], out_ref, host_sem.at[8])

    def x_again(i):
        return pltpu.make_async_copy(x_in.at[:, pl.ds(i * HALF, HALF)], gat.at[i], host_sem.at[9 + i])

    def side_copy(number, source, target):
        return remote(source, target, side_send.at[number], side_recv.at[number], here.peer())

    def og_side(number, slot):
        return side_copy(number, og8.at[:, 1 - c, slot], og_peer.at[:, slot])

    def nt_side(number, slot):
        return side_copy(number, nt8.at[:, 1 - c, slot], nt_peer.at[:, slot])

    def no_side():
        return side_copy(4, no8.at[:, 1 - c], no_peer)

    def at_side():
        return side_copy(5, at8.at[:, 1 - c], at_peer)

    def gb_side():
        return side_copy(6, gb, gb_peer)

    def pair_side():
        return side_copy(7, nb.at[:, 1 - c], nb_peer)

    def out_copy(m):
        return remote(outs.at[m], outs_peer.at[m], out_send.at[m], out_recv.at[m], here.peer())

    def tri_copy(f, slot):
        return remote(
            tri.at[f, :, slot], tri_peer.at[f, :, slot], tri_send.at[f], tri_recv.at[f], here.peer()
        )

    def spread(value, target, slot):
        for i in range(8):
            target[i // 2, i % 2, slot] = value[:, i * PART : (i + 1) * PART]

    def joined(source, slot):
        return jnp.concatenate([source[i // 2, i % 2, slot] for i in range(8)], axis=1)

    def turned(own_part, peer_part, target):
        for level in range(4):
            rows = slice(level * PART, (level + 1) * PART)
            left, right = own_part(level), peer_part(level)
            target[rows, 0 : left.shape[0]] = low(wide(left).T)
            target[rows, left.shape[0] : 2 * left.shape[0]] = low(wide(right).T)

    og_fetches = [
        pltpu.make_async_copy(og_in.at[:, pl.ds(i * PART, PART)], og8.at[i // 2, i % 2, h], host_sem.at[i])
        for i in range(8)
    ]
    x_fetches = [
        pltpu.make_async_copy(x_in.at[:, pl.ds(i * HALF, HALF)], outs.at[0, i], host_sem.at[9 + i]) for i in range(2)
    ]
    for n in range(early):
        gather.begin(n, parts_of(n), whole_of(n), pack_of(n))
    for copy in og_fetches + x_fetches:
        copy.start()

    @pl.loop(0, tiles)
    def _(f):
        gather.begin(early + f, mlp_parts(f), wm.at[f], pack_m.at[f])

    skipped, begun = (PAD - WINDOW) // rows, PAD // rows
    nothing = jnp.zeros((4, skipped, rows, HALF), jnp.bfloat16)
    for ref in (k_ref, v_ref):
        ref[:, 0:skipped] = nothing

    @pl.when((c == 0) & (k == 0))
    def _():
        for ref in (k_ref, v_ref):
            ref[0:2, skipped:begun] = nothing[0:2]

    @pl.when((c == 1) & (k == 1))
    def _():
        edge_in[:, 1] = jnp.zeros((2, 2, WINDOW, HALF), jnp.bfloat16)

    greet(here.partners())

    steps(0, 0, 1, 2, 3)
    x_copy().start()
    steps(0, 4, 5, 6, 7)
    steps(1, 0, 1, 2, 3)
    steps(2, 0, 1, 2, 3)
    steps(1, 4, 5)
    steps(3, 0, 1, 2, 3)
    for copy in og_fetches:
        copy.wait()
    og_side(0, h).start()
    steps(4, 0)

    gain_rows = wide(flat(wn[...])).T
    gain[0:8, :] = jnp.broadcast_to(gain_rows[0:1, :], (8, gain_rows.shape[1]))
    gain[8:16, :] = jnp.broadcast_to(gain_rows[64:65, :], (8, gain_rows.shape[1]))

    def normed_of(value, row):
        factor = lax.rsqrt(jnp.mean(value * value, axis=-1, keepdims=True) + 1e-05)
        return low(value * factor * gain[row : row + 1, :])

    for copy in x_fetches:
        copy.wait()
    spread(normed_of(wide(jnp.concatenate([outs[0, 0], outs[0, 1]], axis=1)), 0), no8, h)
    x_copy().wait()
    spread(normed_of(wide(xm[...]), 0), no8, 1 - h)
    no_side().start()

    def projected(n, slot):
        return low(mm(joined(no8, slot), flat(wa[n])))

    steps(1, 6)
    for n, ref in ((0, k_ref), (1, v_ref)):
        steps(4, 1 + n)
        for slot in range(2):
            ref[2 * slot : 2 * slot + 2, begun:] = projected(n, slot).reshape(2, piece // rows, rows, HALF)

        @pl.when(c == 0)
        def _(n=n):
            halo(n, 0).start()

        @pl.when(c == 1)
        def _(n=n):
            halo(n, 1).start()

        @pl.when((c == 1) & (k == 0))
        def _(n=n):
            halo(n, 2).start()

        if n == 0:
            steps(2, 4, 5)
        else:
            steps(0, *range(8, total))
            steps(1, 7)

    steps(4, 3)
    for slot in range(2):
        q_ref[slot] = projected(2, slot)
    steps(3, 4, 5)
    steps(2, 6)

    for n in range(2):

        @pl.when(c == 0)
        def _(n=n):
            halo(n, 0).wait_send()
            halo(n, 1).wait_recv()

        @pl.when(c == 1)
        def _(n=n):
            halo(n, 0).wait_recv()
            halo(n, 1).wait_send()

        @pl.when((c == 1) & (k == 0))
        def _(n=n):
            halo(n, 2).wait_send()

        @pl.when((c == 0) & (k == 1))
        def _(n=n):
            halo(n, 2).wait_recv()

    def mask_of(slot, row):
        first = (4 * k + 2 * slot + c) * piece
        query_pos = first + lax.broadcasted_iota(jnp.int32, (piece, PAD + piece), 0)
        key_pos = first - PAD + lax.broadcasted_iota(jnp.int32, (piece, PAD + piece), 1)
        start = jnp.zeros((piece, PAD + piece), jnp.int32)
        reached = 0
        for doc in range(lengths_ref.shape[1]):
            reached = reached + lengths_ref[row, doc]
            start = jnp.maximum(start, jnp.where(query_pos >= reached, reached, 0))
        return (key_pos >= start) & (key_pos <= query_pos) & (query_pos - key_pos < WINDOW)

    def attend(slot, row):
        allowed = mask_of(slot, row)
        span_rows = slice(row * piece, (row + 1) * piece)
        for head in range(HEADS // 2):
            cols = slice(head * HEAD_DIM, (head + 1) * HEAD_DIM)
            scores = nt_dot(q_ref[slot, span_rows, cols], flat(k_ref[2 * slot + row, :, :, cols])) * scale
            scores = jnp.where(allowed, scores, -1e30)
            exps = jnp.exp(scores - jnp.max(scores, axis=-1, keepdims=True))
            probs = exps / jnp.sum(exps, axis=-1, keepdims=True)
            p_ref[slot, row, head] = probs
            atb[slot, head // 2, head % 2, span_rows, :] = low(mm(low(probs), flat(v_ref[2 * slot + row, :, :, cols])))

    attend(1 - h, 0)
    attend(1 - h, 1)
    at_copy().start()
    og_copy(h).start()
    steps(1, 8)
    steps(2, 7)
    steps(3, 6)
    attend(h, 0)
    attend(h, 1)
    at8[pl.ds(2 * h, 2)] = atb[h]
    steps(4, 4, 5)
    at_copy().wait()
    at_side().start()
    attended = jnp.concatenate([at8[i // 2, i % 2] for i in range(8)], axis=1)
    for n in range(2):
        cols = slice(n * HALF, (n + 1) * HALF)
        mid[:, cols] = wide(outs[0, n]) + mm(attended, flat(wo[n]))
    middle = mid[...]
    spread(normed_of(middle, 8), nt8, h)
    nt_copy(h).start()
    nt_side(2, h).start()
    acc[h] = middle
    acc[1 - h] = jnp.zeros(middle.shape, jnp.float32)
    gn[...] = jnp.zeros(gn.shape, jnp.float32)

    def feed(f, slot):
        w_pair = flat(wm[f, :, :, :, :, :, 0 : 2 * PART])
        w_down = flat(wm[f, :, :, :, :, :, 2 * PART : 3 * PART])
        both = mm(joined(nt8, slot), w_pair)
        gates, ups = both[:, 0:PART], both[:, PART:]
        grad_hidden = mm(joined(og8, slot), w_down)
        sigmoid = 1.0 / (1.0 + jnp.exp(-gates))
        silu = gates * sigmoid
        hidden = low(silu * ups)
        grad_gates = low(grad_hidden * ups * sigmoid * (1.0 + gates * (1.0 - sigmoid)))
        grad_ups = low(grad_hidden * silu)
        tri[f, 0, slot] = grad_gates
        tri[f, 1, slot] = grad_ups
        tri[f, 2, slot] = hidden
        tri_copy(f, slot).start()
        acc[slot] += nt_dot(hidden, w_down)
        gn[slot] += nt_dot(jnp.concatenate([grad_gates, grad_ups], axis=1), w_pair)

    n_tokens = 2 * tokens

    def ff_grads(f):
        remote(tri.at[f], tri_peer.at[f], tri_send.at[f], tri_recv.at[f], here.peer()).wait()
        pair = mm(nt_t[:, 0:n_tokens], jnp.concatenate([flat(tri[f, 0]), flat(tri[f, 1])], axis=1)) + mm(
            nt_t[:, n_tokens:], jnp.concatenate([flat(tri_peer[f, 0]), flat(tri_peer[f, 1])], axis=1)
        )
        down = mm(og_t[:, 0:n_tokens], flat(tri[f, 2])) + mm(og_t[:, n_tokens:], flat(tri_peer[f, 2]))
        wm[f, :, 0, :, :, :, 0 : 2 * PART] = low(pair).reshape(4, 2, 2, -1, 2 * PART)
        wm[f, :, 0, :, :, :, 2 * PART : 3 * PART] = low(down).reshape(4, 2, 2, -1, PART)

    chunks = tiles + 6

    def chunk(n):
        if n < tiles:
            return wm.at[n, :, 0], mlp_twos.at[n], mlp_ends.at[n]
        n -= tiles
        if n < 2:
            return k_ref.at[:, pl.ds(4 * n, 4)], mgo_twos.at[n], mgo_ends.at[n]
        if n < 5:
            source = mga if n == 2 else v_ref.at[:, pl.ds(4 * (n - 3), 4)]
            return source, mga_twos.at[n - 2], mga_ends.at[n - 2]
        return nb_sum, nb_twos, nb_ends

    def store_tile(n, mine, others):
        back, across, on = others
        for half, value in ((h, mine + across), (1 - h, back + on)):
            for i, ref in enumerate((og_out, ou_out, od_out)):
                ref[:, lanes_at(half * span + n * PART, PART)] = value[:, i * PART : (i + 1) * PART]

    def store(n, mine, others):
        if n < tiles:
            store_tile(n, mine, others)
            return
        back, across, on = others
        n -= tiles
        if 2 <= n < 5:
            for half, value in ((h, mine + across), (1 - h, back + on)):
                (oq_ref, ok_ref, ov_ref)[n - 2][:, lanes_at(half * HALF, HALF)] = value
            return
        value = mine + back + across + on
        if n < 2:
            oo_ref[:, n * HALF : (n + 1) * HALF] = value
        else:
            on_ref[...] = value

    def sum_tick(t):
        for stage, lag in enumerate(SUM_LAGS):
            n = t - lag
            if not 0 <= n < chunks:
                continue
            source, twos, ends = chunk(n)
            if stage == 0:
                scatter.second(n, source, twos)
            elif stage == 1:
                scatter.third(n, source, twos, ends)
            else:
                store(n, *scatter.fourth(n, source, ends))

    def launch_tile(f):
        scatter.first(f, wm.at[f, :, 0], mlp_twos.at[f])

    def launch(n):
        source, twos, _ = chunk(n)
        scatter.first(n, source, twos)

    @pl.loop(0, FIRST_TILES)
    def _(f):
        tile_steps(f)
        gather.fifth(early + f, wm.at[f])
        feed(f, h)

    og_copy(1 - h).wait()
    og_side(1, 1 - h).start()
    nt_copy(1 - h).wait()
    nt_side(3, 1 - h).start()

    @pl.loop(0, FIRST_TILES)
    def _(f):
        @pl.when(FIRST_TILES + f < tiles)
        def _():
            tile_steps(FIRST_TILES + f)

        feed(f, 1 - h)

    @pl.loop(FIRST_TILES, tiles)
    def _(f):
        gather.fifth(early + f, wm.at[f])
        feed(f, h)
        feed(f, 1 - h)

    swap[0] = low(gn[1 - h])
    swap_copy(0).start()
    for number, slot in ((0, h), (1, 1 - h)):
        og_side(number, slot).wait()
    turned(lambda i: flat(og8[i, c]), lambda i: flat(og_peer[i]), og_t)
    for number, slot in ((2, h), (3, 1 - h)):
        nt_side(number, slot).wait()
    turned(lambda i: flat(nt8[i, c]), lambda i: flat(nt_peer[i]), nt_t)

    @pl.loop(0, tiles)
    def _(f):
        ff_grads(f)
        launch_tile(f)


    def close_middle():
        swap_copy(0).wait()
        middle = mid[...]
        factor = lax.rsqrt(jnp.mean(middle * middle, axis=-1, keepdims=True) + 1e-05)
        grad_normed = gn[h] + wide(swap_in[0])
        through = grad_normed * gain[8:9, :]
        shift = jnp.mean(through * middle, axis=-1, keepdims=True) * factor * factor * factor
        grad_middle = wide(joined(og8, h)) + factor * through - middle * shift
        gi_ref[...] = grad_middle
        gb[...] = low(grad_middle)
        gb_side().start()
        gain[8:16, :] = jnp.broadcast_to(
            jnp.sum(grad_normed * middle * factor, axis=0, keepdims=True), (8, middle.shape[1])
        )

    def to_attended():
        def part(half):
            rows = pl.ds(2 * half, 2)
            return low(nt_dot(gb[:, 0:HALF], flat(wo[0, rows])) + nt_dot(gb[:, HALF:], flat(wo[1, rows])))

        swap[0, :, 0:HALF] = part(1 - h)
        ga_copy().start()
        swap[1] = low(acc[1 - h])
        swap_copy(1).start()
        gat[h] = part(h)

    def keep_out():
        mid[...] = acc[h]

    def close_out():
        swap_copy(1).wait()
        swap[1] = low(mid[...] + wide(swap_in[1]))
        out_store().start()

    def attend_back(slot):
        for row in range(2):
            span_rows = slice(row * piece, (row + 1) * piece)
            for head in range(HEADS // 2):
                cols = slice(head * HEAD_DIM, (head + 1) * HEAD_DIM)
                there = slice(row * HALF + head * HEAD_DIM, row * HALF + (head + 1) * HEAD_DIM)
                grad = gat[slot, span_rows, cols]
                probs = p_ref[slot, row, head]
                gn[slot, :, there] = tn_dot(low(probs), grad)
                grad_probs = nt_dot(grad, flat(v_ref[2 * slot + row, :, :, cols]))
                inner = jnp.sum(grad_probs * probs, axis=-1, keepdims=True)
                grad_scores = low(probs * (grad_probs - inner))
                outs[2, slot, span_rows, cols] = low(mm(grad_scores, flat(k_ref[2 * slot + row, :, :, cols])) * scale)
                acc[slot, :, there] = tn_dot(grad_scores, q_ref[slot, span_rows, cols]) * scale
            there = slice(row * HALF, (row + 1) * HALF)
            edge[0, slot, row] = low(acc[slot, PAD - WINDOW : PAD, there])
            edge[1, slot, row] = low(gn[slot, PAD - WINDOW : PAD, there])

    def send_edge():
        out_copy(2).start()

        @pl.when(c == 1)
        def _():
            edge_copy(0).start()

        @pl.when(c == 0)
        def _():
            edge_copy(1).start()

        @pl.when((c == 0) & (k == 1))
        def _():
            edge_copy(2).start()

    def close_edge():
        @pl.when(c == 1)
        def _():
            edge_copy(0).wait_send()
            edge_copy(1).wait_recv()

        @pl.when(c == 0)
        def _():
            edge_copy(0).wait_recv()
            edge_copy(1).wait_send()

        @pl.when((c == 0) & (k == 1))
        def _():
            edge_copy(2).wait_send()

        @pl.when((c == 1) & (k == 0))
        def _():
            edge_copy(2).wait_recv()

        inside = piece - WINDOW
        for m, source in ((0, acc), (1, gn)):
            for slot in range(2):
                for row in range(2):
                    there = slice(row * HALF, (row + 1) * HALF)
                    first = row * piece
                    outs[m, slot, first : first + inside, :] = low(source[slot, PAD : PAD + inside, there])
                    outs[m, slot, first + inside : first + piece, :] = low(
                        source[slot, PAD + inside : PAD + piece, there] + wide(edge_in[m, slot, row])
                    )
            out_copy(m).start()

    def to_input(slot):
        grad = nt_dot(outs[0, slot], flat(wa[0]))
        for m in (1, 2):
            grad = grad + nt_dot(outs[m, slot], flat(wa[m]))
        return grad

    def inverse_rms(value):
        return lax.rsqrt(jnp.mean(value * value, axis=-1, keepdims=True) + 1e-05)

    def send_input():
        x = wide(xm[...])
        part = to_input(1 - h)
        swap[0] = low(part)
        swap_copy(2).start()
        one = jnp.sum(part * x * inverse_rms(x), axis=0, keepdims=True)
        part = to_input(h)
        acc[0] = part
        for i in range(2):
            x_again(i).wait()
        x = wide(jnp.concatenate([gat[0], gat[1]], axis=1))
        one = one + jnp.sum(part * x * inverse_rms(x), axis=0, keepdims=True)
        width = one.shape[1]
        stacked = jnp.concatenate(
            [
                jnp.broadcast_to(one, (LANES // 2, width)),
                jnp.broadcast_to(gain[8:9, :], (LANES // 2, width)),
            ],
            axis=0,
        )
        nb[...] = low(stacked.T).reshape(nb.shape)
        pair_side().start()

    def close_input():
        swap_copy(2).wait()
        grad_normed = acc[0] + wide(swap_in[2])
        x = wide(jnp.concatenate([gat[0], gat[1]], axis=1))
        factor = inverse_rms(x)
        through = grad_normed * gain[0:1, :]
        shift = jnp.mean(through * x, axis=-1, keepdims=True) * factor * factor * factor
        gi_ref[...] += factor * through - x * shift

    def close_norm():
        pair_side().wait()
        nb_sum[...] = low(wide(nb[:, c]) + wide(nb_peer[...]))

    def turn_normed():
        no_side().wait()
        turned(lambda i: flat(no8[i, c]), lambda i: flat(no_peer[i]), no_t)

    def wout_grads():
        at_side().wait()
        turned(lambda i: at8[i, c], lambda i: at_peer[i], og_t)
        gb_side().wait()
        for n in range(2):
            cols = slice(n * HALF, (n + 1) * HALF)
            grad = mm(og_t[:, 0:tokens], gb[:, cols]) + mm(og_t[:, tokens : 2 * tokens], gb_peer[:, cols])
            k_ref[:, 4 * n : 4 * n + 4] = low(grad).reshape(4, 4, -1, HALF)

    def attn_grads(m):
        out_copy(m).wait()
        grad = mm(no_t[:, 0:n_tokens], flat(outs[m])) + mm(no_t[:, n_tokens:], flat(outs_peer[m]))
        if m == 2:
            mga[...] = low(grad).reshape(mga.shape)
        else:
            v_ref[:, 4 * m : 4 * m + 4] = low(grad).reshape(4, 4, -1, HALF)

    def ticks(first, last):
        for t in range(first, last):
            sum_tick(t)

    ticks(0, 1)
    close_middle()
    to_attended()
    keep_out()
    ticks(1, 3)
    attend_back(h)
    ga_copy().wait()
    ticks(3, 4)
    attend_back(1 - h)
    send_edge()
    for i in range(2):
        x_again(i).start()
    ticks(4, 6)
    turn_normed()
    attn_grads(2)
    wout_grads()
    launch(tiles)
    launch(tiles + 1)
    launch(tiles + 2)
    ticks(6, 8)
    close_edge()
    send_input()
    for m in range(2):
        attn_grads(m)
        launch(tiles + 3 + m)
    close_norm()
    launch(tiles + 5)
    ticks(8, tiles + 1)
    close_out()
    ticks(tiles + 1, tiles + 2)
    close_input()
    ticks(tiles + 2, chunks + SUM_LAGS[-1])
    out_store().wait()


def deliver_kernel(count, *refs):
    sources, targets, held = (refs[i * count : (i + 1) * count] for i in range(3))
    in_sem, out_sem = refs[3 * count :]
    ins = [pltpu.make_async_copy(s, v, in_sem.at[i]) for i, (s, v) in enumerate(zip(sources, held))]
    outs = [pltpu.make_async_copy(v, t, out_sem.at[i]) for i, (v, t) in enumerate(zip(held, targets))]
    for copy in ins:
        copy.start()
    for arrived, leaving in zip(ins, outs):
        arrived.wait()
        leaving.start()
    for copy in outs:
        copy.wait()


def delivered(arrays):
    anywhere = pl.BlockSpec(memory_space=pl.ANY)
    count = len(arrays)
    return pl.pallas_call(
        functools.partial(deliver_kernel, count),
        out_shape=[jax.ShapeDtypeStruct(a.shape, a.dtype) for a in arrays],
        in_specs=[anywhere] * count,
        out_specs=[anywhere] * count,
        scratch_shapes=[pltpu.VMEM(a.shape, a.dtype) for a in arrays]
        + [pltpu.SemaphoreType.DMA((count,)), pltpu.SemaphoreType.DMA((count,))],
        compiler_params=pltpu.CompilerParams(vmem_limit_bytes=60 * 2**20),
        name="deliver",
    )(*arrays)


def fused(hidden_in, lengths, out_grad, gain_shards, weight_shards):
    hidden = hidden_in.reshape(-1, hidden_in.shape[-1])
    tokens, width = hidden.shape
    gains = jnp.concatenate(
        [jnp.broadcast_to(g[:, None], (g.shape[0], LANES // 2)) for g in gain_shards], axis=1
    )
    rows = gains.shape[0]
    tiles = weight_shards[4].shape[1] // (2 * PART)
    bf, fl = jnp.bfloat16, jnp.float32
    every, mine = (4, 2, 2, 2, rows), (4, 2, 2, rows)
    part = 3 * PART
    dma = pltpu.SemaphoreType.DMA
    vmem, anywhere = pl.BlockSpec(memory_space=pltpu.VMEM), pl.BlockSpec(memory_space=pl.ANY)
    shape = jax.ShapeDtypeStruct
    piece = tokens // 2
    keys = (4, (PAD + piece) // rows, rows, HALF)
    scratch = [
        ((*every, LANES), bf), ((3, *every, HALF), bf), ((2, *every, HALF), bf), ((tiles, *every, part), bf),
        ((3, rows, HALF), bf), ((tiles, rows, part), bf), ((tokens, width), bf),
        *[((4, 2, 2, tokens, PART), bf)] * 3, ((4, 2, tokens, PART), bf), ((2, 2, 2, tokens, PART), bf),
        *[((4, 2, tokens, PART), bf)] * 3, ((4, tokens, PART), bf),
        *[((width // 2, 4 * tokens), bf)] * 2,
        ((2, tokens, HALF), bf), (keys, bf), (keys, bf), ((2, 2, HEADS // 2, piece, PAD + piece), fl),
        ((tokens, width), fl), ((2, tokens, width), fl), ((2, tokens, width), fl),
        ((16, width), fl), ((tiles, 3, 2, tokens, PART), bf), ((tiles, 3, 2, tokens, PART), bf),
        ((2, tokens, width), bf), ((3, tokens, width), bf), ((2, tokens, HALF), bf),
        ((2, 2, 2, WINDOW, HALF), bf), ((2, 2, 2, WINDOW, HALF), bf),
        ((3, 2, tokens, HALF), bf), ((3, 2, tokens, HALF), bf), ((tokens, width), bf), ((tokens, width), bf),
        ((*mine, HALF), bf),
        ((*mine, LANES), bf), ((*mine, LANES), bf),
        ((tiles, 3, 4, rows, part), bf), ((tiles, 3, rows, part), bf),
        ((3, 3, 4, rows, HALF), bf), ((3, 3, rows, HALF), bf),
        ((2, 3, 4, rows, HALF), bf), ((2, 3, rows, HALF), bf),
        ((3, 4, rows, LANES), bf), ((3, rows, LANES), bf),
    ]
    count, chunks = 6 + tiles, 6 + tiles
    results = pl.pallas_call(
        layer_kernel,
        out_shape=[shape((tokens, width), bf), shape((tokens, width), fl)]
        + [shape((rows, width), fl)] * 4 + [shape((rows, 2 * tiles * PART), fl)] * 3
        + [shape((rows, LANES), fl)],
        in_specs=[anywhere, anywhere, pl.BlockSpec(memory_space=pltpu.SMEM)] + [anywhere] * 8,
        out_specs=[anywhere] + [vmem] * 9,
        scratch_shapes=[pltpu.VMEM(*s) for s in scratch]
        + [
            dma((count, 2)), dma((count, 4)), dma((count, 4)), dma((chunks, 4)), dma((chunks, 4)),
            dma((2, 2)), dma((2, 2)), dma((2,)), dma((2,)), dma((8,)), dma((8,)),
            dma((tiles,)), dma((tiles,)), dma((8,)), dma((8,)), dma((3,)), dma((3,)), dma((12,)),
        ],
        compiler_params=pltpu.CompilerParams(
            collective_id=0, has_side_effects=True, vmem_limit_bytes=63 * 2**20
        ),
        name="layer",
    )(hidden, out_grad.reshape(hidden.shape), lengths, gains, *weight_shards)
    block_out, grad_in, query, key, value, wout, gate, up, down, norms = delivered(results)
    return (
        block_out.reshape(hidden_in.shape), grad_in.reshape(hidden_in.shape),
        norms[:, 0], query, key, value, wout, norms[:, LANES // 2], gate, up, down,
    )


def layer(hidden_in, lengths, out_grad, gains, weights):
    score_scale = 1.0 / math.sqrt(HEAD_DIM)
    tokens = hidden_in.shape[1]
    gain_one, gain_two = gains
    w_query, w_key, w_value, w_out, w_gate, w_up, w_down = weights
    inputs = hidden_in.astype(jnp.float32)
    normed_one = rms_scale(inputs, gain_one).astype(jnp.bfloat16)
    queries = project(normed_one, w_query).astype(jnp.bfloat16)
    keys = project(normed_one, w_key).astype(jnp.bfloat16)
    values = project(normed_one, w_value).astype(jnp.bfloat16)
    tails = jnp.stack([keys[:, tokens - WINDOW :], values[:, tokens - WINDOW :]])
    received = passed_along(tails, "seq", 1)
    keys_all = jnp.concatenate([received[0], keys], axis=1)
    values_all = jnp.concatenate([received[1], values], axis=1)
    allowed = window_mask(lengths, lax.axis_index("seq"), tokens)
    scores = scores_of(queries, keys_all, allowed)
    top = jnp.max(scores, axis=-1, keepdims=True)
    exps = jnp.exp(scores - top)
    probs = exps / jnp.sum(exps, axis=-1, keepdims=True)
    probs_low = probs.astype(jnp.bfloat16)
    mixed = jnp.einsum(
        "rhqk,rkhd->rqhd", probs_low, split_heads(values_all), preferred_element_type=jnp.float32
    )
    attended = merge_heads(mixed).astype(jnp.bfloat16)
    middle = inputs + project(attended, w_out)
    normed_two = rms_scale(middle, gain_two).astype(jnp.bfloat16)
    gates = project(normed_two, w_gate)
    ups = project(normed_two, w_up)
    hidden_act = swiglu(gates, ups).astype(jnp.bfloat16)
    block_out = (middle + project_back(hidden_act, w_down)).astype(jnp.bfloat16)
    grad_hidden = project(out_grad, w_down)
    unused, swiglu_back = jax.vjp(swiglu, gates, ups)
    grad_gates, grad_ups = swiglu_back(grad_hidden)
    grad_gates = grad_gates.astype(jnp.bfloat16)
    grad_ups = grad_ups.astype(jnp.bfloat16)
    grad_down = weight_grad(out_grad, hidden_act)
    grad_gate = weight_grad(normed_two, grad_gates)
    grad_up = weight_grad(normed_two, grad_ups)
    grad_normed_two = project_back(grad_gates, w_gate) + project_back(grad_ups, w_up)
    unused, norm_two_back = jax.vjp(rms_scale, middle, gain_two)
    grad_middle_part, grad_norm2 = norm_two_back(grad_normed_two)
    grad_middle = out_grad.astype(jnp.float32) + grad_middle_part
    grad_branch = grad_middle.astype(jnp.bfloat16)
    grad_wout = weight_grad(attended, grad_branch)
    grad_attended = project_back(grad_branch, w_out).astype(jnp.bfloat16)
    grad_heads = split_heads(grad_attended)
    grad_values_all = jnp.einsum(
        "rhqk,rqhd->rkhd", probs_low, grad_heads, preferred_element_type=jnp.float32
    )
    grad_probs = jnp.einsum(
        "rqhd,rkhd->rhqk", grad_heads, split_heads(values_all), preferred_element_type=jnp.float32
    )
    grad_scores = (
        probs * (grad_probs - jnp.sum(grad_probs * probs, axis=-1, keepdims=True))
    ).astype(jnp.bfloat16)
    grad_queries = score_scale * merge_heads(
        jnp.einsum(
            "rhqk,rkhd->rqhd", grad_scores, split_heads(keys_all),
            preferred_element_type=jnp.float32,
        )
    )
    grad_keys_all = score_scale * merge_heads(
        jnp.einsum(
            "rhqk,rqhd->rkhd", grad_scores, split_heads(queries),
            preferred_element_type=jnp.float32,
        )
    )
    grad_values_all = merge_heads(grad_values_all)
    halo_grads = jnp.stack([grad_keys_all[:, :WINDOW], grad_values_all[:, :WINDOW]])
    returned = passed_along(halo_grads.astype(jnp.bfloat16), "seq", -1).astype(halo_grads.dtype)
    grad_keys = (
        grad_keys_all[:, WINDOW:].at[:, tokens - WINDOW :].add(returned[0]).astype(jnp.bfloat16)
    )
    grad_values = (
        grad_values_all[:, WINDOW:].at[:, tokens - WINDOW :].add(returned[1]).astype(jnp.bfloat16)
    )
    grad_queries = grad_queries.astype(jnp.bfloat16)
    grad_query = weight_grad(normed_one, grad_queries)
    grad_key = weight_grad(normed_one, grad_keys)
    grad_value = weight_grad(normed_one, grad_values)
    grad_normed_one = (
        project_back(grad_queries, w_query)
        + project_back(grad_keys, w_key)
        + project_back(grad_values, w_value)
    )
    unused, norm_one_back = jax.vjp(rms_scale, inputs, gain_one)
    grad_inputs_part, grad_norm1 = norm_one_back(grad_normed_one)
    grad_in = grad_middle + grad_inputs_part
    grads = (grad_query, grad_key, grad_value, grad_wout, grad_gate, grad_up, grad_down)
    return block_out, grad_in, (grad_norm1, grad_norm2), grads


def shards(
    hidden_in, lengths, norm1_gain, w_query, w_key, w_value, w_out,
    norm2_gain, w_gate, w_up, w_down, out_grad,
):
    gain_shards = (norm1_gain, norm2_gain)
    weight_shards = (w_query, w_key, w_value, w_out, w_gate, w_up, w_down)
    if (lax.axis_size("seq"), lax.axis_size("rows")) == (SEQ_PIECES, ROW_GROUPS):
        return fused(hidden_in, lengths, out_grad, gain_shards, weight_shards)
    gains = [g.astype(jnp.float32) for g in gathered_by_xla(gain_shards)]
    weights = gathered_by_xla(weight_shards)
    block_out, grad_in, norms, grads = layer(hidden_in, lengths, out_grad, gains, weights)
    norms, grads = scattered_by_xla(norms), scattered_by_xla(grads)
    return (
        block_out, grad_in, norms[0], grads[0], grads[1], grads[2], grads[3],
        norms[1], grads[4], grads[5], grads[6],
    )


def solution(mesh):
    tokens = P("rows", "seq", None)
    vector = P(("seq", "rows"))
    matrix = P(("seq", "rows"), None)
    in_specs = (
        tokens, P("rows", None), vector, matrix, matrix, matrix, matrix,
        vector, matrix, matrix, matrix, tokens,
    )
    out_specs = (
        tokens, tokens, vector, matrix, matrix, matrix, matrix,
        vector, matrix, matrix, matrix,
    )
    return jax.shard_map(shards, mesh=mesh, in_specs=in_specs, out_specs=out_specs, check_vma=False)
```

time: 365 us -> 194 us (0.53)
  Pallas kernels: 274 us -> 189 us
  matrix products: 55.2 us -> 0 us
  local copies, waits for them, and re-layouts: 18.5 us -> 2.78 us
  other arithmetic: 10.6 us -> 0.68 us
  starting transfers between devices: 4.6 us -> 0 us
    pallas_call x2, Pallas kernels: 274 us -> 189 us  [the longest x1 186 us: fused(): pl.pallas_call(layer_kernel, out_shape=[shape((tokens, width), bf), shape...]
    dot_general x26 -> x0, matrix products: 54.5 us -> none  [the longest x7 22.9 us: weight_grad(): jnp.einsum('rtd,rtf->df', left, grad, preferred_element_type=jnp.float32)]
    unnamed x89 -> x6, local copies, waits for them, and re-layouts: 11.4 us -> 1.94 us
    ppermute x2 -> x0, starting transfers between devices: 4.6 us -> none  [passed_along(): return lax.ppermute(block, axis, route)]
  transfers between devices with their start and end apart: 2 -> 0, of which waited for: 0 -> 0; matrix products, arithmetic and copies ran while one was open for 4% -> 0% of each run, Pallas kernels for 0% -> 0%
where the time goes in v3:
time: 194 us
  Pallas kernels  189 us (97%)
  local copies, waits for them, and re-layouts  2.78 us (1%)
    pallas_call x1, Pallas kernels, fused(): pl.pallas_call(layer_kernel, out_shape=[shape((tokens, width), bf), shape...  186 us

profile of v3, /device:TPU:0, one launch (start us, length us, event | category | flops | bytes accessed | tf_op | source)
XLA Modules:
  0.0 193.6 jit_solution(2021486569917330541)
XLA Ops:
  0.6 0.0 copy-start.1
  0.7 0.6 copy-done.1
  1.3 0.0 copy-start.2
  1.3 0.1 broadcast_in_dim.4
  1.4 0.6 copy-done.2
  2.0 0.1 broadcast_in_dim.5
  2.0 0.7 pad_maximum_fusion.gains_in
  2.7 186.4 %layer.1 = (bf16[256,1024]{1,0:T(8,128)(2,1)}, f32[256,1024]{1,0:T(8,128)}, f32[32,1024]{1,0:T(8,128)}, f32[32,1024]{1,0:T(8,128)}, f32[32,1024]{1,0:T(8,128)}, ...) custom-call(bf16[256,1024]{1,0:T(8,128)(2,1)} %bitcast.4, ...), custom_call_target="tpu_custom_call" | custom-call | tf_op jit(solution)/shard_map/layer/pallas_call | solution.py:1028
  189.1 3.1 %deliver.1 = (bf16[256,1024]{1,0:T(8,128)(2,1)}, f32[256,1024]{1,0:T(8,128)}, f32[32,1024]{1,0:T(8,128)}, f32[32,1024]{1,0:T(8,128)}, f32[32,1024]{1,0:T(8,128)}...) custom-call(bf16[256,1024]{1,0:T(8,128)(2,1)} %get-tuple-element.31., ...), custom_call_target="tpu_custom_call" | custom-call | tf_op jit(solution)/shard_map/deliver/pallas_call | solution.py:980
  192.2 0.0 copy-start
  192.2 0.7 copy-done
  192.9 0.7 slice_reduce_fusion
Async XLA Ops:
  0.6 0.7 copy-start.1
  1.3 0.7 copy-start.2
  192.2 0.7 copy-start

commit v4 on v3

--- a/solution.py
+++ b/solution.py
@@ -104,9 +104,9 @@
 PART = 128
 HALF = 512
 PAD = 128
-AHEAD = (11, 3, 2, 1)
+AHEAD = (11, 6, 4, 2)
 FIRST_TILES = 7
-SUM_LAGS = (0, 2, 4)
+SUM_LAGS = (0, 4, 8)
 
 
 class Place:
@@ -220,9 +220,10 @@
             if pack is not None:
                 pltpu.make_async_copy(given, pack.at[:, pl.ds(first, width)], self.own_sem.at[n, 1]).start()
 
-    def first(self, n, whole, pack):
+    def first(self, n, whole, pack, fetched=True):
         slot = self.slot(whole)
-        pltpu.make_async_copy(slot, slot, self.own_sem.at[n, 0]).wait()
+        if fetched:
+            pltpu.make_async_copy(slot, slot, self.own_sem.at[n, 0]).wait()
         if pack is not None:
             pltpu.make_async_copy(pack, pack, self.own_sem.at[n, 1]).wait()
         for step in (1, 2, 3):
@@ -310,7 +311,7 @@
 
 
 def layer_kernel(
-    x_in, og_in, lengths_ref, gains_in, wq_in, wk_in, wv_in, wo_in, wg_in, wu_in, wd_in,
+    x_in, og_in, lengths_ref, one_in, two_in, wq_in, wk_in, wv_in, wo_in, wg_in, wu_in, wd_in,
     out_ref, gi_ref, oq_ref, ok_ref, ov_ref, oo_ref, og_out, ou_out, od_out, on_ref,
     wn, wa, wo, wm, pack_a, pack_m, xm, og8, nt8, no8, at8, atb, og_peer, nt_peer, no_peer, at_peer,
     og_t, nt_t, q_ref, k_ref, v_ref, p_ref, mid, acc, gn, gain, tri, tri_peer,
@@ -343,7 +344,7 @@
 
     def parts_of(n):
         if n == 0:
-            return [(gains_in, None, 0, LANES)]
+            return []
         if n < 4:
             source = (wk_in, wv_in, wq_in)[n - 1]
             return [(source.at[:, lanes_at(h * HALF, HALF)], source.at[:, lanes_at((1 - h) * HALF, HALF)], 0, HALF)]
@@ -363,7 +364,7 @@
         late = n >= early
         whole = wm.at[n - early] if late else whole_of(n)
         if stage == 0:
-            gather.first(n, whole, pack_m.at[n - early] if late else pack_of(n))
+            gather.first(n, whole, pack_m.at[n - early] if late else pack_of(n), n != 0)
         else:
             (gather.second, gather.third, gather.fourth, gather.fifth)[stage - 1](n, whole)
 
@@ -473,6 +474,12 @@
             target[rows, 0 : left.shape[0]] = low(wide(left).T)
             target[rows, left.shape[0] : 2 * left.shape[0]] = low(wide(right).T)
 
+    def turned_slot(source, peer, target, slot):
+        for level in range(4):
+            rows = slice(level * PART, (level + 1) * PART)
+            target[rows, lanes_at(slot * tokens, tokens)] = low(wide(source[level, c, slot]).T)
+            target[rows, lanes_at((2 + slot) * tokens, tokens)] = low(wide(peer[level, slot]).T)
+
     og_fetches = [
         pltpu.make_async_copy(og_in.at[:, pl.ds(i * PART, PART)], og8.at[i // 2, i % 2, h], host_sem.at[i])
         for i in range(8)
@@ -482,6 +489,8 @@
     ]
     for n in range(early):
         gather.begin(n, parts_of(n), whole_of(n), pack_of(n))
+    gain_columns = [jnp.broadcast_to(wide(g[...])[None, :], (LANES // 2, rows)) for g in (one_in, two_in)]
+    gather.slot(wn)[...] = low(jnp.concatenate(gain_columns, axis=0).T)
     for copy in og_fetches + x_fetches:
         copy.start()
 
@@ -556,7 +565,7 @@
         if n == 0:
             steps(2, 4, 5)
         else:
-            steps(0, *range(8, total))
+            steps(0, 8, 9, 10)
             steps(1, 7)
 
     steps(4, 3)
@@ -611,14 +620,17 @@
     attend(1 - h, 0)
     attend(1 - h, 1)
     at_copy().start()
+    steps(0, *range(11, total))
     og_copy(h).start()
-    steps(1, 8)
+    steps(1, 8, 9)
     steps(2, 7)
     steps(3, 6)
     attend(h, 0)
     attend(h, 1)
     at8[pl.ds(2 * h, 2)] = atb[h]
     steps(4, 4, 5)
+    steps(1, 10)
+    steps(2, 8)
     at_copy().wait()
     at_side().start()
     attended = jnp.concatenate([at8[i // 2, i % 2] for i in range(8)], axis=1)
@@ -629,6 +641,9 @@
     spread(normed_of(middle, 8), nt8, h)
     nt_copy(h).start()
     nt_side(2, h).start()
+    steps(1, 11)
+    steps(2, 9)
+    steps(3, 7)
     acc[h] = middle
     acc[1 - h] = jnp.zeros(middle.shape, jnp.float32)
     gn[...] = jnp.zeros(gn.shape, jnp.float32)
@@ -651,6 +666,10 @@
         acc[slot] += nt_dot(hidden, w_down)
         gn[slot] += nt_dot(jnp.concatenate([grad_gates, grad_ups], axis=1), w_pair)
 
+    og_side(0, h).wait()
+    turned_slot(og8, og_peer, og_t, h)
+    nt_side(2, h).wait()
+    turned_slot(nt8, nt_peer, nt_t, h)
     n_tokens = 2 * tokens
 
     def ff_grads(f):
@@ -744,12 +763,10 @@
 
     swap[0] = low(gn[1 - h])
     swap_copy(0).start()
-    for number, slot in ((0, h), (1, 1 - h)):
-        og_side(number, slot).wait()
-    turned(lambda i: flat(og8[i, c]), lambda i: flat(og_peer[i]), og_t)
-    for number, slot in ((2, h), (3, 1 - h)):
-        nt_side(number, slot).wait()
-    turned(lambda i: flat(nt8[i, c]), lambda i: flat(nt_peer[i]), nt_t)
+    og_side(1, 1 - h).wait()
+    turned_slot(og8, og_peer, og_t, 1 - h)
+    nt_side(3, 1 - h).wait()
+    turned_slot(nt8, nt_peer, nt_t, 1 - h)
 
     @pl.loop(0, tiles)
     def _(f):
@@ -925,77 +942,81 @@
         for t in range(first, last):
             sum_tick(t)
 
-    ticks(0, 1)
+    ticks(0, 2)
     close_middle()
     to_attended()
     keep_out()
-    ticks(1, 3)
+    ticks(2, 4)
     attend_back(h)
     ga_copy().wait()
-    ticks(3, 4)
     attend_back(1 - h)
     send_edge()
     for i in range(2):
         x_again(i).start()
-    ticks(4, 6)
+    ticks(4, 7)
     turn_normed()
     attn_grads(2)
     wout_grads()
     launch(tiles)
     launch(tiles + 1)
     launch(tiles + 2)
-    ticks(6, 8)
+    ticks(7, 9)
     close_edge()
+    ticks(9, 10)
     send_input()
     for m in range(2):
         attn_grads(m)
         launch(tiles + 3 + m)
     close_norm()
     launch(tiles + 5)
-    ticks(8, tiles + 1)
+    ticks(10, 14)
     close_out()
-    ticks(tiles + 1, tiles + 2)
     close_input()
-    ticks(tiles + 2, chunks + SUM_LAGS[-1])
+    ticks(14, chunks + SUM_LAGS[-1])
     out_store().wait()
 
 
 def deliver_kernel(count, *refs):
-    sources, targets, held = (refs[i * count : (i + 1) * count] for i in range(3))
-    in_sem, out_sem = refs[3 * count :]
+    sources, targets, refs = refs[:count], refs[count : 2 * count + 1], refs[2 * count + 1 :]
+    held, vectors, (in_sem, out_sem) = refs[:count], refs[count : count + 2], refs[count + 2 :]
     ins = [pltpu.make_async_copy(s, v, in_sem.at[i]) for i, (s, v) in enumerate(zip(sources, held))]
-    outs = [pltpu.make_async_copy(v, t, out_sem.at[i]) for i, (v, t) in enumerate(zip(held, targets))]
+    leave = (*vectors, *held[1:])
+    outs = [pltpu.make_async_copy(v, t, out_sem.at[i]) for i, (v, t) in enumerate(zip(leave, targets))]
     for copy in ins:
         copy.start()
-    for arrived, leaving in zip(ins, outs):
+    ins[0].wait()
+    turned = held[0][...].T
+    for i in range(2):
+        vectors[i][...] = turned[i * LANES // 2, :]
+        outs[i].start()
+    for arrived, leaving in zip(ins[1:], outs[2:]):
         arrived.wait()
         leaving.start()
     for copy in outs:
         copy.wait()
 
 
-def delivered(arrays):
+def delivered(norms, arrays):
     anywhere = pl.BlockSpec(memory_space=pl.ANY)
-    count = len(arrays)
+    count = len(arrays) + 1
+    vector = (norms.shape[:1], norms.dtype)
     return pl.pallas_call(
         functools.partial(deliver_kernel, count),
-        out_shape=[jax.ShapeDtypeStruct(a.shape, a.dtype) for a in arrays],
+        out_shape=[jax.ShapeDtypeStruct(*vector)] * 2 + [jax.ShapeDtypeStruct(a.shape, a.dtype) for a in arrays],
         in_specs=[anywhere] * count,
-        out_specs=[anywhere] * count,
-        scratch_shapes=[pltpu.VMEM(a.shape, a.dtype) for a in arrays]
-        + [pltpu.SemaphoreType.DMA((count,)), pltpu.SemaphoreType.DMA((count,))],
+        out_specs=[anywhere] * (count + 1),
+        scratch_shapes=[pltpu.VMEM(a.shape, a.dtype) for a in (norms, *arrays)]
+        + [pltpu.VMEM(*vector)] * 2
+        + [pltpu.SemaphoreType.DMA((count,)), pltpu.SemaphoreType.DMA((count + 1,))],
         compiler_params=pltpu.CompilerParams(vmem_limit_bytes=60 * 2**20),
         name="deliver",
-    )(*arrays)
+    )(norms, *arrays)
 
 
 def fused(hidden_in, lengths, out_grad, gain_shards, weight_shards):
     hidden = hidden_in.reshape(-1, hidden_in.shape[-1])
     tokens, width = hidden.shape
-    gains = jnp.concatenate(
-        [jnp.broadcast_to(g[:, None], (g.shape[0], LANES // 2)) for g in gain_shards], axis=1
-    )
-    rows = gains.shape[0]
+    rows = weight_shards[0].shape[0]
     tiles = weight_shards[4].shape[1] // (2 * PART)
     bf, fl = jnp.bfloat16, jnp.float32
     every, mine = (4, 2, 2, 2, rows), (4, 2, 2, rows)
@@ -1030,7 +1051,7 @@
         out_shape=[shape((tokens, width), bf), shape((tokens, width), fl)]
         + [shape((rows, width), fl)] * 4 + [shape((rows, 2 * tiles * PART), fl)] * 3
         + [shape((rows, LANES), fl)],
-        in_specs=[anywhere, anywhere, pl.BlockSpec(memory_space=pltpu.SMEM)] + [anywhere] * 8,
+        in_specs=[anywhere, anywhere, pl.BlockSpec(memory_space=pltpu.SMEM), vmem, vmem] + [anywhere] * 7,
         out_specs=[anywhere] + [vmem] * 9,
         scratch_shapes=[pltpu.VMEM(*s) for s in scratch]
         + [
@@ -1042,11 +1063,11 @@
             collective_id=0, has_side_effects=True, vmem_limit_bytes=63 * 2**20
         ),
         name="layer",
-    )(hidden, out_grad.reshape(hidden.shape), lengths, gains, *weight_shards)
-    block_out, grad_in, query, key, value, wout, gate, up, down, norms = delivered(results)
+    )(hidden, out_grad.reshape(hidden.shape), lengths, *gain_shards, *weight_shards)
+    one, two, block_out, grad_in, query, key, value, wout, gate, up, down = delivered(results[9], results[:9])
     return (
         block_out.reshape(hidden_in.shape), grad_in.reshape(hidden_in.shape),
-        norms[:, 0], query, key, value, wout, norms[:, LANES // 2], gate, up, down,
+        one, query, key, value, wout, two, gate, up, down,
     )
 
 

time: 194 us -> 181 us (0.933)
  Pallas kernels: 189 us -> 179 us
  local copies, waits for them, and re-layouts: 2.78 us -> 0 us
    pallas_call x1, Pallas kernels: 186 us -> 176 us  [fused(): pl.pallas_call(layer_kernel, out_shape=[shape((tokens, width), bf), shape...]
    unnamed x6 -> x0, local copies, waits for them, and re-layouts: 1.94 us -> none
where the time goes in v4:
time: 181 us; the launch traced here: 180 us
  Pallas kernels  179 us (99%)
    pallas_call x1, Pallas kernels, fused(): pl.pallas_call(layer_kernel, out_shape=[shape((tokens, width), bf), shape...  176 us

profile of v4, /device:TPU:0, one launch (start us, length us, event | category | flops | bytes accessed | tf_op | source)
XLA Modules:
  0.0 180.2 jit_solution(11680788254488238258)
XLA Ops:
  0.6 176.3 %layer.1 = (bf16[256,1024]{1,0:T(8,128)(2,1)}, f32[256,1024]{1,0:T(8,128)}, f32[32,1024]{1,0:T(8,128)}, f32[32,1024]{1,0:T(8,128)}, f32[32,1024]{1,0:T(8,128)}, ...) custom-call(bf16[256,1024]{1,0:T(8,128)(2,1)} %bitcast.4, ...), custom_call_target="tpu_custom_call" | custom-call | tf_op jit(solution)/shard_map/layer/pallas_call | solution.py:1049
  177.0 3.1 %deliver.1 = (f32[32]{0:T(128)}, f32[32]{0:T(128)}, bf16[256,1024]{1,0:T(8,128)(2,1)}, f32[256,1024]{1,0:T(8,128)}, f32[32,1024]{1,0:T(8,128)}, /*index=5*/f32[3...) custom-call(f32[32,128]{1,0:T(8,128)} %get-tuple-element.32.refs_0_,, ...), custom_call_target="tpu_custom_call" | custom-call | tf_op jit(solution)/shard_map/deliver/pallas_call | solution.py:1003

commit v5 on v4

--- a/solution.py
+++ b/solution.py
@@ -312,15 +312,16 @@
 
 def layer_kernel(
     x_in, og_in, lengths_ref, one_in, two_in, wq_in, wk_in, wv_in, wo_in, wg_in, wu_in, wd_in,
-    out_ref, gi_ref, oq_ref, ok_ref, ov_ref, oo_ref, og_out, ou_out, od_out, on_ref,
+    out_ref, gi_to, oq_to, ok_to, ov_to, oo_to, og_to, ou_to, od_to, on_to,
+    gi_ref, oq_ref, ok_ref, ov_ref, oo_ref, og_out, ou_out, od_out, on_ref,
     wn, wa, wo, wm, pack_a, pack_m, xm, og8, nt8, no8, at8, atb, og_peer, nt_peer, no_peer, at_peer,
     og_t, nt_t, q_ref, k_ref, v_ref, p_ref, mid, acc, gn, gain, tri, tri_peer,
     swap, swap_in, gat, edge, edge_in, outs, outs_peer, gb, gb_peer, mga,
     nb_peer, nb_sum, mlp_twos, mlp_ends, mga_twos, mga_ends, mgo_twos, mgo_ends, nb_twos, nb_ends,
     own_sem, g_send, g_recv, s_send, s_recv, halo_send, halo_recv, edge_send, edge_recv,
-    side_send, side_recv, tri_send, tri_recv, swap_send, swap_recv, out_send, out_recv, host_sem,
+    side_send, side_recv, tri_send, tri_recv, swap_send, swap_recv, out_send, out_recv, host_sem, row_send, row_recv,
 ):
-    nb, ga_send, no_t = wn, swap.at[0, :, 0:HALF], nt_t
+    nb, no_t = wn, nt_t
     here = Place()
     z, c, k, h = here.z, here.c, here.k, here.h
     tiles = wm.shape[0]
@@ -417,8 +418,15 @@
     def at_copy():
         return remote(atb.at[1 - h], at8.at[pl.ds(2 * h, 2)], swap_send.at[3], swap_recv.at[3], here.mate())
 
-    def ga_copy():
-        return remote(ga_send, gat.at[h], swap_send.at[4], swap_recv.at[4], here.mate())
+    def ga_copy(row):
+        there = pl.ds(row * piece, piece)
+        return remote(
+            swap.at[0, there, pl.ds(0, HALF)], gat.at[h, there], row_send.at[2 + row], row_recv.at[2 + row], here.mate()
+        )
+
+    def gn_copy(row):
+        there = pl.ds(row * piece, piece)
+        return remote(swap.at[0, there], swap_in.at[0, there], row_send.at[row], row_recv.at[row], here.mate())
 
     def swap_copy(number):
         return remote(
@@ -562,17 +570,14 @@
         def _(n=n):
             halo(n, 2).start()
 
-        if n == 0:
-            steps(2, 4, 5)
-        else:
-            steps(0, 8, 9, 10)
+        if n == 1:
+            steps(0, 8, 9)
             steps(1, 7)
+            steps(2, 4)
 
     steps(4, 3)
     for slot in range(2):
         q_ref[slot] = projected(2, slot)
-    steps(3, 4, 5)
-    steps(2, 6)
 
     for n in range(2):
 
@@ -620,17 +625,18 @@
     attend(1 - h, 0)
     attend(1 - h, 1)
     at_copy().start()
-    steps(0, *range(11, total))
-    og_copy(h).start()
-    steps(1, 8, 9)
-    steps(2, 7)
-    steps(3, 6)
+    steps(0, 10, 11, 12, 13, 14, 15, 16)
+    steps(2, 5)
+    steps(1, 8)
     attend(h, 0)
     attend(h, 1)
     at8[pl.ds(2 * h, 2)] = atb[h]
+    steps(3, 4)
+    steps(2, 6)
+    steps(3, 5)
     steps(4, 4, 5)
-    steps(1, 10)
-    steps(2, 8)
+    steps(1, 9)
+    steps(2, 7)
     at_copy().wait()
     at_side().start()
     attended = jnp.concatenate([at8[i // 2, i % 2] for i in range(8)], axis=1)
@@ -641,30 +647,39 @@
     spread(normed_of(middle, 8), nt8, h)
     nt_copy(h).start()
     nt_side(2, h).start()
-    steps(1, 11)
+    og_copy(h).start()
+    steps(1, 10, 11)
+    steps(2, 8)
+    steps(3, 6)
     steps(2, 9)
     steps(3, 7)
     acc[h] = middle
     acc[1 - h] = jnp.zeros(middle.shape, jnp.float32)
     gn[...] = jnp.zeros(gn.shape, jnp.float32)
 
-    def feed(f, slot):
-        w_pair = flat(wm[f, :, :, :, :, :, 0 : 2 * PART])
-        w_down = flat(wm[f, :, :, :, :, :, 2 * PART : 3 * PART])
-        both = mm(joined(nt8, slot), w_pair)
-        gates, ups = both[:, 0:PART], both[:, PART:]
-        grad_hidden = mm(joined(og8, slot), w_down)
-        sigmoid = 1.0 / (1.0 + jnp.exp(-gates))
-        silu = gates * sigmoid
-        hidden = low(silu * ups)
-        grad_gates = low(grad_hidden * ups * sigmoid * (1.0 + gates * (1.0 - sigmoid)))
-        grad_ups = low(grad_hidden * silu)
-        tri[f, 0, slot] = grad_gates
-        tri[f, 1, slot] = grad_ups
-        tri[f, 2, slot] = hidden
-        tri_copy(f, slot).start()
-        acc[slot] += nt_dot(hidden, w_down)
-        gn[slot] += nt_dot(jnp.concatenate([grad_gates, grad_ups], axis=1), w_pair)
+    def feed(slot, *numbers):
+        left, out_grad = joined(nt8, slot), joined(og8, slot)
+        w_pairs = [flat(wm[f, :, :, :, :, :, 0 : 2 * PART]) for f in numbers]
+        w_down = jnp.concatenate([flat(wm[f, :, :, :, :, :, 2 * PART : 3 * PART]) for f in numbers], axis=1)
+        grads_hidden = mm(out_grad, w_down)
+        hidden_acts, grads = [], []
+        for i, f in enumerate(numbers):
+            both = mm(left, w_pairs[i])
+            gates, ups = both[:, 0:PART], both[:, PART:]
+            grad_hidden = grads_hidden[:, i * PART : (i + 1) * PART]
+            sigmoid = 1.0 / (1.0 + jnp.exp(-gates))
+            silu = gates * sigmoid
+            hidden = low(silu * ups)
+            grad_gates = low(grad_hidden * ups * sigmoid * (1.0 + gates * (1.0 - sigmoid)))
+            grad_ups = low(grad_hidden * silu)
+            tri[f, 0, slot] = grad_gates
+            tri[f, 1, slot] = grad_ups
+            tri[f, 2, slot] = hidden
+            tri_copy(f, slot).start()
+            hidden_acts.append(hidden)
+            grads += [grad_gates, grad_ups]
+        acc[slot] += nt_dot(jnp.concatenate(hidden_acts, axis=1), w_down)
+        gn[slot] += nt_dot(jnp.concatenate(grads, axis=1), jnp.concatenate(w_pairs, axis=1))
 
     og_side(0, h).wait()
     turned_slot(og8, og_peer, og_t, h)
@@ -740,29 +755,39 @@
     def _(f):
         tile_steps(f)
         gather.fifth(early + f, wm.at[f])
-        feed(f, h)
+        feed(h, f)
 
     og_copy(1 - h).wait()
     og_side(1, 1 - h).start()
     nt_copy(1 - h).wait()
     nt_side(3, 1 - h).start()
 
-    @pl.loop(0, FIRST_TILES)
-    def _(f):
-        @pl.when(FIRST_TILES + f < tiles)
-        def _():
-            tile_steps(FIRST_TILES + f)
-
-        feed(f, 1 - h)
-
-    @pl.loop(FIRST_TILES, tiles)
-    def _(f):
-        gather.fifth(early + f, wm.at[f])
-        feed(f, h)
-        feed(f, 1 - h)
-
-    swap[0] = low(gn[1 - h])
-    swap_copy(0).start()
+    @pl.loop(0, FIRST_TILES // 2)
+    def _(i):
+        for f in (FIRST_TILES + 2 * i, FIRST_TILES + 2 * i + 1):
+
+            @pl.when(f < tiles)
+            def _(f=f):
+                tile_steps(f)
+
+        feed(1 - h, 2 * i, 2 * i + 1)
+
+    feed(1 - h, FIRST_TILES - 1)
+
+    @pl.loop(0, (tiles - FIRST_TILES) // 2)
+    def _(i):
+        f = FIRST_TILES + 2 * i
+        for tile in (f, f + 1):
+            gather.fifth(early + tile, wm.at[tile])
+
+        @pl.loop(0, 2)
+        def _(slot):
+            feed(slot, f, f + 1)
+
+    for row in range(2):
+        there = slice(row * piece, (row + 1) * piece)
+        swap[0, there, :] = low(gn[1 - h, there, :])
+        gn_copy(row).start()
     og_side(1, 1 - h).wait()
     turned_slot(og8, og_peer, og_t, 1 - h)
     nt_side(3, 1 - h).wait()
@@ -774,31 +799,38 @@
         launch_tile(f)
 
 
-    def close_middle():
-        swap_copy(0).wait()
-        middle = mid[...]
+    def close_middle(row):
+        gn_copy(row).wait()
+        there = slice(row * piece, (row + 1) * piece)
+        middle = mid[there, :]
         factor = lax.rsqrt(jnp.mean(middle * middle, axis=-1, keepdims=True) + 1e-05)
-        grad_normed = gn[h] + wide(swap_in[0])
+        grad_normed = gn[h, there, :] + wide(swap_in[0, there, :])
         through = grad_normed * gain[8:9, :]
         shift = jnp.mean(through * middle, axis=-1, keepdims=True) * factor * factor * factor
-        grad_middle = wide(joined(og8, h)) + factor * through - middle * shift
-        gi_ref[...] = grad_middle
-        gb[...] = low(grad_middle)
-        gb_side().start()
-        gain[8:16, :] = jnp.broadcast_to(
-            jnp.sum(grad_normed * middle * factor, axis=0, keepdims=True), (8, middle.shape[1])
-        )
-
-    def to_attended():
+        out_grad = jnp.concatenate([og8[i // 2, i % 2, h, there, :] for i in range(8)], axis=1)
+        grad_middle = wide(out_grad) + factor * through - middle * shift
+        gi_ref[there, :] = grad_middle
+        gb[there, :] = low(grad_middle)
+        return jnp.sum(grad_normed * middle * factor, axis=0, keepdims=True)
+
+    def to_attended(row):
+        there = slice(row * piece, (row + 1) * piece)
+
         def part(half):
             rows = pl.ds(2 * half, 2)
-            return low(nt_dot(gb[:, 0:HALF], flat(wo[0, rows])) + nt_dot(gb[:, HALF:], flat(wo[1, rows])))
-
-        swap[0, :, 0:HALF] = part(1 - h)
-        ga_copy().start()
+            return low(
+                nt_dot(gb[there, 0:HALF], flat(wo[0, rows])) + nt_dot(gb[there, HALF:], flat(wo[1, rows]))
+            )
+
+        swap[0, there, 0:HALF] = part(1 - h)
+        ga_copy(row).start()
+        gat[h, there, :] = part(h)
+
+    def send_out(ones):
+        gb_side().start()
         swap[1] = low(acc[1 - h])
         swap_copy(1).start()
-        gat[h] = part(h)
+        gain[8:16, :] = jnp.broadcast_to(ones[0] + ones[1], (8, gain.shape[1]))
 
     def keep_out():
         mid[...] = acc[h]
@@ -808,23 +840,22 @@
         swap[1] = low(mid[...] + wide(swap_in[1]))
         out_store().start()
 
-    def attend_back(slot):
-        for row in range(2):
-            span_rows = slice(row * piece, (row + 1) * piece)
-            for head in range(HEADS // 2):
-                cols = slice(head * HEAD_DIM, (head + 1) * HEAD_DIM)
-                there = slice(row * HALF + head * HEAD_DIM, row * HALF + (head + 1) * HEAD_DIM)
-                grad = gat[slot, span_rows, cols]
-                probs = p_ref[slot, row, head]
-                gn[slot, :, there] = tn_dot(low(probs), grad)
-                grad_probs = nt_dot(grad, flat(v_ref[2 * slot + row, :, :, cols]))
-                inner = jnp.sum(grad_probs * probs, axis=-1, keepdims=True)
-                grad_scores = low(probs * (grad_probs - inner))
-                outs[2, slot, span_rows, cols] = low(mm(grad_scores, flat(k_ref[2 * slot + row, :, :, cols])) * scale)
-                acc[slot, :, there] = tn_dot(grad_scores, q_ref[slot, span_rows, cols]) * scale
-            there = slice(row * HALF, (row + 1) * HALF)
-            edge[0, slot, row] = low(acc[slot, PAD - WINDOW : PAD, there])
-            edge[1, slot, row] = low(gn[slot, PAD - WINDOW : PAD, there])
+    def attend_back(slot, row):
+        span_rows = slice(row * piece, (row + 1) * piece)
+        for head in range(HEADS // 2):
+            cols = slice(head * HEAD_DIM, (head + 1) * HEAD_DIM)
+            there = slice(row * HALF + head * HEAD_DIM, row * HALF + (head + 1) * HEAD_DIM)
+            grad = gat[slot, span_rows, cols]
+            probs = p_ref[slot, row, head]
+            gn[slot, :, there] = tn_dot(low(probs), grad)
+            grad_probs = nt_dot(grad, flat(v_ref[2 * slot + row, :, :, cols]))
+            inner = jnp.sum(grad_probs * probs, axis=-1, keepdims=True)
+            grad_scores = low(probs * (grad_probs - inner))
+            outs[2, slot, span_rows, cols] = low(mm(grad_scores, flat(k_ref[2 * slot + row, :, :, cols])) * scale)
+            acc[slot, :, there] = tn_dot(grad_scores, q_ref[slot, span_rows, cols]) * scale
+        there = slice(row * HALF, (row + 1) * HALF)
+        edge[0, slot, row] = low(acc[slot, PAD - WINDOW : PAD, there])
+        edge[1, slot, row] = low(gn[slot, PAD - WINDOW : PAD, there])
 
     def send_edge():
         out_copy(2).start()
@@ -882,11 +913,13 @@
         return lax.rsqrt(jnp.mean(value * value, axis=-1, keepdims=True) + 1e-05)
 
     def send_input():
-        x = wide(xm[...])
         part = to_input(1 - h)
         swap[0] = low(part)
         swap_copy(2).start()
-        one = jnp.sum(part * x * inverse_rms(x), axis=0, keepdims=True)
+        x = wide(xm[...])
+        return jnp.sum(part * x * inverse_rms(x), axis=0, keepdims=True)
+
+    def send_norm(one):
         part = to_input(h)
         acc[0] = part
         for i in range(2):
@@ -943,37 +976,62 @@
             sum_tick(t)
 
     ticks(0, 2)
-    close_middle()
-    to_attended()
+    ones = []
+    for row in range(2):
+        ones.append(close_middle(row))
+        to_attended(row)
+    send_out(ones)
     keep_out()
     ticks(2, 4)
-    attend_back(h)
-    ga_copy().wait()
-    attend_back(1 - h)
+    attend_back(h, 0)
+    attend_back(h, 1)
+    for row in range(2):
+        ga_copy(row).wait()
+        attend_back(1 - h, row)
     send_edge()
     for i in range(2):
         x_again(i).start()
-    ticks(4, 7)
     turn_normed()
-    attn_grads(2)
     wout_grads()
     launch(tiles)
     launch(tiles + 1)
+    attn_grads(2)
     launch(tiles + 2)
-    ticks(7, 9)
+    ticks(4, 7)
     close_edge()
-    ticks(9, 10)
-    send_input()
+    one = send_input()
     for m in range(2):
         attn_grads(m)
         launch(tiles + 3 + m)
+    send_norm(one)
+    ticks(7, 9)
     close_norm()
     launch(tiles + 5)
-    ticks(10, 14)
+    ticks(9, 11)
     close_out()
+    ticks(11, 14)
     close_input()
-    ticks(14, chunks + SUM_LAGS[-1])
+    stores = [
+        pltpu.make_async_copy(source, target, host_sem.at[12 + i])
+        for i, (source, target) in enumerate(
+            zip(
+                (gi_ref, og_out, ou_out, od_out, oo_ref, oq_ref, ok_ref, ov_ref, on_ref),
+                (gi_to, og_to, ou_to, od_to, oo_to, oq_to, ok_to, ov_to, on_to),
+            )
+        )
+    ]
+    stores[0].start()
+    ticks(14, tiles + SUM_LAGS[-1])
+    for store_out in stores[1:4]:
+        store_out.start()
+    ticks(tiles + SUM_LAGS[-1], tiles + SUM_LAGS[-1] + 2)
+    stores[4].start()
+    ticks(tiles + SUM_LAGS[-1] + 2, chunks + SUM_LAGS[-1])
+    for store_out in stores[5:]:
+        store_out.start()
     out_store().wait()
+    for store_out in stores:
+        store_out.wait()
 
 
 def deliver_kernel(count, *refs):
@@ -1046,18 +1104,18 @@
         ((3, 4, rows, LANES), bf), ((3, rows, LANES), bf),
     ]
     count, chunks = 6 + tiles, 6 + tiles
+    sums = [((tokens, width), fl)] + [((rows, width), fl)] * 4
+    sums += [((rows, 2 * tiles * PART), fl)] * 3 + [((rows, LANES), fl)]
     results = pl.pallas_call(
         layer_kernel,
-        out_shape=[shape((tokens, width), bf), shape((tokens, width), fl)]
-        + [shape((rows, width), fl)] * 4 + [shape((rows, 2 * tiles * PART), fl)] * 3
-        + [shape((rows, LANES), fl)],
+        out_shape=[shape((tokens, width), bf)] + [shape(*s) for s in sums],
         in_specs=[anywhere, anywhere, pl.BlockSpec(memory_space=pltpu.SMEM), vmem, vmem] + [anywhere] * 7,
-        out_specs=[anywhere] + [vmem] * 9,
-        scratch_shapes=[pltpu.VMEM(*s) for s in scratch]
+        out_specs=[anywhere] * 10,
+        scratch_shapes=[pltpu.VMEM(*s) for s in sums + scratch]
         + [
             dma((count, 2)), dma((count, 4)), dma((count, 4)), dma((chunks, 4)), dma((chunks, 4)),
             dma((2, 2)), dma((2, 2)), dma((2,)), dma((2,)), dma((8,)), dma((8,)),
-            dma((tiles,)), dma((tiles,)), dma((8,)), dma((8,)), dma((3,)), dma((3,)), dma((12,)),
+            dma((tiles,)), dma((tiles,)), dma((8,)), dma((8,)), dma((3,)), dma((3,)), dma((21,)), dma((4,)), dma((4,)),
         ],
         compiler_params=pltpu.CompilerParams(
             collective_id=0, has_side_effects=True, vmem_limit_bytes=63 * 2**20

time: 181 us -> 177 us (0.978)
  Pallas kernels: 179 us -> 175 us
    pallas_call x1, Pallas kernels: 176 us -> 172 us  [fused(): pl.pallas_call(layer_kernel, out_shape=[shape((tokens, width), bf)] + [sh...]
where the time goes in v5:
time: 177 us; the launch traced here: 176 us
  Pallas kernels  175 us (99%)
    pallas_call x1, Pallas kernels, fused(): pl.pallas_call(layer_kernel, out_shape=[shape((tokens, width), bf)] + [sh...  172 us

profile of v5, /device:TPU:0, one launch (start us, length us, event | category | flops | bytes accessed | tf_op | source)
XLA Modules:
  0.0 176.3 jit_solution(9450588484903262634)
XLA Ops:
  0.6 172.4 %layer.1 = (bf16[256,1024]{1,0:T(8,128)(2,1)}, f32[256,1024]{1,0:T(8,128)}, f32[32,1024]{1,0:T(8,128)}, f32[32,1024]{1,0:T(8,128)}, f32[32,1024]{1,0:T(8,128)}, ...) custom-call(bf16[256,1024]{1,0:T(8,128)(2,1)} %bitcast.4, ...), custom_call_target="tpu_custom_call" | custom-call | tf_op jit(solution)/shard_map/layer/pallas_call | solution.py:1109
  173.0 3.1 %deliver.1 = (f32[32]{0:T(128)}, f32[32]{0:T(128)}, bf16[256,1024]{1,0:T(8,128)(2,1)}, f32[256,1024]{1,0:T(8,128)}, f32[32,1024]{1,0:T(8,128)}, /*index=5*/f32[3...) custom-call(f32[32,128]{1,0:T(8,128)} %get-tuple-element.32.refs_0_,, ...), custom_call_target="tpu_custom_call" | custom-call | tf_op jit(solution)/shard_map/deliver/pallas_call | solution.py:1061

commit v6 on v5

--- a/solution.py
+++ b/solution.py
@@ -105,7 +105,7 @@
 HALF = 512
 PAD = 128
 AHEAD = (11, 6, 4, 2)
-FIRST_TILES = 7
+FIRST_TILES = 9
 SUM_LAGS = (0, 4, 8)
 
 
@@ -523,8 +523,9 @@
     greet(here.partners())
 
     steps(0, 0, 1, 2, 3)
+    steps(0, 4, 5)
     x_copy().start()
-    steps(0, 4, 5, 6, 7)
+    steps(0, 6, 7)
     steps(1, 0, 1, 2, 3)
     steps(2, 0, 1, 2, 3)
     steps(1, 4, 5)
@@ -997,14 +998,14 @@
     launch(tiles + 1)
     attn_grads(2)
     launch(tiles + 2)
-    ticks(4, 7)
+    ticks(4, 8)
     close_edge()
     one = send_input()
     for m in range(2):
         attn_grads(m)
         launch(tiles + 3 + m)
     send_norm(one)
-    ticks(7, 9)
+    ticks(8, 9)
     close_norm()
     launch(tiles + 5)
     ticks(9, 11)

time: 177 us -> 175 us (0.989)
  no operation moved by 1% of the time
where the time goes in v6:
time: 175 us
  Pallas kernels  174 us (99%)
    pallas_call x1, Pallas kernels, fused(): pl.pallas_call(layer_kernel, out_shape=[shape((tokens, width), bf)] + [sh...  171 us

profile of v6, /device:TPU:0, one launch (start us, length us, event | category | flops | bytes accessed | tf_op | source)
XLA Modules:
  0.0 175.0 jit_solution(16365838827187953411)
XLA Ops:
  0.6 171.0 %layer.1 = (bf16[256,1024]{1,0:T(8,128)(2,1)}, f32[256,1024]{1,0:T(8,128)}, f32[32,1024]{1,0:T(8,128)}, f32[32,1024]{1,0:T(8,128)}, f32[32,1024]{1,0:T(8,128)}, ...) custom-call(bf16[256,1024]{1,0:T(8,128)(2,1)} %bitcast.4, ...), custom_call_target="tpu_custom_call" | custom-call | tf_op jit(solution)/shard_map/layer/pallas_call | solution.py:1110
  171.7 3.1 %deliver.1 = (f32[32]{0:T(128)}, f32[32]{0:T(128)}, bf16[256,1024]{1,0:T(8,128)(2,1)}, f32[256,1024]{1,0:T(8,128)}, f32[32,1024]{1,0:T(8,128)}, /*index=5*/f32[3...) custom-call(f32[32,128]{1,0:T(8,128)} %get-tuple-element.32.refs_0_,, ...), custom_call_target="tpu_custom_call" | custom-call | tf_op jit(solution)/shard_map/deliver/pallas_call | solution.py:1062
